TPU v7x, 32 devices: a whole 2x2x4 slice. The times are simulated.
32 devices in a mesh: dp: 8 (over z, x), mp: 4 (over y, core).
Axes of the slice: x: 2, y: 2, z: 4, core: 2. Of those that a mesh axis runs over, the one named last changes fastest.
Arguments:
- tokens: bfloat16 [16384, 1024], P(('dp', 'mp')), may hold values from -6 to 6
- cotangent: bfloat16 [16384, 1024], P(('dp', 'mp'))
- lengths: int32 [8, 4], P('dp'), may hold values from 0 to 2048, as said below
- attend: float32 [3, 1024, 1024], P(None, 'dp', 'mp'), may hold values from -0.1875 to 0.1875
- mixing: float32 [1024, 1024], P('mp', 'dp'), may hold values from -0.1875 to 0.1875
- expand: float32 [1024, 4096], P('dp', 'mp'), may hold values from -0.1875 to 0.1875
- contract: float32 [4096, 1024], P('mp', 'dp'), may hold values from -0.09375 to 0.09375
- outer_norms: float32 [4, 1024], P(None, ('dp', 'mp'))
- head_norms: float32 [2, 1024], P(None, ('dp', 'mp'))
- unit_norms: float32 [2, 4096], P(None, ('dp', 'mp'))
- attend_moment: float32 [3, 1024, 1024], P(None, 'dp', 'mp'), may hold values from -0.00018310547 to 0.00018310547
- mixing_moment: float32 [1024, 1024], P('mp', 'dp'), may hold values from -0.00018310547 to 0.00018310547
- expand_moment: float32 [1024, 4096], P('dp', 'mp'), may hold values from -0.00018310547 to 0.00018310547
- contract_moment: float32 [4096, 1024], P('mp', 'dp'), may hold values from -0.00018310547 to 0.00018310547
- outer_moment: float32 [4, 1024], P(None, ('dp', 'mp')), may hold values from -0.00018310547 to 0.00018310547
- head_moment: float32 [2, 1024], P(None, ('dp', 'mp')), may hold values from -0.00018310547 to 0.00018310547
- unit_moment: float32 [2, 4096], P(None, ('dp', 'mp')), may hold values from -0.00018310547 to 0.00018310547
- attend_square: float32 [3, 1024, 1024], P(None, 'dp', 'mp'), may hold values from 1e-09 to 1.6e-08
- mixing_square: float32 [1024, 1024], P('mp', 'dp'), may hold values from 1e-09 to 1.6e-08
- expand_square: float32 [1024, 4096], P('dp', 'mp'), may hold values from 1e-09 to 1.6e-08
- contract_square: float32 [4096, 1024], P('mp', 'dp'), may hold values from 1e-09 to 1.6e-08
- outer_square: float32 [4, 1024], P(None, ('dp', 'mp')), may hold values from 1e-09 to 1.6e-08
- head_square: float32 [2, 1024], P(None, ('dp', 'mp')), may hold values from 1e-09 to 1.6e-08
- unit_square: float32 [2, 4096], P(None, ('dp', 'mp')), may hold values from 1e-09 to 1.6e-08
Outputs:
- output: bfloat16 [16384, 1024], P(('dp', 'mp'))
- input_grad: float32 [16384, 1024], P(('dp', 'mp'))
- grad_norm: float32 [], replicated
- attend_grad: float32 [3, 1024, 1024], P(None, 'dp', 'mp')
- attend_moment_new: float32 [3, 1024, 1024], P(None, 'dp', 'mp')
- attend_square_new: float32 [3, 1024, 1024], P(None, 'dp', 'mp')
- attend_change: float32 [3, 1024, 1024], P(None, 'dp', 'mp')
- mixing_grad: float32 [1024, 1024], P('mp', 'dp')
- mixing_moment_new: float32 [1024, 1024], P('mp', 'dp')
- mixing_square_new: float32 [1024, 1024], P('mp', 'dp')
- mixing_change: float32 [1024, 1024], P('mp', 'dp')
- expand_grad: float32 [1024, 4096], P('dp', 'mp')
- expand_moment_new: float32 [1024, 4096], P('dp', 'mp')
- expand_square_new: float32 [1024, 4096], P('dp', 'mp')
- expand_change: float32 [1024, 4096], P('dp', 'mp')
- contract_grad: float32 [4096, 1024], P('mp', 'dp')
- contract_moment_new: float32 [4096, 1024], P('mp', 'dp')
- contract_square_new: float32 [4096, 1024], P('mp', 'dp')
- contract_change: float32 [4096, 1024], P('mp', 'dp')
- outer_grad: float32 [4, 1024], P(None, ('dp', 'mp'))
- outer_moment_new: float32 [4, 1024], P(None, ('dp', 'mp'))
- outer_square_new: float32 [4, 1024], P(None, ('dp', 'mp'))
- outer_change: float32 [4, 1024], P(None, ('dp', 'mp'))
- head_grad: float32 [2, 1024], P(None, ('dp', 'mp'))
- head_moment_new: float32 [2, 1024], P(None, ('dp', 'mp'))
- head_square_new: float32 [2, 1024], P(None, ('dp', 'mp'))
- head_change: float32 [2, 1024], P(None, ('dp', 'mp'))
- unit_grad: float32 [2, 4096], P(None, ('dp', 'mp'))
- unit_moment_new: float32 [2, 4096], P(None, ('dp', 'mp'))
- unit_square_new: float32 [2, 4096], P(None, ('dp', 'mp'))
- unit_change: float32 [2, 4096], P(None, ('dp', 'mp'))
Inputs may be any that keep to these rules, and one draw needn't show every extreme that they name: Row g lists the lengths of up to 4 sequences packed in order from the first slot of group g; a row sums to at most 2048, and the slots after its sum are padding. In every draw one sequence fills all 2048 slots of some group.
All inputs are finite; a program needn't handle non-finite values.
Results may differ from a plain program's by a relative error of at most 0.0181.
Values may be sent and summed in bfloat16 or wider, within the bound.
No kernel may reach another device: no remote copies, remote signals or barrier semaphores. Data moves between devices by JAX's collectives and lax.ppermute only.
A program may use at most 192 MiB of HBM per device.

v0:
```python
from functools import partial

import jax
import jax.numpy as jnp
from jax import lax
from jax.sharding import PartitionSpec as P

D = 1024
HD = 64
FF = 4096
ADAM_STEP = 10


NORM_EPS = 1e-05
MASKED = -1e30
RATE = 0.02
BETA_ONE = 0.9
BETA_TWO = 0.95
ADAM_EPS = 1e-08
DECAY = 0.1
MAX_NORM = 1.0


def layer_norm(value, gain, bias):
    mean = jnp.mean(value, axis=-1, keepdims=True)
    centered = value - mean
    variance = jnp.mean(centered * centered, axis=-1, keepdims=True)
    return centered * lax.rsqrt(variance + NORM_EPS) * gain + bias


def segment_ids(lengths_row, length_all):
    ends = jnp.cumsum(lengths_row)
    places = jnp.arange(length_all, dtype=jnp.int32)
    return jnp.sum((places[:, None] >= ends[None, :]).astype(jnp.int32), axis=1)


def spread_rows(block_rows):
    return lax.all_gather(block_rows, "mp", axis=0, tiled=True)


def sum_rows(term, height):
    return lax.psum_scatter(
        term(jnp.int32(0), lax.axis_size("mp") * height), "mp", scatter_dimension=0, tiled=True
    )


def token_totals(first, second):
    return lax.psum((first, second), "mp")


def split_norm(value, gain, bias, width):
    first, second = token_totals(jnp.sum(value, axis=1), jnp.sum(value * value, axis=1))
    mean = first / width
    variance = second / width - mean * mean
    factor = lax.rsqrt(variance + NORM_EPS)
    normed = (value - mean[:, None]) * factor[:, None]
    return (normed * gain + bias, normed, factor)


def split_norm_back(grad, normed, factor, gain, width):
    weighted = grad * gain
    first, second = token_totals(jnp.sum(weighted, axis=1), jnp.sum(weighted * normed, axis=1))
    result = factor[:, None] * (
        weighted - first[:, None] / width - normed * (second[:, None] / width)
    )
    return (result, jnp.sum(grad * normed, axis=0), jnp.sum(grad, axis=0))


def block_scores(query_part, segment_part, keys, segment, factor):
    scores = (
        jnp.einsum("qhd,khd->hqk", query_part, keys, preferred_element_type=jnp.float32) * factor
    )
    allowed = segment_part[:, None] == segment[None, :]
    return jnp.where(allowed[None], scores, MASKED)


def attention_forward(query, keys, values, segment, block):
    length_all, count_heads, head_size = query.shape
    factor = head_size ** (-0.5)

    def one_block(index):
        start = index * block
        query_part = lax.dynamic_slice_in_dim(query, start, block, 0)
        segment_part = lax.dynamic_slice_in_dim(segment, start, block, 0)
        scores = block_scores(query_part, segment_part, keys, segment, factor)
        highest = jnp.max(scores, axis=2, keepdims=True)
        weights = jnp.exp(scores - highest)
        totals = jnp.sum(weights, axis=2, keepdims=True)
        probs = (weights / totals).astype(jnp.bfloat16)
        mixed = jnp.einsum("hqk,khd->qhd", probs, values, preferred_element_type=jnp.float32)
        return (mixed.astype(jnp.bfloat16), (highest + jnp.log(totals))[:, :, 0])

    outputs, log_totals = lax.map(one_block, jnp.arange(length_all // block))
    return (outputs.reshape(length_all, count_heads * head_size), log_totals)


def attention_backward(query, keys, values, segment, log_totals, grad_out, block):
    length_all, count_heads, head_size = query.shape
    factor = head_size ** (-0.5)

    def one_block(carry, index):
        key_back, value_back = carry
        start = index * block
        query_part = lax.dynamic_slice_in_dim(query, start, block, 0)
        segment_part = lax.dynamic_slice_in_dim(segment, start, block, 0)
        grad_part = lax.dynamic_slice_in_dim(grad_out, start, block, 0)
        scores = block_scores(query_part, segment_part, keys, segment, factor)
        probs = jnp.exp(scores - log_totals[index][:, :, None])
        value_back = value_back + jnp.einsum(
            "hqk,qhd->khd",
            probs.astype(jnp.bfloat16),
            grad_part,
            preferred_element_type=jnp.float32,
        )
        probs_back = jnp.einsum(
            "qhd,khd->hqk", grad_part, values, preferred_element_type=jnp.float32
        )
        centered = probs_back - jnp.sum(probs * probs_back, axis=2, keepdims=True)
        score_back = (probs * centered).astype(jnp.bfloat16)
        query_back = (
            jnp.einsum("hqk,khd->qhd", score_back, keys, preferred_element_type=jnp.float32)
            * factor
        )
        key_back = (
            key_back
            + jnp.einsum("hqk,qhd->khd", score_back, query_part, preferred_element_type=jnp.float32)
            * factor
        )
        return ((key_back, value_back), query_back)

    empty = jnp.zeros(query.shape, jnp.float32)
    (key_back, value_back), query_back = lax.scan(
        one_block, (empty, empty), jnp.arange(length_all // block)
    )
    width = count_heads * head_size
    return (
        query_back.reshape(length_all, width),
        key_back.reshape(length_all, width),
        value_back.reshape(length_all, width),
    )


def adamw(param, grad, moment, square, clip, fix_one, fix_two):
    clipped = grad * clip
    moment_new = BETA_ONE * moment + (1.0 - BETA_ONE) * clipped
    square_new = BETA_TWO * square + (1.0 - BETA_TWO) * clipped * clipped
    change = -RATE * (
        moment_new / fix_one / (jnp.sqrt(square_new / fix_two) + ADAM_EPS) + DECAY * param
    )
    return (moment_new, square_new, change)


def local(
    tokens,
    cotangent,
    lengths,
    attend,
    mixing,
    expand,
    contract,
    outer_norms,
    head_norms,
    unit_norms,
    attend_moment,
    mixing_moment,
    expand_moment,
    contract_moment,
    outer_moment,
    head_moment,
    unit_moment,
    attend_square,
    mixing_square,
    expand_square,
    contract_square,
    outer_square,
    head_square,
    unit_square,
):
    height = tokens.shape[0]
    shard_count = lax.axis_size("mp")
    length_all = height * shard_count
    place = lax.axis_index("mp")
    work_in, work_mix, work_exp, work_con = (
        lax.all_gather(attend.astype(jnp.bfloat16), "dp", axis=1, tiled=True),
        lax.all_gather(mixing.astype(jnp.bfloat16), "dp", axis=1, tiled=True),
        lax.all_gather(expand.astype(jnp.bfloat16), "dp", axis=0, tiled=True),
        lax.all_gather(contract.astype(jnp.bfloat16), "dp", axis=1, tiled=True),
    )
    outer, head_gain, unit_gain = (
        lax.all_gather(outer_norms, ("dp", "mp"), axis=1, tiled=True),
        lax.all_gather(head_norms, ("dp", "mp"), axis=1, tiled=True),
        lax.all_gather(unit_norms, ("dp", "mp"), axis=1, tiled=True),
    )
    head_width = work_in.shape[2]
    unit_width = work_exp.shape[1]
    head_local = lax.dynamic_slice_in_dim(head_gain, place * head_width, head_width, 1)
    unit_local = lax.dynamic_slice_in_dim(unit_gain, place * unit_width, unit_width, 1)
    segment = segment_ids(lengths[0], length_all)
    own_segment = lax.dynamic_slice_in_dim(segment, place * height, height, 0)
    live = (own_segment < lengths.shape[1]).astype(jnp.float32)
    inputs = tokens.astype(jnp.float32)
    first_out, first_pull = jax.vjp(layer_norm, inputs, outer[0], outer[1])
    normed_all = spread_rows(first_out.astype(jnp.bfloat16))
    projected = jnp.einsum(
        "td,cde->cte", normed_all, work_in, preferred_element_type=jnp.float32
    ).astype(jnp.bfloat16)
    count_heads = head_width // HD
    query = projected[0].reshape(length_all, count_heads, HD)
    keys = projected[1].reshape(length_all, count_heads, HD)
    values = projected[2].reshape(length_all, count_heads, HD)
    block = min(512, length_all)
    attended, log_totals = attention_forward(query, keys, values, segment, block)
    head_out, head_normed, head_factor = split_norm(
        attended.astype(jnp.float32), head_local[0], head_local[1], D
    )
    mixed_in = head_out.astype(jnp.bfloat16)
    branch = sum_rows(
        lambda start, count: jnp.dot(mixed_in, work_mix, preferred_element_type=jnp.float32), height
    )
    middle = inputs + branch
    second_out, second_pull = jax.vjp(layer_norm, middle, outer[2], outer[3])
    mid_all = spread_rows(second_out.astype(jnp.bfloat16))
    widened = jnp.dot(mid_all, work_exp, preferred_element_type=jnp.float32)
    activated, gelu_pull = jax.vjp(partial(jax.nn.gelu, approximate=False), widened)
    unit_out, unit_normed, unit_factor = split_norm(activated, unit_local[0], unit_local[1], FF)
    unit_low = unit_out.astype(jnp.bfloat16)
    feed = sum_rows(
        lambda start, count: jnp.dot(
            lax.dynamic_slice_in_dim(unit_low, start, count, 0),
            work_con,
            preferred_element_type=jnp.float32,
        ),
        height,
    )
    result = middle + feed
    back_out = cotangent.astype(jnp.float32) * live[:, None]
    back_all = spread_rows(back_out.astype(jnp.bfloat16))
    contract_back = jnp.einsum("tf,td->fd", unit_low, back_all, preferred_element_type=jnp.float32)
    unit_in = jnp.einsum("td,fd->tf", back_all, work_con, preferred_element_type=jnp.float32)
    unit_back, unit_gain_back, unit_bias_back = split_norm_back(
        unit_in, unit_normed, unit_factor, unit_local[0], FF
    )
    (widened_back,) = gelu_pull(unit_back)
    widened_low = widened_back.astype(jnp.bfloat16)
    expand_back = jnp.einsum("td,tf->df", mid_all, widened_low, preferred_element_type=jnp.float32)
    mid_in = sum_rows(
        lambda start, count: jnp.einsum(
            "tf,df->td", widened_low, work_exp, preferred_element_type=jnp.float32
        ),
        height,
    )
    middle_part, gain_two, bias_two = second_pull(mid_in)
    middle_back = back_out + middle_part
    middle_low = middle_back.astype(jnp.bfloat16)
    middle_all = spread_rows(middle_low)
    mixing_back = jnp.einsum("te,td->ed", mixed_in, middle_all, preferred_element_type=jnp.float32)
    mixed_back = jnp.einsum("td,ed->te", middle_all, work_mix, preferred_element_type=jnp.float32)
    heads_back, head_gain_back, head_bias_back = split_norm_back(
        mixed_back, head_normed, head_factor, head_local[0], D
    )
    head_back = lax.dynamic_update_slice_in_dim(
        jnp.zeros((2, D), jnp.float32),
        jnp.stack([head_gain_back, head_bias_back]),
        place * head_width,
        1,
    )
    attended_back = heads_back.astype(jnp.bfloat16)
    query_back, key_back, value_back = attention_backward(
        query,
        keys,
        values,
        segment,
        log_totals,
        attended_back.reshape(length_all, count_heads, HD),
        block,
    )
    projected_back = jnp.stack([query_back, key_back, value_back]).astype(jnp.bfloat16)
    attend_back = jnp.einsum(
        "td,cte->cde", normed_all, projected_back, preferred_element_type=jnp.float32
    )
    normed_back = sum_rows(
        lambda start, count: jnp.einsum(
            "cte,cde->td", projected_back, work_in, preferred_element_type=jnp.float32
        ),
        height,
    )
    input_part, gain_one, bias_one = first_pull(normed_back)
    input_grad = middle_back + input_part
    outer_back = jnp.stack([gain_one, bias_one, gain_two, bias_two])
    unit_full = lax.dynamic_update_slice_in_dim(
        jnp.zeros((2, FF), jnp.float32),
        jnp.stack([unit_gain_back, unit_bias_back]),
        place * unit_width,
        1,
    )
    weight_grads = (
        lax.psum_scatter(
            attend_back.astype(jnp.bfloat16), "dp", scatter_dimension=1, tiled=True
        ).astype(jnp.float32),
        lax.psum_scatter(
            mixing_back.astype(jnp.bfloat16), "dp", scatter_dimension=1, tiled=True
        ).astype(jnp.float32),
        lax.psum_scatter(
            expand_back.astype(jnp.bfloat16), "dp", scatter_dimension=0, tiled=True
        ).astype(jnp.float32),
        lax.psum_scatter(
            contract_back.astype(jnp.bfloat16), "dp", scatter_dimension=1, tiled=True
        ).astype(jnp.float32),
    )
    norm_grads = (
        lax.psum_scatter(outer_back, ("dp", "mp"), scatter_dimension=1, tiled=True),
        lax.psum_scatter(head_back, ("dp", "mp"), scatter_dimension=1, tiled=True),
        lax.psum_scatter(unit_full, ("dp", "mp"), scatter_dimension=1, tiled=True),
    )
    gradients = tuple(weight_grads) + tuple(norm_grads)
    local_squares = jnp.float32(0.0)
    for gradient in gradients:
        local_squares = local_squares + jnp.sum(gradient * gradient)
    total_squares = lax.psum(local_squares, ("dp", "mp"))
    norm = jnp.sqrt(total_squares)
    clip = jnp.minimum(1.0, MAX_NORM / (norm + 1e-06))
    count_steps = jnp.float32(ADAM_STEP)
    fix_one = 1.0 - jnp.power(jnp.float32(BETA_ONE), count_steps)
    fix_two = 1.0 - jnp.power(jnp.float32(BETA_TWO), count_steps)
    first = adamw(attend, gradients[0], attend_moment, attend_square, clip, fix_one, fix_two)
    second = adamw(mixing, gradients[1], mixing_moment, mixing_square, clip, fix_one, fix_two)
    third = adamw(expand, gradients[2], expand_moment, expand_square, clip, fix_one, fix_two)
    fourth = adamw(contract, gradients[3], contract_moment, contract_square, clip, fix_one, fix_two)
    fifth = adamw(outer_norms, gradients[4], outer_moment, outer_square, clip, fix_one, fix_two)
    sixth = adamw(head_norms, gradients[5], head_moment, head_square, clip, fix_one, fix_two)
    seventh = adamw(unit_norms, gradients[6], unit_moment, unit_square, clip, fix_one, fix_two)
    return (
        result.astype(jnp.bfloat16),
        input_grad,
        norm,
        gradients[0],
        first[0],
        first[1],
        first[2],
        gradients[1],
        second[0],
        second[1],
        second[2],
        gradients[2],
        third[0],
        third[1],
        third[2],
        gradients[3],
        fourth[0],
        fourth[1],
        fourth[2],
        gradients[4],
        fifth[0],
        fifth[1],
        fifth[2],
        gradients[5],
        sixth[0],
        sixth[1],
        sixth[2],
        gradients[6],
        seventh[0],
        seventh[1],
        seventh[2],
    )


def solution(mesh):
    return jax.shard_map(
        local,
        mesh=mesh,
        in_specs=(
            P(("dp", "mp"), None),
            P(("dp", "mp"), None),
            P("dp", None),
            P(None, "dp", "mp"),
            P("mp", "dp"),
            P("dp", "mp"),
            P("mp", "dp"),
            P(None, ("dp", "mp")),
            P(None, ("dp", "mp")),
            P(None, ("dp", "mp")),
            P(None, "dp", "mp"),
            P("mp", "dp"),
            P("dp", "mp"),
            P("mp", "dp"),
            P(None, ("dp", "mp")),
            P(None, ("dp", "mp")),
            P(None, ("dp", "mp")),
            P(None, "dp", "mp"),
            P("mp", "dp"),
            P("dp", "mp"),
            P("mp", "dp"),
            P(None, ("dp", "mp")),
            P(None, ("dp", "mp")),
            P(None, ("dp", "mp")),
        ),
        out_specs=(
            P(("dp", "mp"), None),
            P(("dp", "mp"), None),
            P(),
            P(None, "dp", "mp"),
            P(None, "dp", "mp"),
            P(None, "dp", "mp"),
            P(None, "dp", "mp"),
            P("mp", "dp"),
            P("mp", "dp"),
            P("mp", "dp"),
            P("mp", "dp"),
            P("dp", "mp"),
            P("dp", "mp"),
            P("dp", "mp"),
            P("dp", "mp"),
            P("mp", "dp"),
            P("mp", "dp"),
            P("mp", "dp"),
            P("mp", "dp"),
            P(None, ("dp", "mp")),
            P(None, ("dp", "mp")),
            P(None, ("dp", "mp")),
            P(None, ("dp", "mp")),
            P(None, ("dp", "mp")),
            P(None, ("dp", "mp")),
            P(None, ("dp", "mp")),
            P(None, ("dp", "mp")),
            P(None, ("dp", "mp")),
            P(None, ("dp", "mp")),
            P(None, ("dp", "mp")),
            P(None, ("dp", "mp")),
        ),
        check_vma=False,
    )
```

profile of v0, /device:TPU:0, one launch (start us, length us, event | category | flops | bytes accessed | tf_op | source)
XLA Modules:
  0.0 1558.3 jit_solution(18077144064112892348)
XLA Ops:
  9.4 44.2 %all-gather = f32[32,32,4]{1,2,0:T(4,128)S(1)} all-gather(f32[1,32,4]{1,2,0:T(4,128)} %bitcast.213), channel_id=1, replica_groups=mesh['dp'=8,'mp'=4] {'dp','mp'}, dimensions={0}, use_global_device_ids=true | all-gather | bytes 16896 | tf_op jit(solution)/shard_map/all_gather | solution.py:190
  59.7 36.6 %all-gather.1 = f32[32,32,2]{1,2,0:T(2,128)S(1)} all-gather(f32[1,32,2]{1,2,0:T(2,128)S(1)} %bitcast.214), channel_id=1, replica_groups=mesh['dp'=8,'mp'=4] {'dp','mp'}, dimensions={0}, use_global_device_ids=true | all-gather | bytes 8448 | tf_op jit(solution)/shard_map/all_gather | solution.py:191
  97.2 28.9 %all_gather.37 = bf16[256,1024]{1,0:T(8,128)(2,1)} all-gather(bf16[256,128]{1,0:T(8,128)(2,1)S(1)} %convert_element_type.120), channel_id=1, replica_groups=mesh['dp'=8,'mp'=4] {'dp'}, dimensions={1}, use_global_device_ids=true | all-gather | bytes 589824 | tf_op jit(solution)/shard_map/all_gather | solution.py:185
  132.7 64.4 %while.27 = (s32[]{:T(128)}, bf16[4,512,4,64]{1,3,2,0:T(8,128)(2,1)}, f32[4,4,512]{2,1,0:T(4,128)}, s32[4]{0:T(128)S(1)}, s32[2048]{0:T(1024)S(1)}, /*index=5*/b...) while((s32[]{:T(128)}, ...), condition=%wide.region_7.8_spmd, body=%wide.region_4.7_spmd.sunk | while | flops 1125251072 | bytes 57227464 | solution.py:93
  225.4 65.9 %reduce-scatter.24.cloned.1.call-done = f32[512,1024]{1,0:T(8,128)} async-done(((f32[2048,1024]{1,0:T(8,128)}), f32[512,1024]{1,0:T(8,128)}) %reduce-scatter.24.cloned.1.call-update) | async-done | bytes 2097168 | tf_op jit(solution)/shard_map/reduce_scatter | solution.py:42
  295.1 40.8 %all_gather.40 = f32[2,4096]{1,0:T(2,128)S(1)} all-gather(f32[2,128]{1,0:T(2,128)S(1)} %copy-done.71), channel_id=1, replica_groups=mesh['dp'=8,'mp'=4] {'dp','mp'}, dimensions={1}, use_global_device_ids=true | all-gather | bytes 33792 | tf_op jit(solution)/shard_map/all_gather | solution.py:192
  345.2 34.2 %all-gather.20.cloned.1.call-done = bf16[2048,1024]{1,0:T(8,128)(2,1)} async-done(((bf16[512,1024]{1,0:T(8,128)(2,1)}), bf16[2048,1024]{1,0:T(8,128)(2,1)}) %all-gather.20.cloned.1.call-update) | async-done | bytes 4194320 | tf_op jit(solution)/shard_map/all_gather | solution.py:38
  399.3 32.1 %all-gather.16.cloned.1.call-done = bf16[1024,1024]{1,0:T(8,128)(2,1)} async-done(((bf16[128,1024]{1,0:T(8,128)(2,1)}), bf16[1024,1024]{1,0:T(8,128)(2,1)}) %all-gather.16.cloned.1.call-update) | async-done | bytes 2097168 | tf_op jit(solution)/shard_map/all_gather | solution.py:186
  431.4 35.2 %all-gather.14.cloned.1.call-done = bf16[2048,1024]{1,0:T(8,128)(2,1)} async-done(((bf16[512,1024]{1,0:T(8,128)(2,1)}), bf16[2048,1024]{1,0:T(8,128)(2,1)}) %all-gather.14.cloned.1.call-update) | async-done | bytes 4194320 | tf_op jit(solution)/shard_map/all_gather | solution.py:38
  466.7 27.2 %fusion.86 = (f32[2048]{0:T(1024)S(1)}, f32[2048]{0:T(1024)S(1)}, f32[2048,1024]{0,1:T(8,128)}, f32[2048,1024]{0,1:T(8,128)}, f32[2048,1024]{0,1:T(8,128)}) fusion(bf16[2048,1024]{1,0:T(8,128)(2,1)} %all-gather.14.cloned.1.call-done, bf16[1024,1024]{1,0:T(8,128)(2,1)} %all-gather.16.cloned.1.call-done), kind=kOutput, calls=%fused_computation.180 | convolution fusion | flops 4435472384 | bytes 31473664 | tf_op jit(solution)/shard_map/dot_general | solution.py:223
  521.9 15.4 add_convert_fusion
  546.1 12.0 fusion.101
  558.6 60.5 %reduce-scatter.28.cloned.1.call-done = f32[512,1024]{1,0:T(8,128)} async-done(((f32[2048,1024]{1,0:T(8,128)}), f32[512,1024]{1,0:T(8,128)}) %reduce-scatter.28.cloned.1.call-update) | async-done | bytes 2097168 | tf_op jit(solution)/shard_map/reduce_scatter | solution.py:42
  622.0 71.4 %reduce-scatter.26.cloned.1.call-done = f32[512,1024]{1,0:T(8,128)} async-done(((f32[2048,1024]{1,0:T(8,128)}), f32[512,1024]{1,0:T(8,128)}) %reduce-scatter.26.cloned.1.call-update) | async-done | bytes 2097168 | tf_op jit(solution)/shard_map/reduce_scatter | solution.py:42
  722.6 12.2 all-gather.22.cloned.1.call-done
  761.2 199.3 %while.28 = (s32[]{:T(128)}, f32[2048,4,64]{0,2,1:T(8,128)}, f32[2048,4,64]{0,2,1:T(8,128)}, bf16[4,512,4,64]{1,3,2,0:T(8,128)(2,1)}, s32[4]{0:T(128)S(1)}, /*in...) while((s32[]{:T(128)}, f32[2048,4,64]{0,2,1:T(8,128)}, ...), condition=%wide.region_33.34_spmd.clone, body=%wide.region_31.33_spmd.clone.sunk | while | flops 2751068160 | bytes 180984176 | solution.py:132
  776.8 11.5 multiply_reduce_fusion.20
  926.0 11.5 multiply_reduce_fusion.20
  1013.3 133.2 %reduce-scatter.42.cloned.1.call-done = f32[32,2]{1,0:T(8,128)} async-done(((f32[1024,2]{1,0:T(8,128)}), f32[32,2]{1,0:T(8,128)}) %reduce-scatter.42.cloned.1.call-update) | async-done | bytes 272
  1147.9 60.6 %reduce-scatter.36.cloned.1.call-done = bf16[128,256]{1,0:T(8,128)(2,1)} async-done(((bf16[1024,256]{1,0:T(8,128)(2,1)}), bf16[128,256]{1,0:T(8,128)(2,1)}) %reduce-scatter.36.cloned.1.call-update) | async-done | bytes 65552
  1210.7 65.4 %reduce-scatter.34.cloned.1.call-done = bf16[128,768]{1,0:T(8,128)(2,1)} async-done(((bf16[1024,768]{1,0:T(8,128)(2,1)}), bf16[128,768]{1,0:T(8,128)(2,1)}) %reduce-scatter.34.cloned.1.call-update) | async-done | bytes 196624
  1281.6 67.8 %reduce-scatter.30.cloned.1.call-done = f32[512,1024]{1,0:T(8,128)} async-done(((f32[2048,1024]{1,0:T(8,128)}), f32[512,1024]{1,0:T(8,128)}) %reduce-scatter.30.cloned.1.call-update) | async-done | bytes 2097168 | tf_op jit(solution)/shard_map/reduce_scatter | solution.py:42
  1355.8 133.6 %reduce-scatter.40.cloned.1.call-done = f32[32,4]{1,0:T(8,128)} async-done(((f32[1024,4]{1,0:T(8,128)}), f32[32,4]{1,0:T(8,128)}) %reduce-scatter.40.cloned.1.call-update) | async-done | bytes 528
  1496.6 36.9 %psum.71 = f32[]{:T(128)} all-reduce(f32[]{:T(128)S(6)} %add.322), channel_id=1, replica_groups=mesh['dp'=8,'mp'=4] {'dp','mp'}, use_global_device_ids=true, to_apply=%region_59.60 | all-reduce | flops 1 | bytes 8 | tf_op jit(solution)/shard_map/psum | solution.py:319
  (393 shorter events, 485.6 us)
Async XLA Ops:
  7.3 118.9 %all-gather.12.cloned.1.call-start = ((), (), s32[]{:S(2)}) async-start(), calls=%async_computation.12 | async-start | bytes 1769472 | tf_op jit(solution)/shard_map/all_gather | solution.py:184
  9.3 116.8 %all-gather.10.cloned.1.call-start = ((), (), s32[]{:S(2)}) async-start(), calls=%async_computation.11 | async-start | bytes 5242880 | tf_op jit(solution)/shard_map/all_gather | solution.py:38
  59.5 231.9 %reduce-scatter.24.cloned.1.call-start = ((), (), s32[]{:S(2)}) async-start(), calls=%async_computation.13 | async-start | bytes 10485760 | tf_op jit(solution)/shard_map/reduce_scatter | solution.py:42
  221.4 123.8 %all-gather.18.cloned.1.call-start = ((), (), s32[]{:S(2)}) async-start(), calls=%async_computation.16 | async-start | bytes 2359296 | tf_op jit(solution)/shard_map/all_gather | solution.py:187
  223.1 156.2 %all-gather.20.cloned.1.call-start = ((), (), s32[]{:S(2)}) async-start(), calls=%async_computation.18 | async-start | bytes 5242880 | tf_op jit(solution)/shard_map/all_gather | solution.py:38
  223.3 474.1 %copy-start.49 = (f32[512]{0:T(512)}, f32[512]{0:T(512)S(1)}, u32[]{:S(2)}) copy-start(f32[512]{0:T(512)S(1)} %fusion.77) | copy-start | bytes 6148
  224.5 206.9 %all-gather.16.cloned.1.call-start = ((), (), s32[]{:S(2)}) async-start(), calls=%async_computation.15 | async-start | bytes 2359296 | tf_op jit(solution)/shard_map/all_gather | solution.py:186
  225.4 241.3 %all-gather.14.cloned.1.call-start = ((), (), s32[]{:S(2)}) async-start(), calls=%async_computation.14 | async-start | bytes 5242880 | tf_op jit(solution)/shard_map/all_gather | solution.py:38
  295.0 324.1 %reduce-scatter.28.cloned.1.call-start = ((), (), s32[]{:S(2)}) async-start(), calls=%async_computation.19 | async-start | bytes 10485760 | tf_op jit(solution)/shard_map/reduce_scatter | solution.py:42
  546.1 147.4 %reduce-scatter.26.cloned.1.call-start = ((), (), s32[]{:S(2)}) async-start(), calls=%async_computation.17 | async-start | bytes 10485760 | tf_op jit(solution)/shard_map/reduce_scatter | solution.py:42
  558.1 176.6 %all-gather.22.cloned.1.call-start = ((), (), s32[]{:S(2)}) async-start(), calls=%async_computation.20 | async-start | bytes 5242880 | tf_op jit(solution)/shard_map/all_gather | solution.py:38
  700.1 297.1 %reduce-scatter.44.cloned.1.call-start = ((), (), s32[]{:S(2)}) async-start(), calls=%async_computation.28 | async-start | bytes 2162688
  702.2 296.5 %reduce-scatter.38.cloned.1.call-start = ((), (), s32[]{:S(2)}) async-start(), calls=%async_computation.25 | async-start | bytes 2359296
  712.9 298.0 %reduce-scatter.32.cloned.1.call-start = ((), (), s32[]{:S(2)}) async-start(), calls=%async_computation.22 | async-start | bytes 2359296 | tf_op jit(solution)/shard_map/reduce_scatter | solution.py:303
  722.5 424.0 %reduce-scatter.42.cloned.1.call-start = ((), (), s32[]{:S(2)}) async-start(), calls=%async_computation.27 | async-start | bytes 540672
  751.4 457.0 %reduce-scatter.36.cloned.1.call-start = ((), (), s32[]{:S(2)}) async-start(), calls=%async_computation.24 | async-start | bytes 589824
  758.0 518.2 %reduce-scatter.34.cloned.1.call-start = ((), (), s32[]{:S(2)}) async-start(), calls=%async_computation.23 | async-start | bytes 1769472
  985.6 363.9 %reduce-scatter.30.cloned.1.call-start = ((), (), s32[]{:S(2)}) async-start(), calls=%async_computation.21 | async-start | bytes 10485760 | tf_op jit(solution)/shard_map/reduce_scatter | solution.py:42
  994.4 355.0 %copy-start.7 = (bf16[512,1024]{1,0:T(8,128)(2,1)S(1)}, bf16[512,1024]{1,0:T(8,128)(2,1)}, u32[]{:S(2)}) copy-start(bf16[512,1024]{1,0:T(8,128)(2,1)} %param.28) | copy-start | bytes 3145732
  994.4 355.0 %copy-start.45 = (f32[1,1024]{1,0:T(1,128)S(1)}, f32[1,1024]{1,0:T(1,128)}, u32[]{:S(2)}) copy-start(f32[1,1024]{1,0:T(1,128)} %copy-done.44) | copy-start | bytes 12292
  994.4 355.0 %copy-start.47 = (f32[512]{0:T(512)S(1)}, f32[512]{0:T(512)}, u32[]{:S(2)}) copy-start(f32[512]{0:T(512)} %copy-done.46) | copy-start | bytes 6148
  994.4 495.0 %reduce-scatter.40.cloned.1.call-start = ((), (), s32[]{:S(2)}) async-start(), calls=%async_computation.26 | async-start | bytes 540672
  996.3 355.2 %copy-start.54 = (f32[512]{0:T(512)S(1)}, f32[512]{0:T(512)}, u32[]{:S(2)}) copy-start(f32[512]{0:T(512)} %copy-done.53) | copy-start | bytes 6148
  996.3 355.3 %copy-start.52 = (f32[512]{0:T(512)S(1)}, f32[512]{0:T(512)}, u32[]{:S(2)}) copy-start(f32[512]{0:T(512)} %copy-done.51) | copy-start | bytes 6148
  (78 other events, 3031.9 us)
Sparse Core Ops, SparseCore 0:
  10.7 48.0 all-gather.11
  60.9 32.8 all-gather.9
  221.5 69.8 reduce-scatter.23
  294.0 51.0 all-gather.17
  346.6 32.6 all-gather.19
  382.1 49.2 all-gather.15
  433.7 32.9 all-gather.13
  546.2 72.8 reduce-scatter.27
  621.7 71.7 reduce-scatter.25
  700.2 34.4 all-gather.21
  737.1 136.7 reduce-scatter.43
  877.3 63.4 reduce-scatter.37
  944.3 66.5 reduce-scatter.31
  1013.5 132.8 reduce-scatter.41
  1150.6 57.8 reduce-scatter.35
  1212.3 63.7 reduce-scatter.33
  1278.7 70.6 reduce-scatter.29
  1355.4 134.0 reduce-scatter.39
where the time goes:
time: 1560 us
  waiting for transfers between devices  791 us (51%)
  matrix products  285 us (18%)
  blocking collectives  229 us (15%)
  other arithmetic  148 us (9%)
  local copies, waits for them, and re-layouts  67.9 us (4%)
  between operations  21.9 us (1%)
    unnamed x24, waiting for transfers between devices  393 us
    reduce_scatter x4, waiting for transfers between devices, sum_rows(): lax.psum_scatter(term(jnp.int32(0), lax.axis_size('mp') * height), 'mp',...  266 us
    all_gather x4, waiting for transfers between devices, spread_rows(): return lax.all_gather(block_rows, 'mp', axis=0, tiled=True)  81.6 us
    dot_general x4, matrix products, one_block(): jnp.einsum('qhd,khd->hqk', grad_part, values, preferred_element_type=jnp....  46 us
    all_gather x1, blocking collectives, local(): lax.all_gather(outer_norms, ('dp', 'mp'), axis=1, tiled=True)  44.2 us
    convert_element_type x4, other arithmetic, one_block(): score_back = (probs * centered).astype(jnp.bfloat16)  44.1 us
    psum x4, blocking collectives, token_totals(): return lax.psum((first, second), 'mp')  41.5 us
    all_gather x1, blocking collectives, local(): lax.all_gather(unit_norms, ('dp', 'mp'), axis=1, tiled=True)  40.8 us
  transfers between devices with their start and end apart: 18, of which 14 were waited for; matrix products, arithmetic and copies ran while one was open for 21% of the time, Pallas kernels for 0%

commit v1 on v0

v1 whole, which is shorter than its diff:
```python
from functools import partial

import jax
import jax.numpy as jnp
from jax import lax
from jax.experimental import pallas as pl
from jax.experimental.pallas import tpu as pltpu
from jax.sharding import PartitionSpec as P

D = 1024
HD = 64
FF = 4096
ADAM_STEP = 10

NORM_EPS = 1e-05
MASKED = -1e30
RATE = 0.02
BETA_ONE = 0.9
BETA_TWO = 0.95
ADAM_EPS = 1e-08
DECAY = 0.1
MAX_NORM = 1.0

BF = jnp.bfloat16
F32 = jnp.float32
ALL = ("dp", "mp")


def swap(value, bit):
    count = lax.axis_size("mp")
    return lax.ppermute(value, "mp", [(i, i ^ bit) for i in range(count)])


def mp_bits():
    count = lax.axis_size("mp")
    return [1 << b for b in range(count.bit_length() - 1)]


def gather_blocks(own):
    blocks = {0: own}
    for bit in reversed(mp_bits()):
        for r in list(blocks):
            blocks[r | bit] = swap(blocks[r], bit)
    return [blocks[r] for r in range(len(blocks))]


def sum_blocks(blocks):
    current = dict(enumerate(blocks))
    for bit in mp_bits():
        for r in [r for r in current if r & bit]:
            received = swap(current.pop(r).astype(BF), bit)
            current[r ^ bit] = current[r ^ bit].astype(F32) + received.astype(F32)
    return current[0]


def token_totals(first, second):
    count = lax.axis_size("mp")
    both = jnp.stack([first, second]).reshape(2, count, -1)
    for bit in mp_bits():
        received = swap(both, bit)
        both = both + jnp.stack([received[:, r ^ bit] for r in range(count)], axis=1)
    flat = both.reshape(2, -1)
    return flat[0], flat[1]


def exchange_all(value):
    return lax.all_to_all(value, ALL, 0, 0, tiled=True)


def norm_rows(value):
    mean = jnp.mean(value, axis=-1, keepdims=True)
    centered = value - mean
    variance = jnp.mean(centered * centered, axis=-1, keepdims=True)
    factor = lax.rsqrt(variance + NORM_EPS)
    return centered * factor, factor


def norm_back(grad, normed, factor, gain):
    weighted = grad * gain
    result = factor * (
        weighted
        - jnp.mean(weighted, axis=-1, keepdims=True)
        - normed * jnp.mean(weighted * normed, axis=-1, keepdims=True)
    )
    return result, jnp.sum(grad * normed, axis=0), jnp.sum(grad, axis=0)


def split_norm(value, width):
    first, second = token_totals(jnp.sum(value, axis=1), jnp.sum(value * value, axis=1))
    mean = first / width
    variance = second / width - mean * mean
    factor = lax.rsqrt(variance + NORM_EPS)
    return (value - mean[:, None]) * factor[:, None], factor


def split_norm_back(grad, normed, factor, gain, width):
    weighted = grad * gain
    first, second = token_totals(jnp.sum(weighted, axis=1), jnp.sum(weighted * normed, axis=1))
    result = factor[:, None] * (
        weighted - first[:, None] / width - normed * (second[:, None] / width)
    )
    return (result, jnp.sum(grad * normed, axis=0), jnp.sum(grad, axis=0))


def dot(left, right, left_dim, right_dim):
    return lax.dot_general(
        left, right, (((left_dim,), (right_dim,)), ((), ())), preferred_element_type=F32
    )


def segments_at(rows, table_ref, count):
    slots = rows ^ table_ref[count]
    end = jnp.int32(0)
    segment = jnp.zeros(rows.shape, jnp.int32)
    for i in range(count):
        end = end + table_ref[i]
        segment = segment + (slots >= end).astype(jnp.int32)
    return segment


def forward_kernel(table_ref, q_ref, k_ref, v_ref, o_ref, log_ref, *, block, heads, count):
    length, width = k_ref.shape
    start = pl.program_id(0) * block
    rows = start + lax.broadcasted_iota(jnp.int32, (block, 1), 0)
    columns = lax.broadcasted_iota(jnp.int32, (1, length), 1)
    allowed = segments_at(rows, table_ref, count) == segments_at(columns, table_ref, count)
    lane = lax.broadcasted_iota(jnp.int32, (1, width), 1) // HD
    query = q_ref[...] * BF(HD**-0.5)
    keys = k_ref[...]
    values = v_ref[...]
    out = jnp.zeros((block, width), F32)
    logs = []
    for h in range(heads):
        one = jnp.where(lane == h, query, jnp.zeros_like(query))
        scores = jnp.where(allowed, dot(one, keys, 1, 1), MASKED)
        highest = jnp.max(scores, axis=1, keepdims=True)
        weights = jnp.exp(scores - highest)
        total = jnp.sum(weights, axis=1, keepdims=True)
        mixed = dot(weights.astype(BF), values, 1, 0)
        out = jnp.where(lane == h, mixed * (1.0 / total), out)
        logs.append(highest + jnp.log(total))
    o_ref[...] = out.astype(BF)
    spread = 128 // heads
    logs = jnp.concatenate([jnp.broadcast_to(x, (block, spread)) for x in logs], axis=1)
    turned = jnp.transpose(logs)
    log_ref[...] = jnp.zeros_like(log_ref)
    for h in range(heads):
        log_ref[h : h + 1, :] = turned[h * spread : h * spread + 1, :]


def attention_forward(projected, table):
    length, width = projected.shape[0], projected.shape[1] // 3
    heads = width // HD
    block = min(512, length)
    return pl.pallas_call(
        partial(forward_kernel, block=block, heads=heads, count=table.shape[0] - 1),
        grid_spec=pltpu.PrefetchScalarGridSpec(
            num_scalar_prefetch=1,
            grid=(length // block,),
            in_specs=[
                pl.BlockSpec((block, width), lambda i, t: (i, 0)),
                pl.BlockSpec((length, width), lambda i, t: (0, 1)),
                pl.BlockSpec((length, width), lambda i, t: (0, 2)),
            ],
            out_specs=[
                pl.BlockSpec((block, width), lambda i, t: (i, 0)),
                pl.BlockSpec((8, block), lambda i, t: (0, i)),
            ],
        ),
        out_shape=[
            jax.ShapeDtypeStruct((length, width), BF),
            jax.ShapeDtypeStruct((8, length), F32),
        ],
        cost_estimate=pl.CostEstimate(
            flops=16 * length * length * width,
            transcendentals=heads * length * length,
            bytes_accessed=8 * length * width,
        ),
        compiler_params=pltpu.CompilerParams(vmem_limit_bytes=48 << 20),
        name="attention_forward",
    )(table, projected, projected, projected)


def backward_kernel(
    table_ref, q_ref, k_ref, v_ref, g_ref, o_ref, log_ref, out_q, out_k, out_v, sums, dots, *, block, heads, count
):
    length, width = q_ref.shape
    step = pl.program_id(0)
    lane = lax.broadcasted_iota(jnp.int32, (1, width), 1) // HD
    grad = g_ref[...]

    @pl.when(step == 0)
    def _():
        sums[...] = jnp.zeros_like(sums)
        picks = (
            lax.broadcasted_iota(jnp.int32, (8, width), 0)
            == lax.broadcasted_iota(jnp.int32, (8, width), 1) // HD
        ).astype(F32)
        products = grad.astype(F32) * o_ref[...].astype(F32)
        dots[...] = lax.dot_general(
            picks,
            products,
            (((1,), (1,)), ((), ())),
            precision=lax.Precision.HIGHEST,
            preferred_element_type=F32,
        )

    rows = step * block + lax.broadcasted_iota(jnp.int32, (block, 1), 0)
    columns = lax.broadcasted_iota(jnp.int32, (1, length), 1)
    allowed = segments_at(rows, table_ref, count) == segments_at(columns, table_ref, count)
    query = q_ref[...] * BF(HD**-0.5)
    keys = k_ref[...]
    values = v_ref[...]
    none = jnp.zeros_like(keys)
    key_back = jnp.zeros((block, width), F32)
    value_back = jnp.zeros((block, width), F32)
    for h in range(heads):
        key = jnp.where(lane == h, keys, none)
        value = jnp.where(lane == h, values, none)
        scores = jnp.where(allowed, dot(key, query, 1, 1), MASKED)
        probs = jnp.exp(scores - log_ref[h : h + 1, :])
        probs_back = dot(value, grad, 1, 1)
        score_back = (probs * (probs_back - dots[h : h + 1, :])).astype(BF)
        value_back = jnp.where(lane == h, dot(probs.astype(BF), grad, 1, 0), value_back)
        key_back = jnp.where(lane == h, dot(score_back, query, 1, 0), key_back)
        sums[...] += dot(score_back, key, 0, 0)
    out_k[...] = key_back.astype(BF)
    out_v[...] = value_back.astype(BF)

    @pl.when(step == pl.num_programs(0) - 1)
    def _():
        out_q[...] = (sums[...] * HD**-0.5).astype(BF)


def attention_backward(projected, table, grad, attended, logs):
    length, width = grad.shape
    heads = width // HD
    block = min(512, length)
    whole = pl.BlockSpec((length, width), lambda i, t: (0, 0))
    return pl.pallas_call(
        partial(backward_kernel, block=block, heads=heads, count=table.shape[0] - 1),
        grid_spec=pltpu.PrefetchScalarGridSpec(
            num_scalar_prefetch=1,
            grid=(length // block,),
            in_specs=[
                whole,
                pl.BlockSpec((block, width), lambda i, t: (i, 1)),
                pl.BlockSpec((block, width), lambda i, t: (i, 2)),
                whole,
                whole,
                pl.BlockSpec((8, length), lambda i, t: (0, 0)),
            ],
            out_specs=[
                whole,
                pl.BlockSpec((block, width), lambda i, t: (i, 0)),
                pl.BlockSpec((block, width), lambda i, t: (i, 0)),
            ],
            scratch_shapes=[pltpu.VMEM((length, width), F32), pltpu.VMEM((8, length), F32)],
        ),
        out_shape=[jax.ShapeDtypeStruct((length, width), BF)] * 3,
        cost_estimate=pl.CostEstimate(
            flops=40 * length * length * width,
            transcendentals=heads * length * length,
            bytes_accessed=16 * length * width,
        ),
        compiler_params=pltpu.CompilerParams(vmem_limit_bytes=56 << 20),
        name="attention_backward",
    )(table, projected, projected, projected, grad, attended, logs)


def adamw(param, grad, moment, square, clip, fix_one, fix_two):
    clipped = grad * clip
    moment_new = BETA_ONE * moment + (1.0 - BETA_ONE) * clipped
    square_new = BETA_TWO * square + (1.0 - BETA_TWO) * clipped * clipped
    change = -RATE * (
        moment_new / fix_one / (jnp.sqrt(square_new / fix_two) + ADAM_EPS) + DECAY * param
    )
    return (moment_new, square_new, change)


def local(
    tokens,
    cotangent,
    lengths,
    attend,
    mixing,
    expand,
    contract,
    outer_norms,
    head_norms,
    unit_norms,
    attend_moment,
    mixing_moment,
    expand_moment,
    contract_moment,
    outer_moment,
    head_moment,
    unit_moment,
    attend_square,
    mixing_square,
    expand_square,
    contract_square,
    outer_square,
    head_square,
    unit_square,
):
    height = tokens.shape[0]
    shard_count = lax.axis_size("mp")
    device_count = lax.axis_size("dp") * shard_count
    length_all = height * shard_count
    place = lax.axis_index("mp")
    sequences = lengths.shape[1]
    head_width = attend.shape[2]
    unit_width = expand.shape[1]
    shard = attend.shape[1]

    work_in = lax.all_gather(
        attend.astype(BF).transpose(1, 0, 2).reshape(shard, 3 * head_width), "dp", axis=0, tiled=True
    )
    work_mix = lax.all_gather(mixing.astype(BF).T, "dp", axis=0, tiled=True)
    work_exp = lax.all_gather(expand.astype(BF), "dp", axis=0, tiled=True)
    work_con = lax.all_gather(contract.astype(BF).T, "dp", axis=0, tiled=True)

    sizes = [x.size for x in (outer_norms, head_norms, unit_norms)]
    packed = jnp.concatenate([outer_norms.reshape(-1), head_norms.reshape(-1), unit_norms.reshape(-1)])
    tables = exchange_all(jnp.broadcast_to(packed[None], (device_count, packed.shape[0])))

    def unpack(start, rows):
        part = tables[:, start : start + sizes_at(start)].reshape(device_count, rows, -1)
        return part.transpose(1, 0, 2).reshape(rows, -1)

    def sizes_at(start):
        return {0: sizes[0], sizes[0]: sizes[1], sizes[0] + sizes[1]: sizes[2]}[start]

    outer = unpack(0, 4)
    head_gain = unpack(sizes[0], 2)
    unit_gain = unpack(sizes[0] + sizes[1], 2)
    head_local = lax.dynamic_slice_in_dim(head_gain, place * head_width, head_width, 1)
    unit_local = lax.dynamic_slice_in_dim(unit_gain, place * unit_width, unit_width, 1)

    table = jnp.concatenate([lengths[0], (place * height)[None].astype(jnp.int32)])
    slots = jnp.arange(length_all, dtype=jnp.int32) ^ (place * height)
    live_all = slots < jnp.sum(lengths)
    live = live_all[:height].astype(F32)[:, None]

    token_blocks = gather_blocks(tokens)
    tokens_all = jnp.concatenate(token_blocks, axis=0)
    normed_all = (norm_rows(tokens_all.astype(F32))[0] * outer[0] + outer[1]).astype(BF)
    projected = jnp.dot(normed_all, work_in, preferred_element_type=F32).astype(BF)

    back_raw = jnp.concatenate(gather_blocks(cotangent), axis=0)
    back_all = jnp.where(live_all[:, None], back_raw, jnp.zeros_like(back_raw))

    attended, logs = attention_forward(projected, table)
    head_normed, head_factor = split_norm(attended.astype(F32), D)
    mixed_in = (head_normed * head_local[0] + head_local[1]).astype(BF)

    def row_blocks(value):
        return [value[r * height : (r + 1) * height] for r in range(shard_count)]

    branch = sum_blocks(row_blocks(dot(mixed_in, work_mix, 1, 1).astype(BF)))
    inputs = tokens.astype(F32)
    middle = inputs + branch
    mid_normed, mid_factor = norm_rows(middle)
    mid_own = (mid_normed * outer[2] + outer[3]).astype(BF)
    mid_all = jnp.concatenate(gather_blocks(mid_own), axis=0)

    widened = jnp.dot(mid_all, work_exp, preferred_element_type=F32)
    activated, gelu_pull = jax.vjp(partial(jax.nn.gelu, approximate=False), widened)
    unit_normed, unit_factor = split_norm(activated, FF)
    unit_low = (unit_normed * unit_local[0] + unit_local[1]).astype(BF)
    feed = sum_blocks(row_blocks(dot(unit_low, work_con, 1, 1).astype(BF)))
    result = middle + feed

    back_out = cotangent.astype(F32) * live
    contract_back = dot(back_all, unit_low, 0, 0)
    unit_in = dot(back_all, work_con, 1, 0)
    unit_back, unit_gain_back, unit_bias_back = split_norm_back(
        unit_in, unit_normed, unit_factor, unit_local[0], FF
    )
    (widened_back,) = gelu_pull(unit_back)
    widened_low = widened_back.astype(BF)
    mid_in = sum_blocks(row_blocks(dot(widened_low, work_exp, 1, 1).astype(BF)))
    expand_back = dot(mid_all, widened_low, 0, 0)
    middle_part, gain_two, bias_two = norm_back(mid_in, mid_normed, mid_factor, outer[2])
    middle_back = back_out + middle_part
    middle_all = jnp.concatenate(gather_blocks(middle_back.astype(BF)), axis=0)
    mixed_back = dot(middle_all, work_mix, 1, 0)
    mixing_back = dot(middle_all, mixed_in, 0, 0)
    heads_back, head_gain_back, head_bias_back = split_norm_back(
        mixed_back, head_normed, head_factor, head_local[0], D
    )
    attended_back = heads_back.astype(BF)
    query_back, key_back, value_back = attention_backward(
        projected, table, attended_back, attended, logs
    )
    projected_back = jnp.concatenate([query_back, key_back, value_back], axis=1)
    attend_back = dot(normed_all, projected_back, 0, 0)
    normed_back = sum_blocks(row_blocks(dot(projected_back, work_in, 1, 1).astype(BF)))
    first_normed, first_factor = norm_rows(inputs)
    input_part, gain_one, bias_one = norm_back(normed_back, first_normed, first_factor, outer[0])
    input_grad = middle_back + input_part

    def scatter(value):
        return lax.psum_scatter(value.astype(BF), "dp", scatter_dimension=0, tiled=True).astype(F32)

    contract_grad = scatter(contract_back).T
    expand_grad = scatter(expand_back)
    mixing_grad = scatter(mixing_back).T
    attend_grad = scatter(attend_back).reshape(shard, 3, head_width).transpose(1, 0, 2)

    def widen(parts, width, full):
        return lax.dynamic_update_slice_in_dim(
            jnp.zeros((2, full), F32), jnp.stack(parts), place * width, 1
        )

    def for_owners(value):
        return value.reshape(value.shape[0], device_count, -1).transpose(1, 0, 2).reshape(device_count, -1)

    terms = jnp.concatenate(
        [
            for_owners(jnp.stack([gain_one, bias_one, gain_two, bias_two])),
            for_owners(widen([head_gain_back, head_bias_back], head_width, D)),
            for_owners(widen([unit_gain_back, unit_bias_back], unit_width, FF)),
        ],
        axis=1,
    )
    sums = jnp.sum(exchange_all(terms), axis=0)
    outer_grad = sums[: sizes[0]].reshape(outer_norms.shape)
    head_grad = sums[sizes[0] : sizes[0] + sizes[1]].reshape(head_norms.shape)
    unit_grad = sums[sizes[0] + sizes[1] :].reshape(unit_norms.shape)

    gradients = (attend_grad, mixing_grad, expand_grad, contract_grad, outer_grad, head_grad, unit_grad)
    local_squares = jnp.float32(0.0)
    for gradient in gradients:
        local_squares = local_squares + jnp.sum(gradient * gradient)
    all_squares = exchange_all(jnp.broadcast_to(local_squares, (device_count, 128)))
    norm = jnp.sqrt(jnp.sum(all_squares[:, 0]))
    clip = jnp.minimum(1.0, MAX_NORM / (norm + 1e-06))
    count_steps = jnp.float32(ADAM_STEP)
    fix_one = 1.0 - jnp.power(jnp.float32(BETA_ONE), count_steps)
    fix_two = 1.0 - jnp.power(jnp.float32(BETA_TWO), count_steps)
    params = (attend, mixing, expand, contract, outer_norms, head_norms, unit_norms)
    moments = (
        attend_moment,
        mixing_moment,
        expand_moment,
        contract_moment,
        outer_moment,
        head_moment,
        unit_moment,
    )
    squares = (
        attend_square,
        mixing_square,
        expand_square,
        contract_square,
        outer_square,
        head_square,
        unit_square,
    )
    results = [result.astype(BF), input_grad, norm]
    for param, gradient, moment, square in zip(params, gradients, moments, squares):
        results.append(gradient)
        results.extend(adamw(param, gradient, moment, square, clip, fix_one, fix_two))
    return tuple(results)


def solution(mesh):
    rows = P(ALL, None)
    norms = P(None, ALL)
    weights = (P(None, "dp", "mp"), P("mp", "dp"), P("dp", "mp"), P("mp", "dp"))
    states = weights + (norms,) * 3
    outs = (rows, rows, P())
    for spec in states:
        outs = outs + (spec,) * 4
    return jax.shard_map(
        local,
        mesh=mesh,
        in_specs=(rows, rows, P("dp", None)) + states * 3,
        out_specs=outs,
        check_vma=False,
    )
```

time: 1560 us -> 641 us (0.41)
  waiting for transfers between devices: 791 us -> 226 us
  blocking collectives: 229 us -> 27.8 us
  matrix products: 285 us -> 98.7 us
  Pallas kernels: 0 us -> 86.1 us
  other arithmetic: 148 us -> 87.8 us
  starting transfers between devices: 1.41 us -> 32 us
    unnamed x24 -> x7, waiting for transfers between devices: 393 us -> 0.11 us
    reduce_scatter x5 -> x4, waiting for transfers between devices: 275 us -> 51.8 us  [scatter(): lax.psum_scatter(value.astype(BF), 'dp', scatter_dimension=0, tiled=True)]
    dot_general x40 -> x12, matrix products: 285 us -> 98.7 us  [the longest x10 61.4 us: dot(): lax.dot_general(left, right, (((left_dim,), (right_dim,)), ((), ())), pre...]
    ppermute x0 -> x32, waiting for transfers between devices: none -> 159 us  [swap(): return lax.ppermute(value, 'mp', [(i, i ^ bit) for i in range(count)])]
    all_gather x4 -> x1, blocking collectives: 151 us -> 27.8 us  [local(): work_mix = lax.all_gather(mixing.astype(BF).T, 'dp', axis=0, tiled=True)]
    all_gather x7 -> x3, waiting for transfers between devices: 123 us -> 0.98 us  [the longest x1 0.98 us: local(): lax.all_gather(attend.astype(BF).transpose(1, 0, 2).reshape(shard, 3 * he...]
    pallas_call x0 -> x2, Pallas kernels: none -> 86.1 us  [the longest x1 54.3 us: attention_backward(): pl.pallas_call(partial(backward_kernel, block=block, heads=heads, count=t...]
    psum x5 -> x0, blocking collectives: 78.4 us -> none  [the longest x4 41.5 us: token_totals(): return lax.psum((first, second), 'mp')]
  transfers between devices with their start and end apart: 18 -> 42, of which waited for: 14 -> 20; matrix products, arithmetic and copies ran while one was open for 21% -> 27% of each run, Pallas kernels for 0% -> 9%
where the time goes in v1:
time: 641 us; the launch traced here: 635 us
  waiting for transfers between devices  226 us (35%)
  matrix products  98.7 us (15%)
  other arithmetic  87.8 us (14%)
  Pallas kernels  86.1 us (13%)
  local copies, waits for them, and re-layouts  55.2 us (9%)
  starting transfers between devices  32 us (5%)
  blocking collectives  27.8 us (4%)
  between operations  22 us (3%)
    ppermute x32, waiting for transfers between devices, swap(): return lax.ppermute(value, 'mp', [(i, i ^ bit) for i in range(count)])  159 us
    dot_general x10, matrix products, dot(): lax.dot_general(left, right, (((left_dim,), (right_dim,)), ((), ())), pre...  61.4 us
    pallas_call x1, Pallas kernels, attention_backward(): pl.pallas_call(partial(backward_kernel, block=block, heads=heads, count=t...  54.3 us
    reduce_scatter x4, waiting for transfers between devices, scatter(): lax.psum_scatter(value.astype(BF), 'dp', scatter_dimension=0, tiled=True)  51.8 us
    unnamed x191, local copies, waits for them, and re-layouts  32.7 us
    pallas_call x1, Pallas kernels, attention_forward(): pl.pallas_call(partial(forward_kernel, block=block, heads=heads, count=ta...  31.8 us
    dot_general x1, matrix products, local(): widened = jnp.dot(mid_all, work_exp, preferred_element_type=F32)  28.9 us
    all_gather x1, blocking collectives, local(): work_mix = lax.all_gather(mixing.astype(BF).T, 'dp', axis=0, tiled=True)  27.8 us
  transfers between devices with their start and end apart: 42, of which 20 were waited for; matrix products, arithmetic and copies ran while one was open for 27% of the time, Pallas kernels for 9%

profile of v1, /device:TPU:0, one launch (start us, length us, event | category | flops | bytes accessed | tf_op | source)
XLA Modules:
  0.0 635.1 jit_solution(12028067235491167288)
XLA Ops:
  12.3 21.3 %collective-permute-done.1 = bf16[512,1024]{1,0:T(8,128)(2,1)S(1)} collective-permute-done((bf16[512,1024]{1,0:T(8,128)(2,1)}, bf16[512,1024]{1,0:T(8,128)(2,1)S(1)}, u32[]{:S(2)}, u32[]{:S(2)}) %collective-permute-start.1) | collective-permute-done | bytes 1048608 | tf_op jit(solution)/shard_map/ppermute | solution.py:31
  44.5 6.6 %all-to-all-done = f32[32,1,448]{2,1,0:T(1,128)S(1)} async-done(((f32[32,1,448]{2,1,0:T(1,128)}), f32[32,1,448]{2,1,0:T(1,128)S(1)}, u32[]{:S(2)}, u32[]{:S(2)}) %all-to-all-start) | async-done | bytes 57376 | tf_op jit(solution)/shard_map/all_to_all | solution.py:67
  59.4 8.3 %convolution_convert_fusion.4.q_ref.k_ref.v_ref = bf16[2048,768]{1,0:T(8,128)(2,1)S(1)} fusion(bf16[1024,768]{0,1:T(8,128)(2,1)} %all-gather.4.cloned.1.call-done, f32[1024]{0:T(1024)S(1)} %add.297, f32[1024]{0:T(1024)S(1)} %mul.566, f32[2048]{0:T(1024)S(1)} %add_rsqrt_fusion.2, f32[2048]{0:T(1024)S(1)} %broadcast_multiply_fusion, ...), kind=kOutput, calls=%fused_computation.39 | convolution fusion | flops 3250061312 | bytes 8937472 | tf_op jit(solution)/shard_map/dot_general | solution.py:349
  67.8 31.8 %attention_forward.1 = (bf16[2048,256]{1,0:T(8,128)(2,1)S(1)}, f32[8,2048]{1,0:T(8,128)S(1)}) custom-call(s32[5]{0:T(128)S(1)} %pad_add_fusion.table_ref, bf16[2048,768]{1,0:T(8,128)(2,1)S(1)} %convolution_convert_fusion.4.q_ref.k_ref.v_ref, bf16[2048,768]{1,0:T(8,128)(2,1)S(1)} %convolution_convert_fusion.4.q_ref.k_ref.v_ref, ...), custom_call_target="tpu_custom_call" | custom-call | flops 17179869184 | bytes 4194304 | tf_op jit(solution)/shard_map/attention_forward/pallas_call | solution.py:155
  100.9 27.8 %all_gather.13 = bf16[1024,256]{0,1:T(8,128)(2,1)S(1)} all-gather(bf16[128,256]{0,1:T(8,128)(2,1)S(1)} %convert_bitcast_fusion.3), channel_id=1, replica_groups=mesh['dp'=8,'mp'=4] {'dp'}, dimensions={0}, use_global_device_ids=true | all-gather | bytes 589824 | tf_op jit(solution)/shard_map/all_gather | solution.py:320
  145.0 21.7 %collective-permute-done.7 = bf16[512,1024]{1,0:T(8,128)(2,1)} collective-permute-done((bf16[512,1024]{1,0:T(8,128)(2,1)}, bf16[512,1024]{1,0:T(8,128)(2,1)}, u32[]{:S(2)}, u32[]{:S(2)}) %collective-permute-start.7) | collective-permute-done | bytes 1048608 | tf_op jit(solution)/shard_map/ppermute | solution.py:31
  174.0 24.4 %collective-permute-done.9 = bf16[512,1024]{1,0:T(8,128)(2,1)} collective-permute-done((bf16[512,1024]{1,0:T(8,128)(2,1)}, bf16[512,1024]{1,0:T(8,128)(2,1)}, u32[]{:S(2)}, u32[]{:S(2)}) %collective-permute-start.9) | collective-permute-done | bytes 1048608 | tf_op jit(solution)/shard_map/ppermute | solution.py:31
  201.5 17.9 %collective-permute-done.17 = bf16[512,1024]{1,0:T(8,128)(2,1)} collective-permute-done((bf16[512,1024]{1,0:T(8,128)(2,1)S(1)}, bf16[512,1024]{1,0:T(8,128)(2,1)}, u32[]{:S(2)}, u32[]{:S(2)}) %collective-permute-start.17) | collective-permute-done | bytes 1048608 | tf_op jit(solution)/shard_map/ppermute | solution.py:31
  219.4 28.9 %multiply_reduce_fusion.2 = (f32[2048]{0:T(1024)S(1)}, f32[2048]{0:T(1024)S(1)}, f32[2048,1024]{0,1:T(8,128)}, f32[2048,1024]{0,1:T(8,128)}, f32[2048,1024]{0,1:T(8,128)}) fusion(bf16[1024,1024]{1,0:T(8,128)(2,1)} %all-gather.6.cloned.1.call-done, bf16[512,1024]{1,0:T(8,128)(2,1)} %collective-permute-done.10, bf16[512,1024]{1,0:T(8,128)(2,1)} %collective-permute-done.9, ...), kind=kOutput, calls=%fused_computation.15 | convolution fusion | flops 4452249600 | bytes 31473664 | tf_op jit(solution)/shard_map/dot_general | solution.py:368
  251.5 10.6 %fusion.88 = (f32[1024]{0:T(1024)}, f32[2048,1024]{1,0:T(8,128)}) fusion(bf16[1024,1024]{0,1:T(8,128)(2,1)} %all-gather.8.cloned.1.call-done, bf16[512,1024]{1,0:T(8,128)(2,1)} %collective-permute-done.18, bf16[512,1024]{1,0:T(8,128)(2,1)} %collective-permute-done.17, bf16[512,1024]{1,0:T(8,128)(2,1)} %collective-permute-done.16, ...), kind=kOutput, calls=%fused_computation.219 | convolution fusion | flops 4315937792 | bytes 14686208 | tf_op jit(solution)/shard_map/dot_general | solution.py:106
  262.1 9.2 %copy.182 = f32[2048,1024]{0,1:T(8,128)} copy(f32[2048,1024]{1,0:T(8,128)} %get-tuple-element.335) | data formatting | bytes 16777216 | tf_op jit(solution)/shard_map/dot_general | solution.py:106
  271.4 7.9 %multiply_reduce_fusion = (f32[1024]{0:T(1024)}, f32[2048]{0:T(1024)S(1)}, f32[2048]{0:T(1024)S(1)}) fusion(f32[2048,1024]{0,1:T(8,128)} %copy.182, f32[2048,1024]{0,1:T(8,128)} %get-tuple-element.276, f32[2048]{0:T(1024)S(1)} %add_rsqrt_fusion, f32[2048]{0:T(1024)S(1)} %bitcast.112, f32[1024]{0:T(1024)S(1)} %bitcast.125), kind=kLoop, calls=%fused_computation.10 | loop fusion | flops 16772096 | bytes 16818176 | tf_op jit(solution)/shard_map/reduce_sum | solution.py:102
  284.5 13.4 %add_convert_fusion = (bf16[2048,1024]{0,1:T(8,128)(2,1)S(1)}, bf16[2048,1024]{0,1:T(8,128)(2,1)S(1)}) fusion(f32[2048,1024]{0,1:T(8,128)} %get-tuple-element.277, f32[2048,1024]{0,1:T(8,128)} %get-tuple-element.332, f32[2048,1024]{0,1:T(8,128)} %copy.182, f32[2048,1024]{0,1:T(8,128)} %get-tuple-element.276, f32[2048]{0:T(1024)S(1)} %bitcast.128, ...), kind=kLoop, calls=%fused_computation.11 | loop fusion | flops 50331648 | bytes 41984000 | tf_op jit(solution)/shard_map/convert_element_type | solution.py:382
  314.8 8.1 %convolution_convert_fusion.5 = bf16[1024,1024]{1,0:T(8,128)(2,1)} fusion(bf16[2048,1024]{0,1:T(8,128)(2,1)S(1)} %get-tuple-element.281, bf16[512,1024]{1,0:T(8,128)(2,1)} %collective-permute-done.18, bf16[512,1024]{1,0:T(8,128)(2,1)} %collective-permute-done.17, bf16[512,1024]{1,0:T(8,128)(2,1)} %collective-permute-done.16, ...), kind=kOutput, calls=%fused_computation.83 | convolution fusion | flops 4314890240 | bytes 10487808 | tf_op jit(solution)/shard_map/dot_general | solution.py:106
  329.5 21.7 %collective-permute-done.23 = bf16[512,1024]{1,0:T(8,128)(2,1)S(1)} collective-permute-done((bf16[512,1024]{1,0:T(8,128)(2,1)S(1)}, bf16[512,1024]{1,0:T(8,128)(2,1)S(1)}, u32[]{:S(2)}, u32[]{:S(2)}) %collective-permute-start.23) | collective-permute-done | bytes 1048608 | tf_op jit(solution)/shard_map/ppermute | solution.py:31
  353.0 19.7 %collective-permute-done.15 = bf16[512,1024]{1,0:T(8,128)(2,1)S(1)} collective-permute-done((bf16[512,1024]{1,0:T(8,128)(2,1)S(1)}, bf16[512,1024]{1,0:T(8,128)(2,1)S(1)}, u32[]{:S(2)}, u32[]{:S(2)}) %collective-permute-start.15) | collective-permute-done | bytes 1048608 | tf_op jit(solution)/shard_map/ppermute | solution.py:31
  378.2 8.1 %convolution_convert_fusion.6 = bf16[1024,1024]{1,0:T(8,128)(2,1)} fusion(bf16[2048,1024]{0,1:T(8,128)(2,1)S(1)} %copy-done.12, bf16[512,1024]{1,0:T(8,128)(2,1)} %collective-permute-done.10, bf16[512,1024]{1,0:T(8,128)(2,1)} %collective-permute-done.9, bf16[512,1024]{1,0:T(8,128)(2,1)} %collective-permute-done.8, bf16[512,1024]{1,0:T(8,128)(2,1)} %add_convert_fusion.6), kind=kOutput, calls=%fused_computation.84 | convolution fusion | flops 4312793088 | bytes 10485760 | tf_op jit(solution)/shard_map/dot_general | solution.py:106
  386.6 15.8 %collective-permute-done.25 = bf16[512,1024]{1,0:T(8,128)(2,1)} collective-permute-done((bf16[512,1024]{1,0:T(8,128)(2,1)}, bf16[512,1024]{1,0:T(8,128)(2,1)}, u32[]{:S(2)}, u32[]{:S(2)}) %collective-permute-start.25) | collective-permute-done | bytes 1048608 | tf_op jit(solution)/shard_map/ppermute | solution.py:31
  419.1 7.0 %convolution_convert_fusion.8 = bf16[1024,256]{1,0:T(8,128)(2,1)} fusion(bf16[512,1024]{1,0:T(8,128)(2,1)} %collective-permute-done.26, bf16[512,1024]{1,0:T(8,128)(2,1)} %collective-permute-done.25, bf16[512,1024]{1,0:T(8,128)(2,1)} %collective-permute-done.24, bf16[512,1024]{1,0:T(8,128)(2,1)} %get-tuple-element.274, bf16[2048,256]{1,0:T(8,128)(2,1)S(1)} %copy-done.1, ...), kind=kOutput, calls=%fused_computation.89 | convolution fusion | flops 1093926912 | bytes 5785600 | tf_op jit(solution)/shard_map/dot_general | solution.py:106
  428.8 54.3 %attention_backward.1 = (bf16[2048,256]{1,0:T(8,128)(2,1)}, bf16[2048,256]{1,0:T(8,128)(2,1)}, bf16[2048,256]{1,0:T(8,128)(2,1)}) custom-call(s32[5]{0:T(128)} %copy-done.2, bf16[2048,768]{1,0:T(8,128)(2,1)} %copy-done.3, bf16[2048,768]{1,0:T(8,128)(2,1)} %copy-done.3, bf16[2048,768]{1,0:T(8,128)(2,1)} %copy-done.3, bf16[2048,256]{1,0:T(8,128)(2,1)} %fusion.34.g_ref, ...), custom_call_target="tpu_custom_call" | custom-call | flops 42949672960 | bytes 8388608 | tf_op jit(solution)/shard_map/attention_backward/pallas_call | solution.py:240
  493.5 6.9 %convolution_convert_fusion.7 = bf16[1024,768]{1,0:T(8,128)(2,1)} fusion(bf16[2048,768]{1,0:T(8,128)(2,1)S(1)} %constant_dynamic-update-slice_fusion.8, f32[1024]{0:T(1024)S(1)} %copy-done.60, f32[1024]{0:T(1024)S(1)} %copy-done.39, f32[2048]{0:T(1024)S(1)} %copy-done.52, f32[2048]{0:T(1024)S(1)} %copy-done.45, ...), kind=kOutput, calls=%fused_computation.88 | convolution fusion | flops 3249274880 | bytes 8937472 | tf_op jit(solution)/shard_map/dot_general | solution.py:106
  513.5 8.2 %reduce-scatter.7.cloned.1.call-done = bf16[128,256]{1,0:T(8,128)(2,1)} async-done(((bf16[1024,256]{1,0:T(8,128)(2,1)}), bf16[128,256]{1,0:T(8,128)(2,1)}) %reduce-scatter.7.cloned.1.call-update) | async-done | bytes 65552 | tf_op jit(solution)/shard_map/reduce_scatter | solution.py:405
  537.3 6.8 %all-to-all-done.1 = f32[32,1,448]{2,1,0:T(1,128)S(1)} async-done(((f32[32,1,448]{2,1,0:T(1,128)}), f32[32,1,448]{2,1,0:T(1,128)S(1)}, u32[]{:S(2)}, u32[]{:S(2)}) %all-to-all-start.1) | async-done | bytes 57376 | tf_op jit(solution)/shard_map/all_to_all | solution.py:67
  547.0 43.6 %reduce-scatter.5.cloned.1.call-done = bf16[128,768]{1,0:T(8,128)(2,1)} async-done(((bf16[1024,768]{1,0:T(8,128)(2,1)}), bf16[128,768]{1,0:T(8,128)(2,1)}) %reduce-scatter.5.cloned.1.call-update) | async-done | bytes 196624 | tf_op jit(solution)/shard_map/reduce_scatter | solution.py:405
  (404 shorter events, 183.1 us)
Async XLA Ops:
  7.2 52.2 %all-gather.4.cloned.1.call-start = ((), (), s32[]{:S(2)}) async-start(), calls=%async_computation.7 | async-start | bytes 1769472 | tf_op jit(solution)/shard_map/all_gather | solution.py:317
  7.3 26.4 %collective-permute-start.1 = (bf16[512,1024]{1,0:T(8,128)(2,1)}, bf16[512,1024]{1,0:T(8,128)(2,1)S(1)}, u32[]{:S(2)}, u32[]{:S(2)}) collective-permute-start(bf16[512,1024]{1,0:T(8,128)(2,1)} %param.24), channel_id=1, source_target_pairs={{0,2},{1,3},{2,0},{3,1},{4,6},{5,7},{6,4},{7,5},{8,10},{9,11},{10,... | collective-permute-start | bytes 3145736 | tf_op jit(solution)/shard_map/ppermute | solution.py:31
  12.2 39.3 %collective-permute-start = (bf16[512,1024]{1,0:T(8,128)(2,1)}, bf16[512,1024]{1,0:T(8,128)(2,1)}, u32[]{:S(2)}, u32[]{:S(2)}) collective-permute-start(bf16[512,1024]{1,0:T(8,128)(2,1)} %param.24), channel_id=1, source_target_pairs={{0,1},{1,0},{2,3},{3,2},{4,5},{5,4},{6,7},{7,6},{8,9},{9,8},{10,11... | collective-permute-start | bytes 3145736 | tf_op jit(solution)/shard_map/ppermute | solution.py:31
  42.8 176.6 %all-gather.6.cloned.1.call-start = ((), (), s32[]{:S(2)}) async-start(), calls=%async_computation.8 | async-start | bytes 2359296 | tf_op jit(solution)/shard_map/all_gather | solution.py:321
  100.8 28.0 %collective-permute-start.3 = (f32[2,4,512]{2,1,0:T(4,128)S(1)}, f32[2,4,512]{2,1,0:T(4,128)S(1)}, u32[]{:S(2)}, u32[]{:S(2)}) collective-permute-start(f32[2,4,512]{2,1,0:T(4,128)S(1)} %constant_dynamic-update-slice_fusion), channel_id=1, source_target_pairs={{0,1},{1,0},{2,3},{3,2},{4,5},{5,4},{6,7},{7,6},{8,9},{9,8},{10,11... | collective-permute-start | bytes 49160 | tf_op jit(solution)/shard_map/ppermute | solution.py:31
  141.2 25.5 %collective-permute-start.7 = (bf16[512,1024]{1,0:T(8,128)(2,1)}, bf16[512,1024]{1,0:T(8,128)(2,1)}, u32[]{:S(2)}, u32[]{:S(2)}) collective-permute-start(bf16[512,1024]{1,0:T(8,128)(2,1)} %add_convert_fusion.7), channel_id=1, source_target_pairs={{0,2},{1,3},{2,0},{3,1},{4,6},{5,7},{6,4},{7,5},{8,10},{9,11},{10,... | collective-permute-start | bytes 3145736 | tf_op jit(solution)/shard_map/ppermute | solution.py:31
  143.6 107.9 %all-gather.8.cloned.1.call-start = ((), (), s32[]{:S(2)}) async-start(), calls=%async_computation.9 | async-start | bytes 2359296 | tf_op jit(solution)/shard_map/all_gather | solution.py:322
  171.9 26.4 %collective-permute-start.9 = (bf16[512,1024]{1,0:T(8,128)(2,1)}, bf16[512,1024]{1,0:T(8,128)(2,1)}, u32[]{:S(2)}, u32[]{:S(2)}) collective-permute-start(bf16[512,1024]{1,0:T(8,128)(2,1)} %add_convert_fusion.6), channel_id=1, source_target_pairs={{0,2},{1,3},{2,0},{3,1},{4,6},{5,7},{6,4},{7,5},{8,10},{9,11},{10,... | collective-permute-start | bytes 3145736 | tf_op jit(solution)/shard_map/ppermute | solution.py:31
  173.6 45.8 %collective-permute-start.17 = (bf16[512,1024]{1,0:T(8,128)(2,1)S(1)}, bf16[512,1024]{1,0:T(8,128)(2,1)}, u32[]{:S(2)}, u32[]{:S(2)}) collective-permute-start(bf16[512,1024]{1,0:T(8,128)(2,1)S(1)} %copy-done.24), channel_id=1, source_target_pairs={{0,2},{1,3},{2,0},{3,1},{4,6},{5,7},{6,4},{7,5},{8,10},{9,11},{10,... | collective-permute-start | bytes 3145736 | tf_op jit(solution)/shard_map/ppermute | solution.py:31
  174.0 45.4 %collective-permute-start.8 = (bf16[512,1024]{1,0:T(8,128)(2,1)}, bf16[512,1024]{1,0:T(8,128)(2,1)}, u32[]{:S(2)}, u32[]{:S(2)}) collective-permute-start(bf16[512,1024]{1,0:T(8,128)(2,1)} %add_convert_fusion.6), channel_id=1, source_target_pairs={{0,1},{1,0},{2,3},{3,2},{4,5},{5,4},{6,7},{7,6},{8,9},{9,8},{10,11... | collective-permute-start | bytes 3145736 | tf_op jit(solution)/shard_map/ppermute | solution.py:31
  198.4 53.2 %collective-permute-start.16 = (bf16[512,1024]{1,0:T(8,128)(2,1)S(1)}, bf16[512,1024]{1,0:T(8,128)(2,1)}, u32[]{:S(2)}, u32[]{:S(2)}) collective-permute-start(bf16[512,1024]{1,0:T(8,128)(2,1)S(1)} %copy-done.24), channel_id=1, source_target_pairs={{0,1},{1,0},{2,3},{3,2},{4,5},{5,4},{6,7},{7,6},{8,9},{9,8},{10,11... | collective-permute-start | bytes 3145736 | tf_op jit(solution)/shard_map/ppermute | solution.py:31
  199.6 305.8 %reduce-scatter.11.cloned.1.call-start = ((), (), s32[]{:S(2)}) async-start(), calls=%async_computation.13 | async-start | bytes 2359296 | tf_op jit(solution)/shard_map/reduce_scatter | solution.py:405
  219.4 32.1 %collective-permute-start.18 = (bf16[512,1024]{1,0:T(8,128)(2,1)}, bf16[512,1024]{1,0:T(8,128)(2,1)}, u32[]{:S(2)}, u32[]{:S(2)}) collective-permute-start(bf16[512,1024]{1,0:T(8,128)(2,1)} %collective-permute-done.17), channel_id=1, source_target_pairs={{0,1},{1,0},{2,3},{3,2},{4,5},{5,4},{6,7},{7,6},{8,9},{9,8},{10,11... | collective-permute-start | bytes 3145736 | tf_op jit(solution)/shard_map/ppermute | solution.py:31
  249.8 21.5 %collective-permute-start.12 = (f32[2,4,512]{2,1,0:T(4,128)S(1)}, f32[2,4,512]{2,1,0:T(4,128)S(1)}, u32[]{:S(2)}, u32[]{:S(2)}) collective-permute-start(f32[2,4,512]{2,1,0:T(4,128)S(1)} %maximum_add_fusion.2), channel_id=1, source_target_pairs={{0,2},{1,3},{2,0},{3,1},{4,6},{5,7},{6,4},{7,5},{8,10},{9,11},{10,... | collective-permute-start | bytes 49160 | tf_op jit(solution)/shard_map/ppermute | solution.py:31
  322.9 188.1 %reduce-scatter.9.cloned.1.call-start = ((), (), s32[]{:S(2)}) async-start(), calls=%async_computation.12 | async-start | bytes 2359296 | tf_op jit(solution)/shard_map/reduce_scatter | solution.py:405
  325.1 26.1 %collective-permute-start.23 = (bf16[512,1024]{1,0:T(8,128)(2,1)S(1)}, bf16[512,1024]{1,0:T(8,128)(2,1)S(1)}, u32[]{:S(2)}, u32[]{:S(2)}) collective-permute-start(bf16[512,1024]{1,0:T(8,128)(2,1)S(1)} %add_convert_fusion.3), channel_id=1, source_target_pairs={{0,2},{1,3},{2,0},{3,1},{4,6},{5,7},{6,4},{7,5},{8,10},{9,11},{10,... | collective-permute-start | bytes 3145736 | tf_op jit(solution)/shard_map/ppermute | solution.py:31
  325.6 27.4 %collective-permute-start.13 = (bf16[512,1024]{1,0:T(8,128)(2,1)}, bf16[512,1024]{1,0:T(8,128)(2,1)S(1)}, u32[]{:S(2)}, u32[]{:S(2)}) collective-permute-start(bf16[512,1024]{1,0:T(8,128)(2,1)} %get-tuple-element.286), channel_id=1, source_target_pairs={{0,1},{1,0},{2,3},{3,2},{4,5},{5,4},{6,7},{7,6},{8,9},{9,8},{10,11... | collective-permute-start | bytes 3145736 | tf_op jit(solution)/shard_map/ppermute | solution.py:31
  327.7 45.0 %collective-permute-start.15 = (bf16[512,1024]{1,0:T(8,128)(2,1)S(1)}, bf16[512,1024]{1,0:T(8,128)(2,1)S(1)}, u32[]{:S(2)}, u32[]{:S(2)}) collective-permute-start(bf16[512,1024]{1,0:T(8,128)(2,1)S(1)} %add_convert_fusion.5), channel_id=1, source_target_pairs={{0,2},{1,3},{2,0},{3,1},{4,6},{5,7},{6,4},{7,5},{8,10},{9,11},{10,... | collective-permute-start | bytes 3145736 | tf_op jit(solution)/shard_map/ppermute | solution.py:31
  377.6 24.7 %collective-permute-start.25 = (bf16[512,1024]{1,0:T(8,128)(2,1)}, bf16[512,1024]{1,0:T(8,128)(2,1)}, u32[]{:S(2)}, u32[]{:S(2)}) collective-permute-start(bf16[512,1024]{1,0:T(8,128)(2,1)} %get-tuple-element.274), channel_id=1, source_target_pairs={{0,2},{1,3},{2,0},{3,1},{4,6},{5,7},{6,4},{7,5},{8,10},{9,11},{10,... | collective-permute-start | bytes 3145736 | tf_op jit(solution)/shard_map/ppermute | solution.py:31
  386.4 135.3 %reduce-scatter.7.cloned.1.call-start = ((), (), s32[]{:S(2)}) async-start(), calls=%async_computation.11 | async-start | bytes 589824 | tf_op jit(solution)/shard_map/reduce_scatter | solution.py:405
  386.5 24.8 %collective-permute-start.24 = (bf16[512,1024]{1,0:T(8,128)(2,1)}, bf16[512,1024]{1,0:T(8,128)(2,1)}, u32[]{:S(2)}, u32[]{:S(2)}) collective-permute-start(bf16[512,1024]{1,0:T(8,128)(2,1)} %get-tuple-element.274), channel_id=1, source_target_pairs={{0,1},{1,0},{2,3},{3,2},{4,5},{5,4},{6,7},{7,6},{8,9},{9,8},{10,11... | collective-permute-start | bytes 3145736 | tf_op jit(solution)/shard_map/ppermute | solution.py:31
  426.1 164.5 %reduce-scatter.5.cloned.1.call-start = ((), (), s32[]{:S(2)}) async-start(), calls=%async_computation.10 | async-start | bytes 1769472 | tf_op jit(solution)/shard_map/reduce_scatter | solution.py:405
  500.7 24.1 %collective-permute-start.29 = (bf16[512,1024]{1,0:T(8,128)(2,1)}, bf16[512,1024]{1,0:T(8,128)(2,1)}, u32[]{:S(2)}, u32[]{:S(2)}) collective-permute-start(bf16[512,1024]{1,0:T(8,128)(2,1)} %get-tuple-element.282), channel_id=1, source_target_pairs={{0,1},{1,0},{2,3},{3,2},{4,5},{5,4},{6,7},{7,6},{8,9},{9,8},{10,11... | collective-permute-start | bytes 3145736 | tf_op jit(solution)/shard_map/ppermute | solution.py:31
  503.5 25.8 %collective-permute-start.31 = (bf16[512,1024]{1,0:T(8,128)(2,1)}, bf16[512,1024]{1,0:T(8,128)(2,1)}, u32[]{:S(2)}, u32[]{:S(2)}) collective-permute-start(bf16[512,1024]{1,0:T(8,128)(2,1)} %add_convert_fusion.2), channel_id=1, source_target_pairs={{0,2},{1,3},{2,0},{3,1},{4,6},{5,7},{6,4},{7,5},{8,10},{9,11},{10,... | collective-permute-start | bytes 3145736 | tf_op jit(solution)/shard_map/ppermute | solution.py:31
  (95 other events, 1336.7 us)
Sparse Core Ops, SparseCore 0:
  12.4 46.9 all-gather.3
  143.7 45.4 all-gather.5
  199.7 48.2 all-gather.7
  323.1 63.8 reduce-scatter.10
  390.3 66.6 reduce-scatter.8
  460.8 60.8 reduce-scatter.6
  525.5 65.0 reduce-scatter.4

commit v2 on v1

v2 whole, which is shorter than its diff:
```python
from functools import partial

import jax
import jax.numpy as jnp
from jax import lax
from jax.experimental import pallas as pl
from jax.experimental.pallas import tpu as pltpu
from jax.sharding import PartitionSpec as P

D = 1024
HD = 64
FF = 4096
ADAM_STEP = 10

NORM_EPS = 1e-05
MASKED = -1e30
RATE = 0.02
BETA_ONE = 0.9
BETA_TWO = 0.95
ADAM_EPS = 1e-08
DECAY = 0.1
MAX_NORM = 1.0

BF = jnp.bfloat16
F32 = jnp.float32
ALL = ("dp", "mp")


def swap(value, bit):
    count = lax.axis_size("mp")
    return lax.ppermute(value, "mp", [(i, i ^ bit) for i in range(count)])


def mp_bits():
    count = lax.axis_size("mp")
    return [1 << b for b in range(count.bit_length() - 1)]


def after(values, others):
    values, _ = lax.optimization_barrier((tuple(values), tuple(others)))
    return list(values)


def gather_near(own):
    even = {0: own}
    for bit in reversed(mp_bits()[1:]):
        for r in list(even):
            even[r | bit] = swap(even[r], bit)
    return [own, swap(own, 1)], [even[r] for r in range(2, 2 * len(even), 2)]


def gather_far(even):
    return [block for value in even for block in (value, swap(value, 1))]


def sum_chip(terms):
    return [
        terms[2 * i].astype(F32) + swap(terms[2 * i + 1], 1).astype(F32)
        for i in range(len(terms) // 2)
    ]


def sum_far(sums):
    even = {2 * i + 2: value for i, value in enumerate(sums)}
    arrived = []
    for bit in mp_bits()[1:]:
        for r in [r for r in even if r & bit]:
            received = swap(even.pop(r).astype(BF), bit)
            if r == bit:
                arrived.append(received)
            else:
                even[r ^ bit] = even[r ^ bit].astype(F32) + received.astype(F32)
    return arrived


def sum_near(terms, arrived):
    total = terms[0].astype(F32) + swap(terms[1], 1).astype(F32)
    for value in arrived:
        total = total + value.astype(F32)
    return total


def token_totals(values):
    count = lax.axis_size("mp")
    height = values.shape[1] // count
    for bit in mp_bits():
        received = swap(values, bit)
        parts = [received[:, (r ^ bit) * height : ((r ^ bit) + 1) * height] for r in range(count)]
        values = values + jnp.concatenate(parts, axis=1)
    return values


def exchange_all(value):
    return lax.all_to_all(value, ALL, 0, 0, tiled=True)


def dp_swap(value, bits):
    count = lax.axis_size("dp")
    return lax.ppermute(value, "dp", [(i, i ^ bits) for i in range(count)])


def place_kernel(table_ref, *refs):
    blocks, outs = refs[:8], refs[8:]
    rows = blocks[0].shape[0]
    for r, ref in enumerate(blocks):
        start = pl.multiple_of((table_ref[0] ^ r) * rows, rows)
        first = 0
        for out in outs:
            out[pl.ds(start, rows), :] = ref[:, first : first + out.shape[1]]
            first += out.shape[1]


def smem():
    return pl.BlockSpec(memory_space=pltpu.SMEM)


def vmem():
    return pl.BlockSpec(memory_space=pltpu.VMEM)


def gather_groups(shard):
    if lax.axis_size("dp") != 8:
        return [lax.all_gather(shard, "dp", axis=0, tiled=True)]
    return [shard] + [dp_swap(shard, bits) for bits in (2, 4, 6)]


def cross_groups(even, others):
    if len(even) == 1:
        return []
    first = dp_swap(even[0], 1)
    odd = [first, dp_swap(first, 2)]
    return odd + [dp_swap(value, 1) for value in after(even[2:], odd + even[1:2] + others)]


def place_groups(even, odd, widths):
    if len(even) == 1:
        return list(jnp.split(even[0], [sum(widths[: k + 1]) for k in range(len(widths) - 1)], axis=1))
    blocks = [block for both in zip(even, odd) for block in both]
    place = lax.axis_index("dp").astype(jnp.int32)[None]
    rows = even[0].shape[0]
    return pl.pallas_call(
        place_kernel,
        in_specs=[smem()] + [vmem()] * 8,
        out_specs=[vmem()] * len(widths),
        out_shape=[jax.ShapeDtypeStruct((8 * rows, width), even[0].dtype) for width in widths],
        cost_estimate=about(2),
        name="place_rows",
    )(place, *blocks)


def exchange_groups(value):
    return lax.all_to_all(value, "dp", 0, 0, tiled=True)


HINT = 4.0


def about(microseconds, hint=HINT):
    return pl.CostEstimate(
        flops=int(microseconds * hint * 1.15e9),
        transcendentals=0,
        bytes_accessed=int(microseconds * hint * 1e5),
    )


def dot(left, right, left_dim, right_dim):
    return lax.dot_general(
        left, right, (((left_dim,), (right_dim,)), ((), ())), preferred_element_type=F32
    )


def norm_rows(value):
    mean = jnp.mean(value, axis=-1, keepdims=True)
    centered = value - mean
    variance = jnp.mean(centered * centered, axis=-1, keepdims=True)
    factor = lax.rsqrt(variance + NORM_EPS)
    return centered * factor, factor


def norm_back(grad, normed, factor, gain):
    weighted = grad * gain
    result = factor * (
        weighted
        - jnp.mean(weighted, axis=-1, keepdims=True)
        - normed * jnp.mean(weighted * normed, axis=-1, keepdims=True)
    )
    return result, jnp.sum(grad * normed, axis=0), jnp.sum(grad, axis=0)


def as_rows(columns, count):
    rows = columns[0].shape[0]
    lane = lax.broadcasted_iota(jnp.int32, (rows, 128), 1)
    spread = jnp.zeros((rows, 128), F32)
    for i, column in enumerate(columns):
        spread = jnp.where(lane == i, column, spread)
    return jnp.transpose(spread)[:count]


def as_columns(values):
    count, rows = values.shape
    padded = jnp.concatenate([values, jnp.zeros((128 - count, rows), F32)], axis=0)
    turned = jnp.transpose(padded)
    return [turned[:, i : i + 1] for i in range(count)]


def fold(value):
    return jnp.sum(value.reshape(value.shape[0] // 8, 8, value.shape[1]), axis=0)


def moments(first, second, width):
    mean = first / width
    variance = second / width - mean * mean
    return mean, lax.rsqrt(variance + NORM_EPS)


class Rows:
    def __init__(self, blocks, height, step):
        self.blocks = blocks
        self.per = height // step
        self.step = step
        self.height = height
        self.grid = (len(blocks) * self.per,)

    def at(self, i):
        return i + self.blocks[0] * self.per

    def whole(self, width, column=0):
        return pl.BlockSpec((self.step, width), lambda i, *t: (self.at(i), column))

    def stats(self, count):
        return pl.BlockSpec((count, self.step), lambda i, *t: (0, self.at(i)))

    def pieces(self, width):
        per = self.per
        return [
            pl.BlockSpec(
                (self.step, width), lambda i, *t, first=k * per: (jnp.clip(i - first, 0, per - 1), 0)
            )
            for k in range(len(self.blocks))
        ]

    def load(self, refs, into):
        for k, ref in enumerate(refs):

            @pl.when(pl.program_id(0) // self.per == k)
            def _():
                into[...] = ref[...]

    def store(self, refs, value):
        for k, ref in enumerate(refs):

            @pl.when(pl.program_id(0) // self.per == k)
            def _():
                ref[...] = value


def fixed(shape, *index):
    index = index or (0,) * len(shape)
    return pl.BlockSpec(shape, lambda i, *t: index)


ANY = pl.BlockSpec(memory_space=pl.ANY)


def call(kernel, part, name, ins, in_specs, outs, out_specs, scratch=(), kept=None, table=None, cost=8, pieces=False):
    ins, in_specs = list(ins), list(in_specs)
    aliases = {}
    tables = [] if table is None else [table]
    if kept is not None:
        for k, value in enumerate(kept):
            aliases[len(tables) + len(ins)] = k
            ins.append(value)
            in_specs.append(ANY)
    dropped = 0 if kept is None else len(kept)
    used = len(tables) + len(ins) - dropped

    def body(*refs):
        kernel(*refs[:used], *refs[used + dropped :])

    hbm = len(outs) - len(part.blocks) if pieces else len(outs)
    return pl.pallas_call(
        body,
        grid_spec=pltpu.PrefetchScalarGridSpec(
            num_scalar_prefetch=len(tables),
            grid=part.grid,
            in_specs=in_specs,
            out_specs=list(out_specs),
            scratch_shapes=list(scratch),
        ),
        out_shape=[jax.ShapeDtypeStruct(*out) for out in outs[:hbm]]
        + [pltpu.HBM(*out) for out in outs[hbm:]],
        input_output_aliases=aliases,
        cost_estimate=about(cost * len(part.blocks) / 4),
        compiler_params=pltpu.CompilerParams(vmem_limit_bytes=50 << 20),
        name=name,
    )(*tables, *ins)


def project(part, blocks, work_in, outer):
    count, length = len(blocks), len(blocks) * part.height
    width = work_in.shape[1]

    def kernel(*refs):
        work_ref, gain_ref, normed_ref, out_ref, row = refs[count:]
        part.load(refs[:count], row)
        normed = norm_rows(row[...].astype(F32))[0]
        normed_ref[...] = normed.astype(BF)
        normed = (normed * gain_ref[0:1] + gain_ref[1:2]).astype(BF)
        out_ref[...] = dot(normed, work_ref[...], 1, 0).astype(BF)

    return call(
        kernel,
        part,
        "project",
        [*blocks, work_in, outer],
        [*part.pieces(D), fixed(work_in.shape), fixed(outer.shape)],
        [((length, D), BF), ((length, width), BF)],
        [part.whole(D), part.whole(width)],
        [pltpu.VMEM((part.step, D), BF)],
    )


def columns_of(table_ref, index, r, width):
    return pl.ds(pl.multiple_of((table_ref[index] ^ r) * width, width), width)


def head_norm(att_refs):
    parts = [ref[...].astype(F32) for ref in att_refs]
    mean = sum(jnp.sum(part, axis=1, keepdims=True) for part in parts) / D
    parts = [part - mean for part in parts]
    variance = sum(jnp.sum(part * part, axis=1, keepdims=True) for part in parts) / D
    factor = lax.rsqrt(variance + NORM_EPS)
    return [part * factor for part in parts], factor


def own_call(kernel, name, table, ins, in_specs, outs, out_specs, height, cost, scratch=()):
    return pl.pallas_call(
        kernel,
        grid_spec=pltpu.PrefetchScalarGridSpec(
            num_scalar_prefetch=1,
            grid=(height // OWN_STEP,),
            in_specs=in_specs,
            out_specs=out_specs,
            scratch_shapes=list(scratch),
        ),
        out_shape=[pltpu.HBM(*out) if out[1] == BF else jax.ShapeDtypeStruct(*out) for out in outs],
        cost_estimate=about(cost),
        compiler_params=pltpu.CompilerParams(vmem_limit_bytes=50 << 20),
        name=name,
    )(table, *ins)


OWN_STEP = 256


def own(width):
    return pl.BlockSpec((OWN_STEP, width), lambda i, t: (i, 0))


def mix_rows(table, sequences, blocks, mixes, gains, tokens, outer):
    count, (height, width) = len(blocks), blocks[0].shape

    def kernel(table_ref, *refs):
        att_refs, mix_refs = refs[:count], refs[count : 2 * count]
        gain_ref, token_ref, outer_ref, middle_ref, mid_ref, in_ref = refs[2 * count :]
        middle = token_ref[...].astype(F32)
        for r, normed in enumerate(head_norm(att_refs)[0]):
            columns = columns_of(table_ref, sequences + 1, r, width)
            low = (normed * gain_ref[0:1, columns] + gain_ref[1:2, columns]).astype(BF)
            in_ref[:, r * width : (r + 1) * width] = low
            middle = middle + dot(low, mix_refs[r][...], 1, 1)
        middle_ref[...] = middle
        mid_ref[...] = (norm_rows(middle)[0] * outer_ref[2:3] + outer_ref[3:4]).astype(BF)

    return own_call(
        kernel,
        "mix_rows",
        table,
        [*blocks, *mixes, gains, tokens, outer],
        [own(width)] * count + [fixed((D, width))] * count + [fixed((2, D)), own(D), fixed((4, D))],
        [((height, D), F32), ((height, D), BF), ((height, D), BF)],
        [own(D)] * 3,
        height,
        6,
    )


def mix_rows_back(table, sequences, terms, middle, cotangent, outer, blocks, mixes, gains):
    count, (height, width) = len(blocks), blocks[0].shape

    def kernel(table_ref, *refs):
        term_refs, refs = refs[: len(terms)], refs[len(terms) :]
        middle_ref, back_ref, outer_ref, gain_ref = refs[:4]
        att_refs, mix_refs = refs[4 : 4 + count], refs[4 + count : 4 + 2 * count]
        out_ref, low_ref, outer_sum, head_sum, *outs = refs[4 + 2 * count :]

        @pl.when(pl.program_id(0) == 0)
        def _():
            outer_sum[...] = jnp.zeros_like(outer_sum)
            head_sum[...] = jnp.zeros_like(head_sum)

        grad = sum(ref[...].astype(F32) for ref in term_refs)
        normed, factor = norm_rows(middle_ref[...])
        weighted = grad * outer_ref[2:3]
        first = jnp.mean(weighted, axis=1, keepdims=True)
        second = jnp.mean(weighted * normed, axis=1, keepdims=True)
        outer_sum[0:8] += fold(grad * normed)
        outer_sum[8:16] += fold(grad)
        rows = pl.program_id(0) * OWN_STEP + lax.broadcasted_iota(jnp.int32, (OWN_STEP, 1), 0)
        live = segments_at(rows, table_ref, sequences) < sequences
        back = jnp.where(live, back_ref[...].astype(F32), 0.0)
        back = back + factor * (weighted - first - normed * second)
        out_ref[...] = back
        low = back.astype(BF)
        low_ref[...] = low
        normed, factor = head_norm(att_refs)
        weighted = []
        first, second = 0.0, 0.0
        for r in range(count):
            columns = columns_of(table_ref, sequences + 1, r, width)
            grad = dot(low, mix_refs[r][...], 1, 0)
            head_sum[0:8, columns] += fold(grad * normed[r])
            head_sum[8:16, columns] += fold(grad)
            weighted.append(grad * gain_ref[0:1, columns])
            first = first + jnp.sum(weighted[r], axis=1, keepdims=True)
            second = second + jnp.sum(weighted[r] * normed[r], axis=1, keepdims=True)
        for r in range(count):
            value = factor * (weighted[r] - first / D - normed[r] * (second / D))
            outs[r][...] = value.astype(BF)

    return own_call(
        kernel,
        "mix_rows_back",
        table,
        [*terms, middle, cotangent, outer, gains, *blocks, *mixes],
        [own(D)] * (len(terms) + 2)
        + [fixed((4, D)), fixed((2, D))]
        + [own(width)] * count
        + [fixed((D, width))] * count,
        [((height, D), F32), ((height, D), BF), ((16, D), F32), ((16, D), F32)]
        + [((height, width), BF)] * count,
        [own(D), own(D), fixed((16, D)), fixed((16, D))] + [own(width)] * count,
        height,
        8,
    )


def mix_grads(low, mixed_in, count):
    height, width = low.shape[0], mixed_in.shape[1] // count
    block = 256

    def kernel(low_ref, in_ref, *outs):
        for r in range(count):
            outs[r][...] = dot(low_ref[...], in_ref[:, r * width : (r + 1) * width], 0, 0).astype(BF)

    return pl.pallas_call(
        kernel,
        grid=(D // block,),
        in_specs=[
            pl.BlockSpec((height, block), lambda i: (0, i)),
            pl.BlockSpec((height, D), lambda i: (0, 0)),
        ],
        out_specs=[pl.BlockSpec((block, width), lambda i: (i, 0))] * count,
        out_shape=[pltpu.HBM((D, width), BF)] * count,
        cost_estimate=about(4),
        compiler_params=pltpu.CompilerParams(vmem_limit_bytes=50 << 20),
        name="mix_grads",
    )(low, mixed_in)


def feed_back(part, blocks, table, sequences, weights):
    count, length = len(blocks), len(blocks) * part.height
    units = weights.shape[1] // 2

    def kernel(table_ref, *refs):
        work_ref, back_ref, out_ref, row = refs[count:]
        part.load(refs[:count], row)
        rows = pl.program_id(0) * part.step + lax.broadcasted_iota(jnp.int32, (part.step, 1), 0)
        live = segments_at(rows, table_ref, sequences) < sequences
        back = jnp.where(live, row[...].astype(F32), 0.0).astype(BF)
        back_ref[...] = back
        out_ref[...] = dot(back, work_ref[...], 1, 0).astype(BF)

    return call(
        kernel,
        part,
        "feed_back",
        [*blocks, weights],
        [*part.pieces(D), fixed((D, units), 0, 1)],
        [((length, D), BF), ((length, units), BF)],
        [part.whole(D), part.whole(units)],
        [pltpu.VMEM((part.step, D), BF)],
        table=table,
    )


def widen(part, blocks, weights, unit_in, gains, kept=None):
    count, (length, units) = len(blocks), unit_in.shape

    def kernel(*refs):
        work_ref, in_ref, gain_ref, mid_ref, act_ref, slope_ref, total_ref, row = refs[count:]
        part.load(refs[:count], row)
        mid_ref[...] = row[...]
        wide = dot(row[...], work_ref[...], 1, 0)
        share = 0.5 + 0.5 * lax.erf(wide * 0.7071067811865476)
        act = wide * share
        act_ref[...] = act
        slope_ref[...] = (share + wide * (0.3989422804014327 * jnp.exp(-0.5 * wide * wide))).astype(BF)
        weighted = in_ref[...].astype(F32) * gain_ref[0:1]
        values = (act, act * act, weighted, weighted * act)
        total_ref[...] = as_rows([jnp.sum(v, axis=1, keepdims=True) for v in values], 4)

    return call(
        kernel,
        part,
        "widen",
        [*blocks, weights, unit_in, gains],
        [*part.pieces(D), fixed((D, units), 0, 0), part.whole(units), fixed(gains.shape)],
        [((length, D), BF), ((length, units), F32), ((length, units), BF), ((4, length), F32)],
        [part.whole(D), part.whole(units), part.whole(units), part.stats(4)],
        [pltpu.VMEM((part.step, D), BF)],
        kept=kept,
    )


def narrow_back(part, act, slope, unit_in, totals, gains, weights, kept=None):
    length, units = act.shape

    def kernel(act_ref, slope_ref, in_ref, total_ref, gain_ref, work_ref, low_ref, wide_ref, sum_ref, *outs):
        first, second, third, fourth = as_columns(total_ref[...])
        mean, factor = moments(first, second, FF)
        normed = (act_ref[...] - mean) * factor
        low_ref[...] = (normed * gain_ref[0:1] + gain_ref[1:2]).astype(BF)
        grad = in_ref[...].astype(F32)
        inner = factor * (fourth - mean * third)
        back = factor * (grad * gain_ref[0:1] - third / FF - normed * (inner / FF))
        wide = (back * slope_ref[...].astype(F32)).astype(BF)
        wide_ref[...] = wide

        @pl.when(pl.program_id(0) == 0)
        def _():
            sum_ref[...] = jnp.zeros_like(sum_ref)

        sum_ref[0:8] += fold(grad * normed)
        sum_ref[8:16] += fold(grad)
        part.store(outs, dot(wide, work_ref[...], 1, 1).astype(BF))

    return call(
        kernel,
        part,
        "narrow_back",
        [act, slope, unit_in, totals, gains, weights],
        [part.whole(units)] * 3 + [part.stats(4), fixed(gains.shape), fixed((D, units), 0, 0)],
        [((length, units), BF)] * 2
        + [((16, units), F32)]
        + [((part.height, D), BF)] * len(part.blocks),
        [part.whole(units)] * 2 + [fixed((16, units))] + part.pieces(D),
        kept=kept,
        pieces=True,
    )


def weight_grad(left, right):
    length, block = left.shape[0], 256

    def kernel(left_ref, right_ref, out_ref):
        out_ref[...] = dot(left_ref[...], right_ref[...], 0, 0).astype(BF)

    return pl.pallas_call(
        kernel,
        grid=(left.shape[1] // block,),
        in_specs=[
            pl.BlockSpec((length, block), lambda i: (0, i)),
            pl.BlockSpec(right.shape, lambda i: (0, 0)),
        ],
        out_specs=pl.BlockSpec((block, right.shape[1]), lambda i: (i, 0)),
        out_shape=jax.ShapeDtypeStruct((left.shape[1], right.shape[1]), BF),
        cost_estimate=about(8),
        compiler_params=pltpu.CompilerParams(vmem_limit_bytes=50 << 20),
        name="weight_grad",
    )(left, right)


def feed_rows(part, low, weights):
    units = low.shape[1]

    def kernel(low_ref, work_ref, *outs):
        part.store(outs, dot(low_ref[...], work_ref[...], 1, 1).astype(BF))

    return call(
        kernel,
        part,
        "feed_rows",
        [low, weights],
        [part.whole(units), fixed((D, units), 0, 1)],
        [((part.height, D), BF)] * len(part.blocks),
        part.pieces(D),
        pieces=True,
    )


EXTRA = 16


def attend_rows(normed_all, back, extra=()):
    length, width = back.shape
    groups = lax.axis_size("dp")
    shard = D // groups
    more = extra[0].shape[1] if extra else 0

    def kernel(normed_ref, back_ref, *refs):
        out_ref, total_ref = refs[-2:]

        @pl.when(pl.program_id(0) == 0)
        def _():
            value = jnp.sum(fold(back_ref[...].astype(F32)), axis=0, keepdims=True)
            row = lax.broadcasted_iota(jnp.int32, (EXTRA, width), 0)
            total = jnp.zeros((EXTRA, width), F32)
            for k in range(3):
                piece = value.astype(BF).astype(F32)
                total = jnp.where(row == k, piece, total)
                value = value - piece
            total_ref[...] = total.astype(BF)

        start = pl.multiple_of(pl.program_id(0) * shard, shard)
        if shard % 128 == 0:
            normed = normed_ref[:, pl.ds(start, shard)]
        else:
            normed = normed_ref[...]
        out_ref[0, :shard, :width] = dot(normed, back_ref[...], 0, 0).astype(BF)
        out_ref[0, shard:, :width] = total_ref[...]
        if extra:
            value = sum(ref[...].astype(F32) for ref in refs[:-2])
            out_ref[0, :shard, width:] = value.astype(BF)
            out_ref[0, shard:, width:] = jnp.zeros((EXTRA, more), BF)

    if shard % 128 != 0:
        return attend_rows_narrow(normed_all, back, extra)
    return pl.pallas_call(
        kernel,
        grid=(groups,),
        in_specs=[
            pl.BlockSpec((length, D), lambda i: (0, 0)),
            pl.BlockSpec((length, width), lambda i: (0, 0)),
        ]
        + [pl.BlockSpec((shard, more), lambda i: (i, 0))] * len(extra),
        out_specs=pl.BlockSpec((1, shard + EXTRA, width + more), lambda i: (i, 0, 0)),
        out_shape=jax.ShapeDtypeStruct((groups, shard + EXTRA, width + more), BF),
        scratch_shapes=[pltpu.VMEM((EXTRA, width), BF)],
        cost_estimate=about(5),
        compiler_params=pltpu.CompilerParams(vmem_limit_bytes=50 << 20),
        name="attend_rows",
    )(normed_all, back, *extra)


def attend_rows_narrow(normed_all, back, extra):
    groups = lax.axis_size("dp")
    grads = dot(normed_all, back, 0, 0)
    total = jnp.sum(back.astype(F32), axis=0)
    addends = []
    for _ in range(3):
        addends.append(total.astype(BF))
        total = total - addends[-1].astype(F32)
    below = jnp.concatenate([jnp.stack(addends), jnp.zeros((EXTRA - 3, back.shape[1]), BF)], axis=0)
    if extra:
        grads = jnp.concatenate([grads, sum(value.astype(F32) for value in extra)], axis=1)
        below = jnp.concatenate([below, jnp.zeros((EXTRA, extra[0].shape[1]), BF)], axis=1)
    grads = grads.astype(BF).reshape(groups, D // groups, -1)
    below = jnp.broadcast_to(below[None], (groups,) + below.shape)
    return jnp.concatenate([grads, below], axis=1)


def attend_sums(piece, work, gains, width):
    groups, rows, columns = piece.shape
    shard = rows - EXTRA

    def kernel(piece_ref, work_ref, gain_ref, grad_ref, *outs):
        total = piece_ref[0].astype(F32)
        for k in range(1, groups):
            total = total + piece_ref[k].astype(F32)
        grad = total[:shard, :width]
        below = jnp.sum(total[shard:, :width], axis=0, keepdims=True)
        gain, bias = gain_ref[:, 0:1], gain_ref[:, 1:2]
        work = work_ref[...].astype(F32)
        grad_ref[...] = gain * grad + bias * below
        for k, value in enumerate((grad * work, below * work)):
            outs[0][:, k : k + 1] = jnp.sum(value, axis=1, keepdims=True)
        if columns > width:
            outs[1][...] = total[:shard, width:]

    outs = [((shard, width), F32), ((shard, 2), F32)]
    if columns > width:
        outs.append(((shard, columns - width), F32))
    return pl.pallas_call(
        kernel,
        in_specs=[vmem()] * 3,
        out_specs=[vmem()] * len(outs),
        out_shape=[jax.ShapeDtypeStruct(shape, kind) for shape, kind in outs],
        cost_estimate=about(2),
        compiler_params=pltpu.CompilerParams(vmem_limit_bytes=50 << 20),
        name="attend_sums",
    )(piece, work, gains)


def input_back(part, grads, work_in):
    width = grads[0].shape[1]

    def kernel(*refs):
        work_ref, outs = refs[len(grads)], refs[len(grads) + 1 :]
        term = dot(refs[0][...], work_ref[:, :width], 1, 1)
        for k in range(1, len(grads)):
            term = term + dot(refs[k][...], work_ref[:, k * width : (k + 1) * width], 1, 1)
        part.store(outs, term.astype(BF))

    return call(
        kernel,
        part,
        "input_back",
        [*grads, work_in],
        [part.whole(width)] * len(grads) + [fixed((D, len(grads) * width))],
        [((part.height, D), BF)] * len(part.blocks),
        part.pieces(D),
        pieces=True,
    )


def segments_at(rows, table_ref, count):
    slots = rows ^ table_ref[count]
    end = jnp.int32(0)
    segment = jnp.zeros(rows.shape, jnp.int32)
    for i in range(count):
        end = end + table_ref[i]
        segment = segment + (slots >= end).astype(jnp.int32)
    return segment


LANES = 128
PAIR = LANES // HD


def attention_forward(part, projected, table):
    length, width = projected.shape[0], projected.shape[1] // 3
    pairs = width // LANES
    block = part.height
    count = table.shape[0] - 2
    blocks = len(part.blocks)

    def kernel(table_ref, *refs):
        outs, log_ref, low = refs[3 * pairs : -2], refs[-2], refs[-1]
        start = pl.program_id(0) * block
        rows = start + lax.broadcasted_iota(jnp.int32, (block, 1), 0)
        columns = lax.broadcasted_iota(jnp.int32, (1, length), 1)
        allowed = segments_at(rows, table_ref, count) == segments_at(columns, table_ref, count)
        lane = lax.broadcasted_iota(jnp.int32, (1, LANES), 1) // HD
        for p in range(pairs):
            query = refs[3 * p][...] * BF(HD**-0.5)
            keys = refs[3 * p + 1][...]
            values = refs[3 * p + 2][...]
            out = jnp.zeros((block, LANES), F32)
            logs = []
            for h in range(PAIR):
                one = jnp.where(lane == h, query, jnp.zeros_like(query))
                scores = jnp.where(allowed, dot(one, keys, 1, 1), MASKED)
                highest = jnp.max(scores, axis=1, keepdims=True)
                weights = jnp.exp(scores - highest)
                total = jnp.sum(weights, axis=1, keepdims=True)
                mixed = dot(weights.astype(BF), values, 1, 0)
                out = jnp.where(lane == h, mixed * (1.0 / total), out)
                logs.append(highest + jnp.log(total))
            low[:, p * LANES : (p + 1) * LANES] = out.astype(BF)
            log_ref[8 * p : 8 * p + 8, :] = as_rows(logs, 8)
        part.store(outs, low[...])

    specs = []
    for p in range(pairs):
        specs.append(pl.BlockSpec((block, LANES), lambda i, t, p=p: (i, 3 * p)))
        specs.append(fixed((length, LANES), 0, 3 * p + 1))
        specs.append(fixed((length, LANES), 0, 3 * p + 2))
    *outs, logs = pl.pallas_call(
        kernel,
        grid_spec=pltpu.PrefetchScalarGridSpec(
            num_scalar_prefetch=1,
            grid=(blocks,),
            in_specs=specs,
            out_specs=part.pieces(width) + [pl.BlockSpec((8 * pairs, block), lambda i, t: (0, i))],
            scratch_shapes=[pltpu.VMEM((block, width), BF)],
        ),
        out_shape=[jax.ShapeDtypeStruct((block, width), BF)] * blocks
        + [jax.ShapeDtypeStruct((8 * pairs, length), F32)],
        cost_estimate=about(16 * pairs, 4.0),
        compiler_params=pltpu.CompilerParams(vmem_limit_bytes=48 << 20),
        name="attention_forward",
    )(table, *[projected] * (3 * pairs))
    return outs, logs


def backward_kernel(
    table_ref, q_ref, k_ref, v_ref, log_ref, *refs, block, count
):
    out, sums, dots, grads = refs[-4:]
    blocks = (len(refs) - 4) // 2
    length = q_ref.shape[0]
    step = pl.program_id(0)
    lane = lax.broadcasted_iota(jnp.int32, (1, LANES), 1) // HD

    @pl.when(step == 0)
    def _():
        sums[...] = jnp.zeros_like(sums)
        for r in range(blocks):
            low, attended = refs[r][...], refs[blocks + r][...]
            height = low.shape[0]
            grads[r * height : (r + 1) * height, :] = low
            products = low.astype(F32) * attended.astype(F32)
            dots[:, r * height : (r + 1) * height] = as_rows(
                [
                    jnp.sum(jnp.where(lane == h, products, 0.0), axis=1, keepdims=True)
                    for h in range(PAIR)
                ],
                8,
            )

    grad = grads[...]
    start = pl.multiple_of(step * block, block)
    rows = start + lax.broadcasted_iota(jnp.int32, (block, 1), 0)
    columns = lax.broadcasted_iota(jnp.int32, (1, length), 1)
    allowed = segments_at(rows, table_ref, count) == segments_at(columns, table_ref, count)
    query = q_ref[...] * BF(HD**-0.5)
    keys = k_ref[...]
    values = v_ref[...]
    none = jnp.zeros_like(keys)
    key_back = jnp.zeros((block, LANES), F32)
    value_back = jnp.zeros((block, LANES), F32)
    for h in range(PAIR):
        key = jnp.where(lane == h, keys, none)
        value = jnp.where(lane == h, values, none)
        scores = jnp.where(allowed, dot(key, query, 1, 1), MASKED)
        probs = jnp.exp(scores - log_ref[h : h + 1, :])
        probs_back = dot(value, grad, 1, 1)
        score_back = (probs * (probs_back - dots[h : h + 1, :])).astype(BF)
        value_back = jnp.where(lane == h, dot(probs.astype(BF), grad, 1, 0), value_back)
        key_back = jnp.where(lane == h, dot(score_back, query, 1, 0), key_back)
        sums[...] += dot(score_back, key, 0, 0)
    out[pl.ds(start, block), LANES : 2 * LANES] = key_back.astype(BF)
    out[pl.ds(start, block), 2 * LANES :] = value_back.astype(BF)

    @pl.when(step == pl.num_programs(0) - 1)
    def _():
        out[:, :LANES] = (sums[...] * HD**-0.5).astype(BF)


def attention_backward(pair, projected, table, grads, attended, logs):
    length = projected.shape[0]
    block = min(512, length)

    def column(c):
        return pl.BlockSpec((length, LANES), lambda i, t: (0, c))

    return pl.pallas_call(
        partial(backward_kernel, block=block, count=table.shape[0] - 2),
        grid_spec=pltpu.PrefetchScalarGridSpec(
            num_scalar_prefetch=1,
            grid=(length // block,),
            in_specs=[
                column(3 * pair),
                pl.BlockSpec((block, LANES), lambda i, t: (i, 3 * pair + 1)),
                pl.BlockSpec((block, LANES), lambda i, t: (i, 3 * pair + 2)),
                fixed((8, length), pair, 0),
            ]
            + [fixed((value.shape[0], LANES), 0, pair) for value in (*grads, *attended)],
            out_specs=fixed((length, 3 * LANES)),
            scratch_shapes=[
                pltpu.VMEM((length, LANES), F32),
                pltpu.VMEM((8, length), F32),
                pltpu.VMEM((length, LANES), BF),
            ],
        ),
        out_shape=jax.ShapeDtypeStruct((length, 3 * LANES), BF),
        cost_estimate=about(30, 4.0),
        compiler_params=pltpu.CompilerParams(vmem_limit_bytes=56 << 20),
        name="attention_backward",
    )(table, projected, projected, projected, logs, *grads, *attended)


def adamw_kernel(scale_ref, *refs, turned, parts):
    clip, fix_one, fix_two = scale_ref[0], scale_ref[1], scale_ref[2]
    step = pl.program_id(0)
    grads, ins, outs = refs[: 6 + parts], refs[6 + parts : 27 + parts], refs[27 + parts :]

    def update(k, grad):
        param, moment, square = (ref[...] for ref in ins[3 * k : 3 * k + 3])
        grad_ref, moment_ref, square_ref, change_ref = outs[4 * k : 4 * k + 4]
        clipped = grad * clip
        moment_new = BETA_ONE * moment + (1.0 - BETA_ONE) * clipped
        square_new = BETA_TWO * square + (1.0 - BETA_TWO) * clipped * clipped
        grad_ref[...] = grad
        moment_ref[...] = moment_new
        square_ref[...] = square_new
        change_ref[...] = -RATE * (
            moment_new / fix_one / (jnp.sqrt(square_new / fix_two) + ADAM_EPS) + DECAY * param
        )

    update(
        0,
        jnp.stack(
            [
                jnp.concatenate([ref[:, c * LANES : (c + 1) * LANES] for ref in grads[:parts]], axis=1)
                for c in range(3)
            ]
        ),
    )
    update(2, grads[parts + 1][...].astype(F32))
    update(3, jnp.transpose(grads[parts + 2][...].astype(F32)))

    @pl.when(step < turned)
    def _():
        update(1, jnp.transpose(grads[parts][...]))

    @pl.when(step == 0)
    def _():
        for k in range(3):
            update(4 + k, grads[parts + 3 + k][...])


def in_hbm(value):
    return pltpu.with_memory_space_constraint(value, pltpu.HBM)


def adamw(scales, attend_parts, others, params, firsts, squares):
    shard = params[0].shape[1]
    steps = params[3].shape[0] // LANES
    turned = params[1].shape[0] // LANES
    rows = shard // steps

    def last(i):
        return jnp.minimum(i, turned - 1)

    state = [
        pl.BlockSpec((3, rows, params[0].shape[2]), lambda i: (0, i, 0)),
        pl.BlockSpec((LANES, shard), lambda i: (last(i), 0)),
        pl.BlockSpec((rows, params[2].shape[1]), lambda i: (i, 0)),
        pl.BlockSpec((LANES, shard), lambda i: (i, 0)),
    ] + [pl.BlockSpec(value.shape, lambda i: (0, 0)) for value in params[4:]]
    grad_specs = (
        [pl.BlockSpec((rows, 3 * LANES), lambda i: (i, 0)) for _ in attend_parts]
        + [
            pl.BlockSpec((shard, LANES), lambda i: (0, last(i))),
            state[2],
            pl.BlockSpec((shard, LANES), lambda i: (0, i)),
        ]
        + state[4:]
    )
    ins = [in_hbm(value) for group in zip(params, firsts, squares) for value in group]
    return pl.pallas_call(
        partial(adamw_kernel, turned=turned, parts=len(attend_parts)),
        grid=(steps,),
        in_specs=[smem()] + grad_specs + [spec for spec in state for _ in range(3)],
        out_specs=[spec for spec in state for _ in range(4)],
        out_shape=[jax.ShapeDtypeStruct(value.shape, F32) for value in params for _ in range(4)],
        cost_estimate=about(6),
        compiler_params=pltpu.CompilerParams(vmem_limit_bytes=50 << 20),
        name="adamw",
    )(scales, *attend_parts, *others, *ins)


def local(
    tokens,
    cotangent,
    lengths,
    attend,
    mixing,
    expand,
    contract,
    outer_norms,
    head_norms,
    unit_norms,
    attend_moment,
    mixing_moment,
    expand_moment,
    contract_moment,
    outer_moment,
    head_moment,
    unit_moment,
    attend_square,
    mixing_square,
    expand_square,
    contract_square,
    outer_square,
    head_square,
    unit_square,
):
    height = tokens.shape[0]
    shard_count = lax.axis_size("mp")
    device_count = lax.axis_size("dp") * shard_count
    length_all = height * shard_count
    place = lax.axis_index("mp")
    sequences = lengths.shape[1]
    head_width = attend.shape[2]
    unit_width = expand.shape[1]
    shard = attend.shape[1]
    pairs = head_width // LANES
    step = height
    everything = Rows(list(range(shard_count)), height, step)
    near = Rows([0, 1], height, step)
    far = Rows(list(range(2, shard_count)), height, step)
    table = jnp.concatenate([lengths[0], jnp.stack([place * height, place]).astype(jnp.int32)])

    by_pair = attend.astype(BF).reshape(3, shard, pairs, LANES).transpose(1, 2, 0, 3)
    by_pair = by_pair.reshape(shard, 3 * head_width)
    work_even = gather_groups(jnp.concatenate([by_pair, mixing.astype(BF).T], axis=1))

    sizes = [x.size for x in (outer_norms, head_norms, unit_norms)]
    starts = [0, sizes[0], sizes[0] + sizes[1]]
    packed = jnp.concatenate([outer_norms.reshape(-1), head_norms.reshape(-1), unit_norms.reshape(-1)])
    tables = exchange_all(jnp.broadcast_to(packed[None], (device_count, packed.shape[0])))

    token_near, token_even = gather_near(tokens)
    work_odd = cross_groups(work_even, [*token_even, tables])
    token_far = gather_far(after(token_even, work_odd))
    work_in, work_mix = place_groups(work_even, work_odd, [3 * head_width, head_width])
    wide_shard = after(
        [jnp.concatenate([expand.astype(BF), contract.astype(BF).T], axis=1)], [work_in]
    )[0]
    weights = lax.all_gather(wide_shard, "dp", axis=0, tiled=True)

    def unpack(k, rows):
        part = tables[:, starts[k] : starts[k] + sizes[k]].reshape(device_count, rows, -1)
        return part.transpose(1, 0, 2).reshape(rows, -1)

    outer = unpack(0, 4)
    head_gains = unpack(1, 2)
    unit_local = lax.dynamic_slice_in_dim(unpack(2, 2), place * unit_width, unit_width, 1)
    normed_all, projected = project(everything, token_near + token_far, work_in, outer)
    mix_near, mix_even = gather_near(work_mix)
    attended, logs = attention_forward(everything, projected, table)
    back_near, back_even = gather_near(after([cotangent], [normed_all])[0])
    attended, logs, mix_near, mix_even, back_even = lax.optimization_barrier(
        (attended, logs, mix_near, mix_even, back_even)
    )
    mixes = mix_near + gather_far(mix_even)
    head_blocks = [attended[0]] + [swap(attended[r], r) for r in range(1, shard_count)]
    middle, mid_own, mixed_in = mix_rows(
        table, sequences, head_blocks, mixes, head_gains, tokens, outer
    )
    mid_near, mid_even = gather_near(mid_own)
    cotangent_blocks = back_near + gather_far(back_even)

    back_all, unit_in = feed_back(everything, cotangent_blocks, table, sequences, weights)
    kept = widen(near, mid_near, weights, unit_in, unit_local)
    mid_far = gather_far(after(mid_even, kept))
    mid_all, activated, slopes, sums = widen(far, mid_far, weights, unit_in, unit_local, kept)
    unit_totals = token_totals(sums)
    low_far, wide_far, sums_far, *far_terms = narrow_back(
        far, activated, slopes, unit_in, unit_totals, unit_local, weights
    )
    far_sums = [value.astype(BF) for value in sum_chip(far_terms)]
    arrived = sum_far(far_sums)
    late_slopes = after([slopes], far_sums)[0]
    unit_low, widened_low, sums_near, *near_terms = narrow_back(
        near, activated, late_slopes, unit_in, unit_totals, unit_local, weights, (low_far, wide_far)
    )
    contract_back = weight_grad(back_all, unit_low)
    arrived = after(arrived, [*near_terms, contract_back])
    mid_terms = [near_terms[0], swap(near_terms[1], 1), *arrived]
    middle_back, middle_low, outer_sums, head_sums, *head_grads = mix_rows_back(
        table, sequences, mid_terms, middle, cotangent, outer, head_blocks, mixes, head_gains
    )

    grad_even = [head_grads[0]] + [swap(head_grads[r], r) for r in range(1, shard_count)]
    feed_terms = feed_rows(everything, after([unit_low], [middle_low])[0], weights)
    expand_back = weight_grad(mid_all, after([widened_low], [middle_low])[0])
    mix_terms = mix_grads(middle_low, mixed_in, shard_count)
    grad_blocks = [grad_even[0]] + after(grad_even[1:], [*feed_terms, *mix_terms, expand_back])

    def column_sums(value):
        return jnp.sum(value.reshape(2, 8, -1), axis=1)

    def for_owners(value):
        return value.reshape(value.shape[0], device_count, -1).transpose(1, 0, 2).reshape(device_count, -1)

    unit_sums = lax.dynamic_update_slice_in_dim(
        jnp.zeros((2, FF), F32), column_sums(sums_near + sums_far), place * unit_width, 1
    )
    terms = jnp.concatenate(
        [
            for_owners(column_sums(outer_sums)),
            for_owners(column_sums(head_sums)),
            for_owners(unit_sums),
        ],
        axis=1,
    )
    feed_sums = [value.astype(BF) for value in sum_chip(feed_terms[2:])]
    mix_sums = [value.astype(BF) for value in sum_chip(mix_terms[2:])]
    grad_blocks = after(grad_blocks, [*feed_sums, *mix_sums])
    term_sums = exchange_all(after([terms], grad_blocks)[0])
    *mix_sums, last = after([*mix_sums, feed_sums[-1]], grad_blocks)
    mix_arrived = sum_far(mix_sums)
    feed_arrived = sum_far([*feed_sums[:-1], last])
    backs = [attention_backward(0, projected, table, grad_blocks, attended, logs)]
    backs, feed_arrived, mix_arrived, term_sums = lax.optimization_barrier(
        (backs, feed_arrived, mix_arrived, term_sums)
    )
    mix_terms = [mix_terms[0], swap(mix_terms[1], 1), *mix_arrived]
    pieces = [exchange_groups(attend_rows(normed_all, backs[0], mix_terms))]
    for pair in range(1, pairs):
        backs.append(attention_backward(pair, projected, table, grad_blocks, attended, logs))
        value = after([attend_rows(normed_all, backs[-1])], pieces)[0]
        pieces.append(exchange_groups(value))
        late = after(backs, [value])

    def scatter(value):
        return lax.psum_scatter(value, "dp", scatter_dimension=0, tiled=True)

    contract_grad = scatter(contract_back)
    expand_grad = scatter(expand_back)
    if pairs == 1:
        late = backs
    far_terms = input_back(far, late, work_in)
    far_sums = [value.astype(BF) for value in sum_chip(far_terms)]
    near_terms = input_back(near, after(late, far_sums), work_in)
    arrived = sum_far(far_sums)
    outer, expand_late, contract_late, term_sums = after(
        [outer, expand_grad, contract_grad, term_sums], near_terms
    )

    local_squares = jnp.float32(0.0)
    for gradient in [expand_late, contract_late]:
        local_squares = local_squares + jnp.sum(jnp.square(gradient.astype(F32)))
    local_squares, near_terms, pieces = lax.optimization_barrier((local_squares, near_terms, pieces))
    norm_sums = jnp.sum(term_sums, axis=0)
    outer_rows = lax.dynamic_slice_in_dim(outer, lax.axis_index("dp") * shard, shard, 1).T
    attend_parts, outer_terms = [], 0.0
    for pair, piece in enumerate(pieces):
        grad, sums, *beside = attend_sums(
            piece, by_pair[:, 3 * LANES * pair : 3 * LANES * (pair + 1)], outer_rows, 3 * LANES
        )
        attend_parts.append(grad)
        outer_terms = outer_terms + sums
        if beside:
            mixing_grad = beside[0]
    outer_terms = outer_terms.T
    for bit in mp_bits():
        outer_terms = outer_terms + swap(outer_terms, bit)
    own_norms = outer_norms.shape[1]
    first_grad = lax.dynamic_slice_in_dim(outer_terms, place * own_norms, own_norms, 1)
    half = sizes[0] // 2
    norm_grads = [
        jnp.concatenate([first_grad, norm_sums[:half].reshape(2, own_norms)], axis=0),
        norm_sums[half : half + sizes[1]].reshape(head_norms.shape),
        norm_sums[half + sizes[1] :].reshape(unit_norms.shape),
    ]

    for gradient in [*norm_grads, mixing_grad, *attend_parts]:
        local_squares = local_squares + jnp.sum(gradient * gradient)
    all_squares = exchange_all(jnp.broadcast_to(local_squares, (device_count, 128)))
    result = middle + sum_near(feed_terms[:2], after(feed_arrived, [local_squares]))
    result = result.astype(BF)
    normed_back = sum_near(near_terms, arrived)
    inputs = tokens.astype(F32)
    first_normed, first_factor = norm_rows(inputs)
    input_grad = middle_back + norm_back(normed_back, first_normed, first_factor, outer[0])[0]
    all_squares, input_grad, result = lax.optimization_barrier((all_squares, input_grad, result))
    norm = jnp.sqrt(jnp.sum(all_squares[:, 0]))
    clip = jnp.minimum(1.0, MAX_NORM / (norm + 1e-06))
    count_steps = jnp.float32(ADAM_STEP)
    fix_one = 1.0 - jnp.power(jnp.float32(BETA_ONE), count_steps)
    fix_two = 1.0 - jnp.power(jnp.float32(BETA_TWO), count_steps)
    results = adamw(
        jnp.stack([clip, fix_one, fix_two]),
        attend_parts,
        [mixing_grad, expand_grad, contract_grad, *norm_grads],
        (attend, mixing, expand, contract, outer_norms, head_norms, unit_norms),
        (
            attend_moment,
            mixing_moment,
            expand_moment,
            contract_moment,
            outer_moment,
            head_moment,
            unit_moment,
        ),
        (
            attend_square,
            mixing_square,
            expand_square,
            contract_square,
            outer_square,
            head_square,
            unit_square,
        ),
    )
    return (result, input_grad, norm, *results)


def solution(mesh):
    rows = P(ALL, None)
    norms = P(None, ALL)
    weights = (P(None, "dp", "mp"), P("mp", "dp"), P("dp", "mp"), P("mp", "dp"))
    states = weights + (norms,) * 3
    outs = (rows, rows, P())
    for spec in states:
        outs = outs + (spec,) * 4
    return jax.shard_map(
        local,
        mesh=mesh,
        in_specs=(rows, rows, P("dp", None)) + states * 3,
        out_specs=outs,
        check_vma=False,
    )
```

time: 641 us -> 433 us (0.68)
  waiting for transfers between devices: 226 us -> 58.1 us
  Pallas kernels: 86.1 us -> 235 us
  matrix products: 98.7 us -> 0 us
  other arithmetic: 87.8 us -> 29.2 us
  local copies, waits for them, and re-layouts: 55.2 us -> 18.1 us
  starting transfers between devices: 32 us -> 47.8 us
  blocking collectives: 27.8 us -> 19.4 us
    pallas_call x2 -> x23, Pallas kernels: 86.1 us -> 235 us  [the longest x9 81.3 us: call(): pl.pallas_call(body, grid_spec=pltpu.PrefetchScalarGridSpec(num_scalar_pr...]
    ppermute x32 -> x34, waiting for transfers between devices: 159 us -> 24.3 us  [swap(): return lax.ppermute(value, 'mp', [(i, i ^ bit) for i in range(count)])]
    dot_general x12 -> x0, matrix products: 98.7 us -> none  [the longest x10 61.4 us: dot(): lax.dot_general(left, right, (((left_dim,), (right_dim,)), ((), ())), pre...]
    reduce_scatter x4 -> x2, waiting for transfers between devices: 51.8 us -> 3.82 us  [scatter(): return lax.psum_scatter(value, 'dp', scatter_dimension=0, tiled=True)]
    all_gather x1 -> x0, blocking collectives: 27.8 us -> none  [local(): work_mix = lax.all_gather(mixing.astype(BF).T, 'dp', axis=0, tiled=True)]
    unnamed x191 -> x96, local copies, waits for them, and re-layouts: 32.7 us -> 12.7 us
    all_to_all x0 -> x1, blocking collectives: none -> 19.4 us  [exchange_all(): return lax.all_to_all(value, ALL, 0, 0, tiled=True)]
    convert_element_type x11 -> x6, other arithmetic: 31.9 us -> 12.5 us  [the longest x2 4.71 us: local(): far_sums = [value.astype(BF) for value in sum_chip(far_terms)]]
  transfers between devices with their start and end apart: 42 -> 48, of which waited for: 20 -> 17; matrix products, arithmetic and copies ran while one was open for 27% -> 8% of each run, Pallas kernels for 9% -> 48%
where the time goes in v2:
time: 433 us; the launch traced here: 429 us
  Pallas kernels  235 us (54%)
  waiting for transfers between devices  58.1 us (13%)
  starting transfers between devices  47.8 us (11%)
  other arithmetic  29.2 us (7%)
  between operations  21.8 us (5%)
  blocking collectives  19.4 us (4%)
  local copies, waits for them, and re-layouts  18.1 us (4%)
    pallas_call x9, Pallas kernels, call(): pl.pallas_call(body, grid_spec=pltpu.PrefetchScalarGridSpec(num_scalar_pr...  81.3 us
    pallas_call x2, Pallas kernels, attention_backward(): pl.pallas_call(partial(backward_kernel, block=block, count=table.shape[0]...  58.2 us
    pallas_call x1, Pallas kernels, attention_forward(): pl.pallas_call(kernel, grid_spec=pltpu.PrefetchScalarGridSpec(num_scalar_...  30.8 us
    ppermute x34, waiting for transfers between devices, swap(): return lax.ppermute(value, 'mp', [(i, i ^ bit) for i in range(count)])  24.3 us
    ppermute x34, starting transfers between devices, swap(): return lax.ppermute(value, 'mp', [(i, i ^ bit) for i in range(count)])  22.4 us
    all_to_all x1, blocking collectives, exchange_all(): return lax.all_to_all(value, ALL, 0, 0, tiled=True)  19.4 us
    pallas_call x2, Pallas kernels, weight_grad(): pl.pallas_call(kernel, grid=(left.shape[1] // block,), in_specs=[pl.Block...  17.3 us
    pallas_call x2, Pallas kernels, attend_rows(): pl.pallas_call(kernel, grid=(groups,), in_specs=[pl.BlockSpec((length, D)...  15.9 us
  transfers between devices with their start and end apart: 48, of which 17 were waited for; matrix products, arithmetic and copies ran while one was open for 8% of the time, Pallas kernels for 48%

profile of v2, /device:TPU:0, one launch (start us, length us, event | category | flops | bytes accessed | tf_op | source)
XLA Modules:
  0.0 428.9 jit_solution(17013416118894779249)
XLA Ops:
  22.4 19.4 %all_to_all.40 = f32[32,1,448]{2,1,0:T(1,128)S(1)} all-to-all(f32[32,1,448]{2,1,0:T(1,128)S(1)} %broadcast_in_dim.8), channel_id=1, replica_groups=mesh['dp'=8,'mp'=4] {'dp','mp'}, dimensions={0} | all-to-all | bytes 114688 | tf_op jit(solution)/shard_map/all_to_all | solution.py:94
  51.5 4.8 %collective-permute-done.8.refs_7_ = bf16[128,1024]{1,0:T(8,128)(2,1)} collective-permute-done((bf16[128,1024]{1,0:T(8,128)(2,1)}, bf16[128,1024]{1,0:T(8,128)(2,1)}, u32[]{:S(2)}, u32[]{:S(2)}) %collective-permute-start.8) | collective-permute-done | bytes 262176 | tf_op jit(solution)/shard_map/ppermute | solution.py:99
  65.6 8.8 %project.1 = (bf16[2048,1024]{1,0:T(8,128)(2,1)}, bf16[2048,768]{1,0:T(8,128)(2,1)}) custom-call(bf16[512,1024]{1,0:T(8,128)(2,1)S(1)} %copy-done, bf16[512,1024]{1,0:T(8,128)(2,1)S(1)} %collective-permute-done.refs_1_, bf16[512,1024]{1,0:T(8,128)(2,1)S(1)} %collective-permute-done.1.refs_2_, bf16[512,1024]{1,0:T(8,128)(2,1)} %collective-permute-done.9.refs_3_, ...), custom_call_target="tpu_custom_call" | custom-call | flops 36800000000 | bytes 3200000 | tf_op jit(solution)/shard_map/project/pallas_call | solution.py:281
  76.9 30.8 %attention_forward.1 = (bf16[512,256]{1,0:T(8,128)(2,1)S(1)}, bf16[512,256]{1,0:T(8,128)(2,1)S(1)}, bf16[512,256]{1,0:T(8,128)(2,1)S(1)}, bf16[512,256]{1,0:T(8,128)(2,1)S(1)}, f32[16,2048]{1,0:T(8,128)S(1)}) custom-call(s32[6]{0:T(128)S(1)} %pad_add_fusion.table_ref.refs_0_, bf16[2048,768]{1,0:T(8,128)(2,1)S(1)} %copy-done.19, ...), custom_call_target="tpu_custom_call" | custom-call | flops 147200000000 | bytes 12800000 | tf_op jit(solution)/shard_map/attention_forward/pallas_call | solution.py:779
  111.7 6.6 %collective-permute-done.14.refs_2_.refs_9_ = bf16[512,256]{1,0:T(8,128)(2,1)} collective-permute-done((bf16[512,256]{1,0:T(8,128)(2,1)S(1)}, bf16[512,256]{1,0:T(8,128)(2,1)}, u32[]{:S(2)}, u32[]{:S(2)}) %collective-permute-start.14) | collective-permute-done | bytes 262176 | tf_op jit(solution)/shard_map/ppermute | solution.py:31
  123.2 5.8 %mix_rows.1 = (f32[512,1024]{1,0:T(8,128)}, bf16[512,1024]{1,0:T(8,128)(2,1)}, bf16[512,1024]{1,0:T(8,128)(2,1)}) custom-call(s32[6]{0:T(128)S(1)} %pad_add_fusion.table_ref.refs_0_, bf16[512,256]{1,0:T(8,128)(2,1)S(1)} %copy-done.22, bf16[512,256]{1,0:T(8,128)(2,1)S(1)} %collective-permute-done.13.refs_1_.refs_8_, ...), custom_call_target="tpu_custom_call" | custom-call | flops 27599998976 | bytes 2400000 | tf_op jit(solution)/shard_map/mix_rows/pallas_call | solution.py:337
  131.3 7.8 %all-gather.2.cloned.1.call-done.refs_5_.refs_2_.refs_1_ = bf16[1024,2048]{1,0:T(8,128)(2,1)} async-done(((bf16[128,2048]{1,0:T(8,128)(2,1)}), bf16[1024,2048]{1,0:T(8,128)(2,1)}) %all-gather.2.cloned.1.call-update) | async-done | bytes 4194320 | tf_op jit(solution)/shard_map/all_gather | solution.py:1023
  139.1 10.0 %feed_back.1 = (bf16[2048,1024]{1,0:T(8,128)(2,1)}, bf16[2048,1024]{1,0:T(8,128)(2,1)}) custom-call(s32[6]{0:T(128)S(1)} %pad_add_fusion.table_ref.refs_0_, bf16[512,1024]{1,0:T(8,128)(2,1)} %refs_4_.1, bf16[512,1024]{1,0:T(8,128)(2,1)S(1)} %collective-permute-done.19.refs_2_, bf16[512,1024]{1,0:T(8,128)(2,1)} %collective-permute-done.12.refs_3_, ...), custom_call_target="tpu_custom_call" | custom-call | flops 36800000000 | bytes 3200000 | tf_op jit(solution)/shard_map/feed_back/pallas_call | solution.py:281
  150.4 8.8 %widen.2 = (bf16[2048,1024]{1,0:T(8,128)(2,1)}, f32[2048,1024]{1,0:T(8,128)}, bf16[2048,1024]{1,0:T(8,128)(2,1)}, f32[4,2048]{1,0:T(4,128)S(1)}) custom-call(bf16[512,1024]{1,0:T(8,128)(2,1)S(1)} %copy-done.7, bf16[512,1024]{1,0:T(8,128)(2,1)} %collective-permute-done.18.refs_1_, bf16[1024,2048]{1,0:T(8,128)(2,1)} %all-gather.2.cloned.1.call-done.refs_5_.refs_2_.refs_1_, ...), custom_call_target="tpu_custom_call" | custom-call | flops 18400000000 | bytes 1600000 | tf_op jit(solution)/shard_map/widen/pallas_call | solution.py:281
  161.9 8.6 %widen.3 = (bf16[2048,1024]{1,0:T(8,128)(2,1)}, f32[2048,1024]{1,0:T(8,128)}, bf16[2048,1024]{1,0:T(8,128)(2,1)}, f32[4,2048]{1,0:T(4,128)S(1)}) custom-call(bf16[512,1024]{1,0:T(8,128)(2,1)S(1)} %collective-permute-done.17.refs_0_, ...), custom_call_target="tpu_custom_call", output_to_operand_aliasing={{0}: (5, {}), {1}: (6, {}), {2}: (7, {}), {3}: (8, {})} | custom-call | flops 18400000000 | bytes 1600000 | tf_op jit(solution)/shard_map/widen/pallas_call | solution.py:281
  175.7 12.0 %narrow_back.2 = (bf16[2048,1024]{1,0:T(8,128)(2,1)}, bf16[2048,1024]{1,0:T(8,128)(2,1)}, f32[16,1024]{1,0:T(8,128)S(1)}, bf16[512,1024]{1,0:T(8,128)(2,1)}, bf16[512,1024]{1,0:T(8,128)(2,1)}) custom-call(f32[2048,1024]{1,0:T(8,128)} %get-tuple-element.197.refs_0_, bf16[2048,1024]{1,0:T(8,128)(2,1)} %get-tuple-element.202.refs_1_, ...), custom_call_target="tpu_custom_call" | custom-call | flops 18400000000 | bytes 1600000 | tf_op jit(solution)/shard_map/narrow_back/pallas_call | solution.py:281
  193.7 12.4 %narrow_back.3 = (bf16[2048,1024]{1,0:T(8,128)(2,1)}, bf16[2048,1024]{1,0:T(8,128)(2,1)}, f32[16,1024]{1,0:T(8,128)S(1)}, bf16[512,1024]{1,0:T(8,128)(2,1)}, bf16[512,1024]{1,0:T(8,128)(2,1)}) custom-call(f32[2048,1024]{1,0:T(8,128)} %get-tuple-element.197.refs_0_, ...), custom_call_target="tpu_custom_call", output_to_operand_aliasing={{0}: (6, {}), {1}: (7, {})} | custom-call | flops 18400000000 | bytes 1600000 | tf_op jit(solution)/shard_map/narrow_back/pallas_call | solution.py:281
  206.0 8.6 %weight_grad.2 = bf16[1024,1024]{1,0:T(8,128)(2,1)} custom-call(bf16[2048,1024]{1,0:T(8,128)(2,1)} %get-tuple-element.208.left_ref, bf16[2048,1024]{1,0:T(8,128)(2,1)} %get-tuple-element.219.right_ref.refs_0_), custom_call_target="tpu_custom_call" | custom-call | flops 36800000000 | bytes 3200000 | tf_op jit(solution)/shard_map/weight_grad/pallas_call | solution.py:569
  217.5 8.9 %mix_rows_back.1 = (f32[512,1024]{1,0:T(8,128)}, bf16[512,1024]{1,0:T(8,128)(2,1)}, f32[16,1024]{1,0:T(8,128)S(1)}, f32[16,1024]{1,0:T(8,128)S(1)}, bf16[512,256...) custom-call(s32[6]{0:T(128)S(1)} %pad_add_fusion.table_ref.refs_0_, ...), custom_call_target="tpu_custom_call" | custom-call | flops 36800000000 | bytes 3200000 | tf_op jit(solution)/shard_map/mix_rows_back/pallas_call | solution.py:337
  228.4 9.8 %feed_rows.1 = (bf16[512,1024]{1,0:T(8,128)(2,1)}, bf16[512,1024]{1,0:T(8,128)(2,1)}, bf16[512,1024]{1,0:T(8,128)(2,1)}, bf16[512,1024]{1,0:T(8,128)(2,1)}) custom-call(bf16[2048,1024]{1,0:T(8,128)(2,1)} %get-tuple-element.219.right_ref.refs_0_, bf16[1024,2048]{1,0:T(8,128)(2,1)} %all-gather.2.cloned.1.call-done.refs_5_.refs_2_.refs_1_), custom_call_target="tpu_custom_call" | custom-call | flops 36800000000 | bytes 3200000 | tf_op jit(solution)/shard_map/feed_rows/pallas_call | solution.py:281
  241.8 8.7 %weight_grad.3 = bf16[1024,1024]{1,0:T(8,128)(2,1)} custom-call(bf16[2048,1024]{1,0:T(8,128)(2,1)} %get-tuple-element.196.left_ref, bf16[2048,1024]{1,0:T(8,128)(2,1)} %get-tuple-element.213.right_ref), custom_call_target="tpu_custom_call" | custom-call | flops 36800000000 | bytes 3200000 | tf_op jit(solution)/shard_map/weight_grad/pallas_call | solution.py:569
  259.6 29.2 %attention_backward.2.back_ref.refs_0_ = bf16[2048,384]{1,0:T(8,128)(2,1)} custom-call(s32[6]{0:T(128)} %copy-done.6, bf16[2048,768]{1,0:T(8,128)(2,1)} %get-tuple-element.171.refs_0_.refs_1_.refs_2_.refs_3_.refs_4_.refs_5_.q_ref.k_ref.v_ref, bf16[2048,768]{1,0:T(8,128)(2,1)} %get-tuple-element.171.refs_0_.refs_1_.refs_2_.refs_3_.refs_4_.refs_5_.q_ref.k_ref.v_ref, ...), custom_call_target="tpu_custom_call" | custom-call | flops 138000007168 | bytes 12000000 | tf_op jit(solution)/shard_map/attention_backward/pallas_call | solution.py:858
  291.7 8.2 %attend_rows.3 = bf16[8,144,640]{2,1,0:T(8,128)(2,1)} custom-call(bf16[2048,1024]{1,0:T(8,128)(2,1)} %get-tuple-element.178.normed_ref, bf16[2048,384]{1,0:T(8,128)(2,1)} %attention_backward.2.back_ref.refs_0_, bf16[1024,256]{1,0:T(8,128)(2,1)S(1)} %copy-done.20, bf16[1024,256]{1,0:T(8,128)(2,1)S(1)} %collective-permute-done.34.refs_1_, ...), custom_call_target="tpu_custom_call" | custom-call | flops 23000000512 | bytes 2000000 | tf_op jit(solution)/shard_map/attend_rows/pallas_call | solution.py:639
  304.4 29.0 %attention_backward.3.back_ref.refs_1_ = bf16[2048,384]{1,0:T(8,128)(2,1)} custom-call(s32[6]{0:T(128)} %copy-done.6, bf16[2048,768]{1,0:T(8,128)(2,1)} %get-tuple-element.171.refs_0_.refs_1_.refs_2_.refs_3_.refs_4_.refs_5_.q_ref.k_ref.v_ref, bf16[2048,768]{1,0:T(8,128)(2,1)} %get-tuple-element.171.refs_0_.refs_1_.refs_2_.refs_3_.refs_4_.refs_5_.q_ref.k_ref.v_ref, ...), custom_call_target="tpu_custom_call" | custom-call | flops 138000007168 | bytes 12000000 | tf_op jit(solution)/shard_map/attention_backward/pallas_call | solution.py:858
  334.9 7.7 %attend_rows.2 = bf16[8,144,384]{2,1,0:T(8,128)(2,1)} custom-call(bf16[2048,1024]{1,0:T(8,128)(2,1)} %get-tuple-element.178.normed_ref, bf16[2048,384]{1,0:T(8,128)(2,1)S(1)} %copy-done.14), custom_call_target="tpu_custom_call" | custom-call | flops 23000000512 | bytes 2000000 | tf_op jit(solution)/shard_map/attend_rows/pallas_call | solution.py:639
  345.6 5.5 %input_back.2 = (bf16[512,1024]{1,0:T(8,128)(2,1)}, bf16[512,1024]{1,0:T(8,128)(2,1)}) custom-call(bf16[2048,384]{1,0:T(8,128)(2,1)S(1)} %copy-done.12, bf16[2048,384]{1,0:T(8,128)(2,1)S(1)} %copy-done.15, bf16[1024,768]{1,0:T(8,128)(2,1)} %get-tuple-element.170.refs_4_.refs_2_), custom_call_target="tpu_custom_call" | custom-call | flops 18400000000 | bytes 1600000 | tf_op jit(solution)/shard_map/input_back/pallas_call | solution.py:281
  361.5 5.6 %input_back.3 = (bf16[512,1024]{1,0:T(8,128)(2,1)}, bf16[512,1024]{1,0:T(8,128)(2,1)}) custom-call(bf16[2048,384]{1,0:T(8,128)(2,1)S(1)} %copy-done.13, bf16[2048,384]{1,0:T(8,128)(2,1)S(1)} %copy-done.16, bf16[1024,768]{1,0:T(8,128)(2,1)} %get-tuple-element.170.refs_4_.refs_2_), custom_call_target="tpu_custom_call" | custom-call | flops 18400000000 | bytes 1600000 | tf_op jit(solution)/shard_map/input_back/pallas_call | solution.py:281
  377.2 6.9 %all-to-all-done.3.piece_ref = bf16[8,144,384]{2,1,0:T(8,128)(2,1)S(1)} async-done(((bf16[8,144,384]{2,1,0:T(8,128)(2,1)}), bf16[8,144,384]{2,1,0:T(8,128)(2,1)S(1)}, u32[]{:S(2)}, u32[]{:S(2)}) %all-to-all-start.3) | async-done | bytes 884768 | tf_op jit(solution)/shard_map/all_to_all | solution.py:152
  412.6 8.4 %adamw.1 = (f32[3,128,256]{2,1,0:T(8,128)}, f32[3,128,256]{2,1,0:T(8,128)}, f32[3,128,256]{2,1,0:T(8,128)}, f32[3,128,256]{2,1,0:T(8,128)}, f32[256,128]{1,0:T(8...) custom-call(f32[3]{0:T(128)S(1)} %pad_maximum_fusion.5.scale_ref, ...), custom_call_target="tpu_custom_call" | custom-call | flops 27599998976 | bytes 2400000 | tf_op jit(solution)/shard_map/adamw/pallas_call | solution.py:953
  (269 shorter events, 134.9 us)
Async XLA Ops:
  7.3 131.9 %all-gather.2.cloned.1.call-start = ((), (), s32[]{:S(2)}) async-start(), calls=%async_computation.7 | async-start | bytes 4718592 | tf_op jit(solution)/shard_map/all_gather | solution.py:1023
  7.3 34.6 %collective-permute-start.1 = (bf16[512,1024]{1,0:T(8,128)(2,1)}, bf16[512,1024]{1,0:T(8,128)(2,1)S(1)}, u32[]{:S(2)}, u32[]{:S(2)}) collective-permute-start(bf16[512,1024]{1,0:T(8,128)(2,1)} %refs_9_.2), channel_id=1, source_target_pairs={{0,2},{1,3},{2,0},{3,1},{4,6},{5,7},{6,4},{7,5},{8,10},{9,11},{10,... | collective-permute-start | bytes 3145736 | tf_op jit(solution)/shard_map/ppermute | solution.py:31
  14.3 27.6 %collective-permute-start.4 = (bf16[128,1024]{1,0:T(8,128)(2,1)S(1)}, bf16[128,1024]{1,0:T(8,128)(2,1)}, u32[]{:S(2)}, u32[]{:S(2)}) collective-permute-start(bf16[128,1024]{1,0:T(8,128)(2,1)S(1)} %pad_maximum_fusion.1.refs_0_), channel_id=1, source_target_pairs={{0,16},{4,20},{8,24},{12,28},{16,0},{20,4},{24,8},{28,12},{1,17},{... | collective-permute-start | bytes 786440 | tf_op jit(solution)/shard_map/ppermute | solution.py:99
  16.9 25.0 %collective-permute-start.5 = (bf16[128,1024]{1,0:T(8,128)(2,1)S(1)}, bf16[128,1024]{1,0:T(8,128)(2,1)}, u32[]{:S(2)}, u32[]{:S(2)}) collective-permute-start(bf16[128,1024]{1,0:T(8,128)(2,1)S(1)} %pad_maximum_fusion.1.refs_0_), channel_id=1, source_target_pairs={{0,24},{4,28},{8,16},{12,20},{16,8},{20,12},{24,0},{28,4},{1,25},{... | collective-permute-start | bytes 786440 | tf_op jit(solution)/shard_map/ppermute | solution.py:99
  18.2 23.7 %collective-permute-start.6 = (bf16[128,1024]{1,0:T(8,128)(2,1)S(1)}, bf16[128,1024]{1,0:T(8,128)(2,1)S(1)}, u32[]{:S(2)}, u32[]{:S(2)}) collective-permute-start(bf16[128,1024]{1,0:T(8,128)(2,1)S(1)} %pad_maximum_fusion.1.refs_0_), channel_id=1, source_target_pairs={{0,8},{4,12},{8,0},{12,4},{16,24},{20,28},{24,16},{28,20},{1,9},{5... | collective-permute-start | bytes 786440 | tf_op jit(solution)/shard_map/ppermute | solution.py:99
  44.1 21.5 %collective-permute-start = (bf16[512,1024]{1,0:T(8,128)(2,1)S(1)}, bf16[512,1024]{1,0:T(8,128)(2,1)S(1)}, u32[]{:S(2)}, u32[]{:S(2)}) collective-permute-start(bf16[512,1024]{1,0:T(8,128)(2,1)S(1)} %copy-done), channel_id=1, source_target_pairs={{0,1},{1,0},{2,3},{3,2},{4,5},{5,4},{6,7},{7,6},{8,9},{9,8},{10,11... | collective-permute-start | bytes 3145736 | tf_op jit(solution)/shard_map/ppermute | solution.py:31
  63.4 45.0 %collective-permute-start.10 = (bf16[1024,256]{1,0:T(8,128)(2,1)}, bf16[1024,256]{1,0:T(8,128)(2,1)}, u32[]{:S(2)}, u32[]{:S(2)}) collective-permute-start(bf16[1024,256]{1,0:T(8,128)(2,1)} %get-tuple-element.184.refs_4_.refs_11_), channel_id=1, source_target_pairs={{0,1},{1,0},{2,3},{3,2},{4,5},{5,4},{6,7},{7,6},{8,9},{9,8},{10,11... | collective-permute-start | bytes 1572872 | tf_op jit(solution)/shard_map/ppermute | solution.py:31
  63.9 44.5 %collective-permute-start.11 = (bf16[1024,256]{1,0:T(8,128)(2,1)}, bf16[1024,256]{1,0:T(8,128)(2,1)}, u32[]{:S(2)}, u32[]{:S(2)}) collective-permute-start(bf16[1024,256]{1,0:T(8,128)(2,1)} %get-tuple-element.184.refs_4_.refs_11_), channel_id=1, source_target_pairs={{0,2},{1,3},{2,0},{3,1},{4,6},{5,7},{6,4},{7,5},{8,10},{9,11},{10,... | collective-permute-start | bytes 1572872 | tf_op jit(solution)/shard_map/ppermute | solution.py:31
  65.4 301.6 %reduce-scatter.5.cloned.1.call-start = ((), (), s32[]{:S(2)}) async-start(), calls=%async_computation.9 | async-start | bytes 2359296 | tf_op jit(solution)/shard_map/reduce_scatter | solution.py:1111
  74.4 34.0 %collective-permute-start.12 = (bf16[512,1024]{1,0:T(8,128)(2,1)}, bf16[512,1024]{1,0:T(8,128)(2,1)}, u32[]{:S(2)}, u32[]{:S(2)}) collective-permute-start(bf16[512,1024]{1,0:T(8,128)(2,1)} %refs_4_.1), channel_id=1, source_target_pairs={{0,2},{1,3},{2,0},{3,1},{4,6},{5,7},{6,4},{7,5},{8,10},{9,11},{10,... | collective-permute-start | bytes 3145736 | tf_op jit(solution)/shard_map/ppermute | solution.py:31
  129.0 30.2 %collective-permute-start.17 = (bf16[512,1024]{1,0:T(8,128)(2,1)}, bf16[512,1024]{1,0:T(8,128)(2,1)S(1)}, u32[]{:S(2)}, u32[]{:S(2)}) collective-permute-start(bf16[512,1024]{1,0:T(8,128)(2,1)} %get-tuple-element.187.refs_0_), channel_id=1, source_target_pairs={{0,2},{1,3},{2,0},{3,1},{4,6},{5,7},{6,4},{7,5},{8,10},{9,11},{10,... | collective-permute-start | bytes 3145736 | tf_op jit(solution)/shard_map/ppermute | solution.py:31
  192.2 25.4 %collective-permute-start.26 = (bf16[512,1024]{1,0:T(8,128)(2,1)S(1)}, bf16[512,1024]{1,0:T(8,128)(2,1)}, u32[]{:S(2)}, u32[]{:S(2)}) collective-permute-start(bf16[512,1024]{1,0:T(8,128)(2,1)S(1)} %add_convert_fusion.3), channel_id=1, source_target_pairs={{0,2},{1,3},{2,0},{3,1},{4,6},{5,7},{6,4},{7,5},{8,10},{9,11},{10,... | collective-permute-start | bytes 3145736 | tf_op jit(solution)/shard_map/ppermute | solution.py:31
  214.7 156.1 %reduce-scatter.3.cloned.1.call-start = ((), (), s32[]{:S(2)}) async-start(), calls=%async_computation.8 | async-start | bytes 2359296 | tf_op jit(solution)/shard_map/reduce_scatter | solution.py:1111
  226.5 24.6 %collective-permute-start.27 = (bf16[512,256]{1,0:T(8,128)(2,1)}, bf16[512,256]{1,0:T(8,128)(2,1)S(1)}, u32[]{:S(2)}, u32[]{:S(2)}) collective-permute-start(bf16[512,256]{1,0:T(8,128)(2,1)} %get-tuple-element.216), channel_id=1, source_target_pairs={{0,1},{1,0},{2,3},{3,2},{4,5},{5,4},{6,7},{7,6},{8,9},{9,8},{10,11... | collective-permute-start | bytes 786440 | tf_op jit(solution)/shard_map/ppermute | solution.py:31
  226.6 24.8 %collective-permute-start.28 = (bf16[512,256]{1,0:T(8,128)(2,1)}, bf16[512,256]{1,0:T(8,128)(2,1)S(1)}, u32[]{:S(2)}, u32[]{:S(2)}) collective-permute-start(bf16[512,256]{1,0:T(8,128)(2,1)} %get-tuple-element.217), channel_id=1, source_target_pairs={{0,2},{1,3},{2,0},{3,1},{4,6},{5,7},{6,4},{7,5},{8,10},{9,11},{10,... | collective-permute-start | bytes 786440 | tf_op jit(solution)/shard_map/ppermute | solution.py:31
  228.1 23.3 %collective-permute-start.29 = (bf16[512,256]{1,0:T(8,128)(2,1)}, bf16[512,256]{1,0:T(8,128)(2,1)}, u32[]{:S(2)}, u32[]{:S(2)}) collective-permute-start(bf16[512,256]{1,0:T(8,128)(2,1)} %get-tuple-element.218), channel_id=1, source_target_pairs={{0,3},{1,2},{2,1},{3,0},{4,7},{5,6},{6,5},{7,4},{8,11},{9,10},{10,... | collective-permute-start | bytes 786440 | tf_op jit(solution)/shard_map/ppermute | solution.py:31
  251.1 40.6 %collective-permute-start.34 = (bf16[1024,256]{1,0:T(8,128)(2,1)}, bf16[1024,256]{1,0:T(8,128)(2,1)S(1)}, u32[]{:S(2)}, u32[]{:S(2)}) collective-permute-start(bf16[1024,256]{1,0:T(8,128)(2,1)} %get-tuple-element.226), channel_id=1, source_target_pairs={{0,1},{1,0},{2,3},{3,2},{4,5},{5,4},{6,7},{7,6},{8,9},{9,8},{10,11... | collective-permute-start | bytes 1572872 | tf_op jit(solution)/shard_map/ppermute | solution.py:31
  253.9 37.8 %collective-permute-start.32 = (bf16[512,1024]{1,0:T(8,128)(2,1)S(1)}, bf16[512,1024]{1,0:T(8,128)(2,1)}, u32[]{:S(2)}, u32[]{:S(2)}) collective-permute-start(bf16[512,1024]{1,0:T(8,128)(2,1)S(1)} %add_convert_fusion.2), channel_id=1, source_target_pairs={{0,2},{1,3},{2,0},{3,1},{4,6},{5,7},{6,4},{7,5},{8,10},{9,11},{10,... | collective-permute-start | bytes 3145736 | tf_op jit(solution)/shard_map/ppermute | solution.py:31
  255.3 36.4 %collective-permute-start.33 = (bf16[1024,256]{1,0:T(8,128)(2,1)S(1)}, bf16[1024,256]{1,0:T(8,128)(2,1)S(1)}, u32[]{:S(2)}, u32[]{:S(2)}) collective-permute-start(bf16[1024,256]{1,0:T(8,128)(2,1)S(1)} %add_convert_fusion.4), channel_id=1, source_target_pairs={{0,2},{1,3},{2,0},{3,1},{4,6},{5,7},{6,4},{7,5},{8,10},{9,11},{10,... | collective-permute-start | bytes 1572872 | tf_op jit(solution)/shard_map/ppermute | solution.py:31
  256.7 34.4 %all-to-all-start.1 = ((f32[32,1,384]{2,1,0:T(1,128)}), f32[32,1,384]{2,1,0:T(1,128)S(1)}, u32[]{:S(2)}, u32[]{:S(2)}) async-start(f32[32,1,384]{2,1,0:T(1,128)} %copy.143), calls=%async_computation.3 | async-start | bytes 98304 | tf_op jit(solution)/shard_map/all_to_all | solution.py:94
  299.9 44.3 %all-to-all-start.2 = ((bf16[8,144,640]{2,1,0:T(8,128)(2,1)}), bf16[8,144,640]{2,1,0:T(8,128)(2,1)}, u32[]{:S(2)}, u32[]{:S(2)}) async-start(bf16[8,144,640]{2,1,0:T(8,128)(2,1)} %attend_rows.3), calls=%async_computation.4 | async-start | bytes 2949120 | tf_op jit(solution)/shard_map/all_to_all | solution.py:152
  352.0 48.8 %collective-permute-start.40 = (bf16[512,1024]{1,0:T(8,128)(2,1)}, bf16[512,1024]{1,0:T(8,128)(2,1)}, u32[]{:S(2)}, u32[]{:S(2)}) collective-permute-start(bf16[512,1024]{1,0:T(8,128)(2,1)} %get-tuple-element.221), channel_id=1, source_target_pairs={{0,1},{1,0},{2,3},{3,2},{4,5},{5,4},{6,7},{7,6},{8,9},{9,8},{10,11... | collective-permute-start | bytes 3145736 | tf_op jit(solution)/shard_map/ppermute | solution.py:31
  352.4 31.7 %all-to-all-start.3 = ((bf16[8,144,384]{2,1,0:T(8,128)(2,1)}), bf16[8,144,384]{2,1,0:T(8,128)(2,1)S(1)}, u32[]{:S(2)}, u32[]{:S(2)}) async-start(bf16[8,144,384]{2,1,0:T(8,128)(2,1)} %attend_rows.2), calls=%async_computation.5 | async-start | bytes 1769472 | tf_op jit(solution)/shard_map/all_to_all | solution.py:152
  360.2 45.0 %collective-permute-start.39 = (bf16[512,1024]{1,0:T(8,128)(2,1)}, bf16[512,1024]{1,0:T(8,128)(2,1)}, u32[]{:S(2)}, u32[]{:S(2)}) collective-permute-start(bf16[512,1024]{1,0:T(8,128)(2,1)} %add_convert_fusion.1), channel_id=1, source_target_pairs={{0,2},{1,3},{2,0},{3,1},{4,6},{5,7},{6,4},{7,5},{8,10},{9,11},{10,... | collective-permute-start | bytes 3145736 | tf_op jit(solution)/shard_map/ppermute | solution.py:31
  (69 other events, 947.5 us)
Sparse Core Ops, SparseCore 0:
  65.5 73.5 all-gather.1
  214.8 64.8 reduce-scatter.4
  283.3 87.4 reduce-scatter.2

commit v3 on v2

--- a/solution.py
+++ b/solution.py
@@ -523,27 +523,35 @@
     )
 
 
+NARROW_ROWS = 64
+NARROW_COLUMNS = 256
+
+
 def narrow_back(part, act, slope, unit_in, totals, gains, weights, kept=None):
     length, units = act.shape
 
     def kernel(act_ref, slope_ref, in_ref, total_ref, gain_ref, work_ref, low_ref, wide_ref, sum_ref, *outs):
         first, second, third, fourth = as_columns(total_ref[...])
         mean, factor = moments(first, second, FF)
-        normed = (act_ref[...] - mean) * factor
-        low_ref[...] = (normed * gain_ref[0:1] + gain_ref[1:2]).astype(BF)
-        grad = in_ref[...].astype(F32)
         inner = factor * (fourth - mean * third)
-        back = factor * (grad * gain_ref[0:1] - third / FF - normed * (inner / FF))
-        wide = (back * slope_ref[...].astype(F32)).astype(BF)
-        wide_ref[...] = wide
 
         @pl.when(pl.program_id(0) == 0)
         def _():
             sum_ref[...] = jnp.zeros_like(sum_ref)
 
-        sum_ref[0:8] += fold(grad * normed)
-        sum_ref[8:16] += fold(grad)
-        part.store(outs, dot(wide, work_ref[...], 1, 1).astype(BF))
+        for start in range(0, part.step, NARROW_ROWS):
+            rows = slice(start, start + NARROW_ROWS)
+            for left in range(0, units, NARROW_COLUMNS):
+                columns = slice(left, left + NARROW_COLUMNS)
+                gain, bias = gain_ref[0:1, columns], gain_ref[1:2, columns]
+                normed = (act_ref[rows, columns] - mean[rows]) * factor[rows]
+                low_ref[rows, columns] = (normed * gain + bias).astype(BF)
+                grad = in_ref[rows, columns].astype(F32)
+                back = factor[rows] * (grad * gain - third[rows] / FF - normed * (inner[rows] / FF))
+                wide_ref[rows, columns] = (back * slope_ref[rows, columns].astype(F32)).astype(BF)
+                sum_ref[0:8, columns] += fold(grad * normed)
+                sum_ref[8:16, columns] += fold(grad)
+        part.store(outs, dot(wide_ref[...], work_ref[...], 1, 1).astype(BF))
 
     return call(
         kernel,
@@ -650,7 +658,7 @@
         cost_estimate=about(5),
         compiler_params=pltpu.CompilerParams(vmem_limit_bytes=50 << 20),
         name="attend_rows",
-    )(normed_all, back, *extra)
+    )(normed_all, in_hbm(back), *extra)
 
 
 def attend_rows_narrow(normed_all, back, extra):
@@ -752,23 +760,29 @@
         columns = lax.broadcasted_iota(jnp.int32, (1, length), 1)
         allowed = segments_at(rows, table_ref, count) == segments_at(columns, table_ref, count)
         lane = lax.broadcasted_iota(jnp.int32, (1, LANES), 1) // HD
-        for p in range(pairs):
+        def scores_of(p, h):
             query = refs[3 * p][...] * BF(HD**-0.5)
-            keys = refs[3 * p + 1][...]
+            one = jnp.where(lane == h, query, jnp.zeros_like(query))
+            return jnp.where(allowed, dot(one, refs[3 * p + 1][...], 1, 1), MASKED)
+
+        heads = [(p, h) for p in range(pairs) for h in range(PAIR)]
+        following = scores_of(*heads[0])
+        for k, (p, h) in enumerate(heads):
+            scores = following
+            if h == 0:
+                out, logs = jnp.zeros((block, LANES), F32), []
+            highest = jnp.max(scores, axis=1, keepdims=True)
+            if k + 1 < len(heads):
+                following = scores_of(*heads[k + 1])
+            weights = jnp.exp(scores - highest).astype(BF)
             values = refs[3 * p + 2][...]
-            out = jnp.zeros((block, LANES), F32)
-            logs = []
-            for h in range(PAIR):
-                one = jnp.where(lane == h, query, jnp.zeros_like(query))
-                scores = jnp.where(allowed, dot(one, keys, 1, 1), MASKED)
-                highest = jnp.max(scores, axis=1, keepdims=True)
-                weights = jnp.exp(scores - highest)
-                total = jnp.sum(weights, axis=1, keepdims=True)
-                mixed = dot(weights.astype(BF), values, 1, 0)
-                out = jnp.where(lane == h, mixed * (1.0 / total), out)
-                logs.append(highest + jnp.log(total))
-            low[:, p * LANES : (p + 1) * LANES] = out.astype(BF)
-            log_ref[8 * p : 8 * p + 8, :] = as_rows(logs, 8)
+            mixed = dot(weights, jnp.where(lane == h, values, jnp.ones_like(values)), 1, 0)
+            total = pltpu.roll(mixed, HD, axis=1)
+            out = jnp.where(lane == h, mixed / total, out)
+            logs.append(highest + jnp.log(total[:, h * HD : h * HD + 1]))
+            if h == PAIR - 1:
+                low[:, p * LANES : (p + 1) * LANES] = out.astype(BF)
+                log_ref[8 * p : 8 * p + 8, :] = as_rows(logs, 8)
         part.store(outs, low[...])
 
     specs = []
@@ -790,7 +804,7 @@
         cost_estimate=about(16 * pairs, 4.0),
         compiler_params=pltpu.CompilerParams(vmem_limit_bytes=48 << 20),
         name="attention_forward",
-    )(table, *[projected] * (3 * pairs))
+    )(table, *[in_hbm(projected)] * (3 * pairs))
     return outs, logs
 
 
@@ -839,13 +853,14 @@
         score_back = (probs * (probs_back - dots[h : h + 1, :])).astype(BF)
         value_back = jnp.where(lane == h, dot(probs.astype(BF), grad, 1, 0), value_back)
         key_back = jnp.where(lane == h, dot(score_back, query, 1, 0), key_back)
-        sums[...] += dot(score_back, key, 0, 0)
+        turned = jnp.transpose(keys)[h * HD : (h + 1) * HD]
+        sums[h * HD : (h + 1) * HD, :] += dot(turned, score_back, 1, 0)
     out[pl.ds(start, block), LANES : 2 * LANES] = key_back.astype(BF)
     out[pl.ds(start, block), 2 * LANES :] = value_back.astype(BF)
 
     @pl.when(step == pl.num_programs(0) - 1)
     def _():
-        out[:, :LANES] = (sums[...] * HD**-0.5).astype(BF)
+        out[:, :LANES] = (jnp.transpose(sums[...]) * HD**-0.5).astype(BF)
 
 
 def attention_backward(pair, projected, table, grads, attended, logs):
@@ -869,7 +884,7 @@
             + [fixed((value.shape[0], LANES), 0, pair) for value in (*grads, *attended)],
             out_specs=fixed((length, 3 * LANES)),
             scratch_shapes=[
-                pltpu.VMEM((length, LANES), F32),
+                pltpu.VMEM((LANES, length), F32),
                 pltpu.VMEM((8, length), F32),
                 pltpu.VMEM((length, LANES), BF),
             ],
@@ -927,8 +942,10 @@
 
 def adamw(scales, attend_parts, others, params, firsts, squares):
     shard = params[0].shape[1]
-    steps = params[3].shape[0] // LANES
-    turned = params[1].shape[0] // LANES
+    block = 2 * LANES
+    mix_block = min(block, params[1].shape[0])
+    steps = params[3].shape[0] // block
+    turned = params[1].shape[0] // mix_block
     rows = shard // steps
 
     def last(i):
@@ -936,16 +953,16 @@
 
     state = [
         pl.BlockSpec((3, rows, params[0].shape[2]), lambda i: (0, i, 0)),
-        pl.BlockSpec((LANES, shard), lambda i: (last(i), 0)),
+        pl.BlockSpec((mix_block, shard), lambda i: (last(i), 0)),
         pl.BlockSpec((rows, params[2].shape[1]), lambda i: (i, 0)),
-        pl.BlockSpec((LANES, shard), lambda i: (i, 0)),
+        pl.BlockSpec((block, shard), lambda i: (i, 0)),
     ] + [pl.BlockSpec(value.shape, lambda i: (0, 0)) for value in params[4:]]
     grad_specs = (
         [pl.BlockSpec((rows, 3 * LANES), lambda i: (i, 0)) for _ in attend_parts]
         + [
-            pl.BlockSpec((shard, LANES), lambda i: (0, last(i))),
+            pl.BlockSpec((shard, mix_block), lambda i: (0, last(i))),
             state[2],
-            pl.BlockSpec((shard, LANES), lambda i: (0, i)),
+            pl.BlockSpec((shard, block), lambda i: (0, i)),
         ]
         + state[4:]
     )
@@ -1014,12 +1031,11 @@
     tables = exchange_all(jnp.broadcast_to(packed[None], (device_count, packed.shape[0])))
 
     token_near, token_even = gather_near(tokens)
-    work_odd = cross_groups(work_even, [*token_even, tables])
+    wide_shard = jnp.concatenate([expand.astype(BF), contract.astype(BF).T], axis=1)
+    work_odd = cross_groups(work_even, [*token_even, tables, wide_shard])
     token_far = gather_far(after(token_even, work_odd))
     work_in, work_mix = place_groups(work_even, work_odd, [3 * head_width, head_width])
-    wide_shard = after(
-        [jnp.concatenate([expand.astype(BF), contract.astype(BF).T], axis=1)], [work_in]
-    )[0]
+    wide_shard = after([wide_shard], [*work_even[1:], tables])[0]
     weights = lax.all_gather(wide_shard, "dp", axis=0, tiled=True)
 
     def unpack(k, rows):
@@ -1105,7 +1121,7 @@
         backs.append(attention_backward(pair, projected, table, grad_blocks, attended, logs))
         value = after([attend_rows(normed_all, backs[-1])], pieces)[0]
         pieces.append(exchange_groups(value))
-        late = after(backs, [value])
+        late = [in_hbm(back) for back in after(backs, [value])]
 
     def scatter(value):
         return lax.psum_scatter(value, "dp", scatter_dimension=0, tiled=True)

time: 433 us -> 424 us (0.979)
  waiting for transfers between devices: 58.1 us -> 80 us
  blocking collectives: 19.4 us -> 0 us
  Pallas kernels: 235 us -> 226 us
    all_to_all x1 -> x0, blocking collectives: 19.4 us -> none  [exchange_all(): return lax.all_to_all(value, ALL, 0, 0, tiled=True)]
    all_to_all x2 -> x3, waiting for transfers between devices: 2.33 us -> 16.7 us  [exchange_all(): return lax.all_to_all(value, ALL, 0, 0, tiled=True)]
    unnamed x96 -> x88, local copies, waits for them, and re-layouts: 12.7 us -> 8.29 us
    all_to_all x2 -> x3, starting transfers between devices: 6.48 us -> 10.4 us  [exchange_all(): return lax.all_to_all(value, ALL, 0, 0, tiled=True)]
  transfers between devices with their start and end apart: 48 -> 49, of which waited for: 17 -> 18; matrix products, arithmetic and copies ran while one was open for 8% -> 8% of each run, Pallas kernels for 48% -> 47%
where the time goes in v3:
time: 424 us; the launch traced here: 420 us
  Pallas kernels  226 us (53%)
  waiting for transfers between devices  80 us (19%)
  starting transfers between devices  50.5 us (12%)
  other arithmetic  27.5 us (6%)
  between operations  21.8 us (5%)
  local copies, waits for them, and re-layouts  14.3 us (3%)
    pallas_call x9, Pallas kernels, call(): pl.pallas_call(body, grid_spec=pltpu.PrefetchScalarGridSpec(num_scalar_pr...  79 us
    pallas_call x2, Pallas kernels, attention_backward(): pl.pallas_call(partial(backward_kernel, block=block, count=table.shape[0]...  55.2 us
    pallas_call x1, Pallas kernels, attention_forward(): pl.pallas_call(kernel, grid_spec=pltpu.PrefetchScalarGridSpec(num_scalar_...  28.2 us
    ppermute x34, waiting for transfers between devices, swap(): return lax.ppermute(value, 'mp', [(i, i ^ bit) for i in range(count)])  25.6 us
    ppermute x34, starting transfers between devices, swap(): return lax.ppermute(value, 'mp', [(i, i ^ bit) for i in range(count)])  22.5 us
    pallas_call x2, Pallas kernels, weight_grad(): pl.pallas_call(kernel, grid=(left.shape[1] // block,), in_specs=[pl.Block...  17.4 us
    all_to_all x3, waiting for transfers between devices, exchange_all(): return lax.all_to_all(value, ALL, 0, 0, tiled=True)  16.7 us
    pallas_call x2, Pallas kernels, attend_rows(): pl.pallas_call(kernel, grid=(groups,), in_specs=[pl.BlockSpec((length, D)...  16.4 us
  transfers between devices with their start and end apart: 49, of which 18 were waited for; matrix products, arithmetic and copies ran while one was open for 8% of the time, Pallas kernels for 47%

profile of v3, /device:TPU:0, one launch (start us, length us, event | category | flops | bytes accessed | tf_op | source)
XLA Modules:
  0.0 419.8 jit_solution(11494182035905212033)
XLA Ops:
  29.0 12.9 %all-to-all-done = f32[32,1,448]{2,1,0:T(1,128)S(1)} async-done(((f32[32,1,448]{2,1,0:T(1,128)}), f32[32,1,448]{2,1,0:T(1,128)S(1)}, u32[]{:S(2)}, u32[]{:S(2)}) %all-to-all-start) | async-done | bytes 57376 | tf_op jit(solution)/shard_map/all_to_all | solution.py:94
  44.0 7.3 %collective-permute-done.7.refs_5_ = bf16[128,1024]{1,0:T(8,128)(2,1)S(1)} collective-permute-done((bf16[128,1024]{1,0:T(8,128)(2,1)}, bf16[128,1024]{1,0:T(8,128)(2,1)S(1)}, u32[]{:S(2)}, u32[]{:S(2)}) %collective-permute-start.7) | collective-permute-done | bytes 262176 | tf_op jit(solution)/shard_map/ppermute | solution.py:99
  64.3 9.0 %project.1 = (bf16[2048,1024]{1,0:T(8,128)(2,1)}, bf16[2048,768]{1,0:T(8,128)(2,1)}) custom-call(bf16[512,1024]{1,0:T(8,128)(2,1)S(1)} %copy-done, bf16[512,1024]{1,0:T(8,128)(2,1)S(1)} %collective-permute-done.refs_1_, bf16[512,1024]{1,0:T(8,128)(2,1)S(1)} %collective-permute-done.1.refs_2_, bf16[512,1024]{1,0:T(8,128)(2,1)} %collective-permute-done.9.refs_3_, ...), custom_call_target="tpu_custom_call" | custom-call | flops 36800000000 | bytes 3200000 | tf_op jit(solution)/shard_map/project/pallas_call | solution.py:281
  73.9 28.2 %attention_forward.1 = (bf16[512,256]{1,0:T(8,128)(2,1)S(1)}, bf16[512,256]{1,0:T(8,128)(2,1)S(1)}, bf16[512,256]{1,0:T(8,128)(2,1)S(1)}, bf16[512,256]{1,0:T(8,128)(2,1)S(1)}, f32[16,2048]{1,0:T(8,128)S(1)}) custom-call(s32[6]{0:T(128)S(1)} %pad_add_fusion.table_ref.refs_0_, ...), custom_call_target="tpu_custom_call" | custom-call | flops 147200000000 | bytes 12800000 | tf_op jit(solution)/shard_map/attention_forward/pallas_call | solution.py:793
  106.1 6.6 %collective-permute-done.14.refs_2_.refs_9_ = bf16[512,256]{1,0:T(8,128)(2,1)} collective-permute-done((bf16[512,256]{1,0:T(8,128)(2,1)S(1)}, bf16[512,256]{1,0:T(8,128)(2,1)}, u32[]{:S(2)}, u32[]{:S(2)}) %collective-permute-start.14) | collective-permute-done | bytes 262176 | tf_op jit(solution)/shard_map/ppermute | solution.py:31
  117.5 5.8 %mix_rows.1 = (f32[512,1024]{1,0:T(8,128)}, bf16[512,1024]{1,0:T(8,128)(2,1)}, bf16[512,1024]{1,0:T(8,128)(2,1)}) custom-call(s32[6]{0:T(128)S(1)} %pad_add_fusion.table_ref.refs_0_, bf16[512,256]{1,0:T(8,128)(2,1)S(1)} %copy-done.18, bf16[512,256]{1,0:T(8,128)(2,1)S(1)} %collective-permute-done.13.refs_1_.refs_8_, ...), custom_call_target="tpu_custom_call" | custom-call | flops 27599998976 | bytes 2400000 | tf_op jit(solution)/shard_map/mix_rows/pallas_call | solution.py:337
  125.6 8.4 %all-gather.2.cloned.1.call-done.refs_5_.refs_2_.refs_1_ = bf16[1024,2048]{1,0:T(8,128)(2,1)} async-done(((bf16[128,2048]{1,0:T(8,128)(2,1)}), bf16[1024,2048]{1,0:T(8,128)(2,1)}) %all-gather.2.cloned.1.call-update) | async-done | bytes 4194320 | tf_op jit(solution)/shard_map/all_gather | solution.py:1039
  134.1 9.8 %feed_back.1 = (bf16[2048,1024]{1,0:T(8,128)(2,1)}, bf16[2048,1024]{1,0:T(8,128)(2,1)}) custom-call(s32[6]{0:T(128)S(1)} %pad_add_fusion.table_ref.refs_0_, bf16[512,1024]{1,0:T(8,128)(2,1)} %refs_4_.1, bf16[512,1024]{1,0:T(8,128)(2,1)S(1)} %collective-permute-done.19.refs_2_, bf16[512,1024]{1,0:T(8,128)(2,1)} %collective-permute-done.12.refs_3_, ...), custom_call_target="tpu_custom_call" | custom-call | flops 36800000000 | bytes 3200000 | tf_op jit(solution)/shard_map/feed_back/pallas_call | solution.py:281
  145.1 9.2 %widen.2 = (bf16[2048,1024]{1,0:T(8,128)(2,1)}, f32[2048,1024]{1,0:T(8,128)}, bf16[2048,1024]{1,0:T(8,128)(2,1)}, f32[4,2048]{1,0:T(4,128)S(1)}) custom-call(bf16[512,1024]{1,0:T(8,128)(2,1)S(1)} %copy-done.7, bf16[512,1024]{1,0:T(8,128)(2,1)} %collective-permute-done.18.refs_1_, bf16[1024,2048]{1,0:T(8,128)(2,1)} %all-gather.2.cloned.1.call-done.refs_5_.refs_2_.refs_1_, ...), custom_call_target="tpu_custom_call" | custom-call | flops 18400000000 | bytes 1600000 | tf_op jit(solution)/shard_map/widen/pallas_call | solution.py:281
  157.0 8.6 %widen.3 = (bf16[2048,1024]{1,0:T(8,128)(2,1)}, f32[2048,1024]{1,0:T(8,128)}, bf16[2048,1024]{1,0:T(8,128)(2,1)}, f32[4,2048]{1,0:T(4,128)S(1)}) custom-call(bf16[512,1024]{1,0:T(8,128)(2,1)S(1)} %collective-permute-done.17.refs_0_, ...), custom_call_target="tpu_custom_call", output_to_operand_aliasing={{0}: (5, {}), {1}: (6, {}), {2}: (7, {}), {3}: (8, {})} | custom-call | flops 18400000000 | bytes 1600000 | tf_op jit(solution)/shard_map/widen/pallas_call | solution.py:281
  170.8 11.1 %narrow_back.2 = (bf16[2048,1024]{1,0:T(8,128)(2,1)}, bf16[2048,1024]{1,0:T(8,128)(2,1)}, f32[16,1024]{1,0:T(8,128)S(1)}, bf16[512,1024]{1,0:T(8,128)(2,1)}, bf16[512,1024]{1,0:T(8,128)(2,1)}) custom-call(f32[2048,1024]{1,0:T(8,128)} %get-tuple-element.197.refs_0_, bf16[2048,1024]{1,0:T(8,128)(2,1)} %get-tuple-element.202.refs_1_, ...), custom_call_target="tpu_custom_call" | custom-call | flops 18400000000 | bytes 1600000 | tf_op jit(solution)/shard_map/narrow_back/pallas_call | solution.py:281
  187.9 11.1 %narrow_back.3 = (bf16[2048,1024]{1,0:T(8,128)(2,1)}, bf16[2048,1024]{1,0:T(8,128)(2,1)}, f32[16,1024]{1,0:T(8,128)S(1)}, bf16[512,1024]{1,0:T(8,128)(2,1)}, bf16[512,1024]{1,0:T(8,128)(2,1)}) custom-call(f32[2048,1024]{1,0:T(8,128)} %get-tuple-element.197.refs_0_, ...), custom_call_target="tpu_custom_call", output_to_operand_aliasing={{0}: (6, {}), {1}: (7, {})} | custom-call | flops 18400000000 | bytes 1600000 | tf_op jit(solution)/shard_map/narrow_back/pallas_call | solution.py:281
  199.0 8.6 %weight_grad.2 = bf16[1024,1024]{1,0:T(8,128)(2,1)} custom-call(bf16[2048,1024]{1,0:T(8,128)(2,1)} %get-tuple-element.208.left_ref, bf16[2048,1024]{1,0:T(8,128)(2,1)} %get-tuple-element.219.right_ref.refs_0_), custom_call_target="tpu_custom_call" | custom-call | flops 36800000000 | bytes 3200000 | tf_op jit(solution)/shard_map/weight_grad/pallas_call | solution.py:577
  211.8 8.9 %mix_rows_back.1 = (f32[512,1024]{1,0:T(8,128)}, bf16[512,1024]{1,0:T(8,128)(2,1)}, f32[16,1024]{1,0:T(8,128)S(1)}, f32[16,1024]{1,0:T(8,128)S(1)}, bf16[512,256...) custom-call(s32[6]{0:T(128)S(1)} %pad_add_fusion.table_ref.refs_0_, ...), custom_call_target="tpu_custom_call" | custom-call | flops 36800000000 | bytes 3200000 | tf_op jit(solution)/shard_map/mix_rows_back/pallas_call | solution.py:337
  222.7 9.7 %feed_rows.1 = (bf16[512,1024]{1,0:T(8,128)(2,1)}, bf16[512,1024]{1,0:T(8,128)(2,1)}, bf16[512,1024]{1,0:T(8,128)(2,1)}, bf16[512,1024]{1,0:T(8,128)(2,1)}) custom-call(bf16[2048,1024]{1,0:T(8,128)(2,1)} %get-tuple-element.219.right_ref.refs_0_, bf16[1024,2048]{1,0:T(8,128)(2,1)} %all-gather.2.cloned.1.call-done.refs_5_.refs_2_.refs_1_), custom_call_target="tpu_custom_call" | custom-call | flops 36800000000 | bytes 3200000 | tf_op jit(solution)/shard_map/feed_rows/pallas_call | solution.py:281
  236.0 8.7 %weight_grad.3 = bf16[1024,1024]{1,0:T(8,128)(2,1)} custom-call(bf16[2048,1024]{1,0:T(8,128)(2,1)} %get-tuple-element.196.left_ref, bf16[2048,1024]{1,0:T(8,128)(2,1)} %get-tuple-element.213.right_ref), custom_call_target="tpu_custom_call" | custom-call | flops 36800000000 | bytes 3200000 | tf_op jit(solution)/shard_map/weight_grad/pallas_call | solution.py:577
  253.8 27.7 %attention_backward.2.back_ref.refs_0_ = bf16[2048,384]{1,0:T(8,128)(2,1)} custom-call(s32[6]{0:T(128)} %copy-done.6, bf16[2048,768]{1,0:T(8,128)(2,1)} %get-tuple-element.171.refs_0_.refs_1_.refs_2_.refs_3_.refs_4_.refs_5_.q_ref.k_ref.v_ref, bf16[2048,768]{1,0:T(8,128)(2,1)} %get-tuple-element.171.refs_0_.refs_1_.refs_2_.refs_3_.refs_4_.refs_5_.q_ref.k_ref.v_ref, ...), custom_call_target="tpu_custom_call" | custom-call | flops 138000007168 | bytes 12000000 | tf_op jit(solution)/shard_map/attention_backward/pallas_call | solution.py:873
  285.9 8.2 %attend_rows.3 = bf16[8,144,640]{2,1,0:T(8,128)(2,1)} custom-call(bf16[2048,1024]{1,0:T(8,128)(2,1)} %get-tuple-element.178.normed_ref, bf16[2048,384]{1,0:T(8,128)(2,1)} %attention_backward.2.back_ref.refs_0_, bf16[1024,256]{1,0:T(8,128)(2,1)S(1)} %copy-done.16, bf16[1024,256]{1,0:T(8,128)(2,1)S(1)} %collective-permute-done.34.refs_1_, ...), custom_call_target="tpu_custom_call" | custom-call | flops 23000000512 | bytes 2000000 | tf_op jit(solution)/shard_map/attend_rows/pallas_call | solution.py:647
  298.7 27.6 %attention_backward.3.back_ref.refs_1_ = bf16[2048,384]{1,0:T(8,128)(2,1)} custom-call(s32[6]{0:T(128)} %copy-done.6, bf16[2048,768]{1,0:T(8,128)(2,1)} %get-tuple-element.171.refs_0_.refs_1_.refs_2_.refs_3_.refs_4_.refs_5_.q_ref.k_ref.v_ref, bf16[2048,768]{1,0:T(8,128)(2,1)} %get-tuple-element.171.refs_0_.refs_1_.refs_2_.refs_3_.refs_4_.refs_5_.q_ref.k_ref.v_ref, ...), custom_call_target="tpu_custom_call" | custom-call | flops 138000007168 | bytes 12000000 | tf_op jit(solution)/shard_map/attention_backward/pallas_call | solution.py:873
  326.3 8.2 %attend_rows.2 = bf16[8,144,384]{2,1,0:T(8,128)(2,1)} custom-call(bf16[2048,1024]{1,0:T(8,128)(2,1)} %get-tuple-element.178.normed_ref, bf16[2048,384]{1,0:T(8,128)(2,1)} %attention_backward.3.back_ref.refs_1_), custom_call_target="tpu_custom_call" | custom-call | flops 23000000512 | bytes 2000000 | tf_op jit(solution)/shard_map/attend_rows/pallas_call | solution.py:647
  352.4 5.3 %input_back.3 = (bf16[512,1024]{1,0:T(8,128)(2,1)}, bf16[512,1024]{1,0:T(8,128)(2,1)}) custom-call(bf16[2048,384]{1,0:T(8,128)(2,1)} %attention_backward.2.back_ref.refs_0_, bf16[2048,384]{1,0:T(8,128)(2,1)} %attention_backward.3.back_ref.refs_1_, bf16[1024,768]{1,0:T(8,128)(2,1)S(1)} %copy-done.13), custom_call_target="tpu_custom_call" | custom-call | flops 18400000000 | bytes 1600000 | tf_op jit(solution)/shard_map/input_back/pallas_call | solution.py:281
  357.7 6.5 %reduce-scatter.3.cloned.1.call-done.refs_3_ = bf16[128,1024]{1,0:T(8,128)(2,1)} async-done(((bf16[1024,1024]{1,0:T(8,128)(2,1)}), bf16[128,1024]{1,0:T(8,128)(2,1)}) %reduce-scatter.3.cloned.1.call-update) | async-done | bytes 262160 | tf_op jit(solution)/shard_map/reduce_scatter | solution.py:1127
  370.5 5.9 %all-to-all-done.3.piece_ref = bf16[8,144,384]{2,1,0:T(8,128)(2,1)S(1)} async-done(((bf16[8,144,384]{2,1,0:T(8,128)(2,1)}), bf16[8,144,384]{2,1,0:T(8,128)(2,1)S(1)}, u32[]{:S(2)}, u32[]{:S(2)}) %all-to-all-start.3) | async-done | bytes 884768 | tf_op jit(solution)/shard_map/all_to_all | solution.py:152
  405.0 6.9 %adamw.1 = (f32[3,128,256]{2,1,0:T(8,128)}, f32[3,128,256]{2,1,0:T(8,128)}, f32[3,128,256]{2,1,0:T(8,128)}, f32[3,128,256]{2,1,0:T(8,128)}, f32[256,128]{1,0:T(8...) custom-call(f32[3]{0:T(128)S(1)} %pad_maximum_fusion.5.scale_ref, ...), custom_call_target="tpu_custom_call" | custom-call | flops 27599998976 | bytes 2400000 | tf_op jit(solution)/shard_map/adamw/pallas_call | solution.py:970
  (262 shorter events, 137.7 us)
Async XLA Ops:
  7.3 34.7 %collective-permute-start.1 = (bf16[512,1024]{1,0:T(8,128)(2,1)}, bf16[512,1024]{1,0:T(8,128)(2,1)S(1)}, u32[]{:S(2)}, u32[]{:S(2)}) collective-permute-start(bf16[512,1024]{1,0:T(8,128)(2,1)} %refs_9_.2), channel_id=1, source_target_pairs={{0,2},{1,3},{2,0},{3,1},{4,6},{5,7},{6,4},{7,5},{8,10},{9,11},{10,... | collective-permute-start | bytes 3145736 | tf_op jit(solution)/shard_map/ppermute | solution.py:31
  14.3 27.6 %collective-permute-start.4 = (bf16[128,1024]{1,0:T(8,128)(2,1)S(1)}, bf16[128,1024]{1,0:T(8,128)(2,1)}, u32[]{:S(2)}, u32[]{:S(2)}) collective-permute-start(bf16[128,1024]{1,0:T(8,128)(2,1)S(1)} %pad_maximum_fusion.1.refs_0_), channel_id=1, source_target_pairs={{0,16},{4,20},{8,24},{12,28},{16,0},{20,4},{24,8},{28,12},{1,17},{... | collective-permute-start | bytes 786440 | tf_op jit(solution)/shard_map/ppermute | solution.py:99
  16.9 25.0 %collective-permute-start.5 = (bf16[128,1024]{1,0:T(8,128)(2,1)S(1)}, bf16[128,1024]{1,0:T(8,128)(2,1)}, u32[]{:S(2)}, u32[]{:S(2)}) collective-permute-start(bf16[128,1024]{1,0:T(8,128)(2,1)S(1)} %pad_maximum_fusion.1.refs_0_), channel_id=1, source_target_pairs={{0,24},{4,28},{8,16},{12,20},{16,8},{20,12},{24,0},{28,4},{1,25},{... | collective-permute-start | bytes 786440 | tf_op jit(solution)/shard_map/ppermute | solution.py:99
  18.2 23.7 %collective-permute-start.6 = (bf16[128,1024]{1,0:T(8,128)(2,1)S(1)}, bf16[128,1024]{1,0:T(8,128)(2,1)}, u32[]{:S(2)}, u32[]{:S(2)}) collective-permute-start(bf16[128,1024]{1,0:T(8,128)(2,1)S(1)} %pad_maximum_fusion.1.refs_0_), channel_id=1, source_target_pairs={{0,8},{4,12},{8,0},{12,4},{16,24},{20,28},{24,16},{28,20},{1,9},{5... | collective-permute-start | bytes 786440 | tf_op jit(solution)/shard_map/ppermute | solution.py:99
  20.6 21.3 %collective-permute-start.3 = (bf16[128,1024]{1,0:T(8,128)(2,1)}, bf16[128,1024]{1,0:T(8,128)(2,1)}, u32[]{:S(2)}, u32[]{:S(2)}) collective-permute-start(bf16[128,1024]{1,0:T(8,128)(2,1)} %collective-permute-done.2.refs_1_), channel_id=1, source_target_pairs={{0,8},{4,12},{8,0},{12,4},{16,24},{20,28},{24,16},{28,20},{1,9},{5... | collective-permute-start | bytes 786440 | tf_op jit(solution)/shard_map/ppermute | solution.py:99
  26.9 107.2 %all-gather.2.cloned.1.call-start = ((), (), s32[]{:S(2)}) async-start(), calls=%async_computation.7 | async-start | bytes 4718592 | tf_op jit(solution)/shard_map/all_gather | solution.py:1039
  59.4 298.3 %reduce-scatter.5.cloned.1.call-start = ((), (), s32[]{:S(2)}) async-start(), calls=%async_computation.9 | async-start | bytes 2359296 | tf_op jit(solution)/shard_map/reduce_scatter | solution.py:1127
  62.4 40.4 %collective-permute-start.10 = (bf16[1024,256]{1,0:T(8,128)(2,1)}, bf16[1024,256]{1,0:T(8,128)(2,1)}, u32[]{:S(2)}, u32[]{:S(2)}) collective-permute-start(bf16[1024,256]{1,0:T(8,128)(2,1)} %get-tuple-element.184.refs_4_.refs_11_), channel_id=1, source_target_pairs={{0,1},{1,0},{2,3},{3,2},{4,5},{5,4},{6,7},{7,6},{8,9},{9,8},{10,11... | collective-permute-start | bytes 1572872 | tf_op jit(solution)/shard_map/ppermute | solution.py:31
  62.9 39.9 %collective-permute-start.11 = (bf16[1024,256]{1,0:T(8,128)(2,1)}, bf16[1024,256]{1,0:T(8,128)(2,1)}, u32[]{:S(2)}, u32[]{:S(2)}) collective-permute-start(bf16[1024,256]{1,0:T(8,128)(2,1)} %get-tuple-element.184.refs_4_.refs_11_), channel_id=1, source_target_pairs={{0,2},{1,3},{2,0},{3,1},{4,6},{5,7},{6,4},{7,5},{8,10},{9,11},{10,... | collective-permute-start | bytes 1572872 | tf_op jit(solution)/shard_map/ppermute | solution.py:31
  73.2 29.6 %collective-permute-start.12 = (bf16[512,1024]{1,0:T(8,128)(2,1)}, bf16[512,1024]{1,0:T(8,128)(2,1)}, u32[]{:S(2)}, u32[]{:S(2)}) collective-permute-start(bf16[512,1024]{1,0:T(8,128)(2,1)} %refs_4_.1), channel_id=1, source_target_pairs={{0,2},{1,3},{2,0},{3,1},{4,6},{5,7},{6,4},{7,5},{8,10},{9,11},{10,... | collective-permute-start | bytes 3145736 | tf_op jit(solution)/shard_map/ppermute | solution.py:31
  123.3 30.9 %collective-permute-start.17 = (bf16[512,1024]{1,0:T(8,128)(2,1)}, bf16[512,1024]{1,0:T(8,128)(2,1)S(1)}, u32[]{:S(2)}, u32[]{:S(2)}) collective-permute-start(bf16[512,1024]{1,0:T(8,128)(2,1)} %get-tuple-element.187.refs_0_), channel_id=1, source_target_pairs={{0,2},{1,3},{2,0},{3,1},{4,6},{5,7},{6,4},{7,5},{8,10},{9,11},{10,... | collective-permute-start | bytes 3145736 | tf_op jit(solution)/shard_map/ppermute | solution.py:31
  186.4 25.4 %collective-permute-start.26 = (bf16[512,1024]{1,0:T(8,128)(2,1)S(1)}, bf16[512,1024]{1,0:T(8,128)(2,1)}, u32[]{:S(2)}, u32[]{:S(2)}) collective-permute-start(bf16[512,1024]{1,0:T(8,128)(2,1)S(1)} %add_convert_fusion.3), channel_id=1, source_target_pairs={{0,2},{1,3},{2,0},{3,1},{4,6},{5,7},{6,4},{7,5},{8,10},{9,11},{10,... | collective-permute-start | bytes 3145736 | tf_op jit(solution)/shard_map/ppermute | solution.py:31
  207.7 156.5 %reduce-scatter.3.cloned.1.call-start = ((), (), s32[]{:S(2)}) async-start(), calls=%async_computation.8 | async-start | bytes 2359296 | tf_op jit(solution)/shard_map/reduce_scatter | solution.py:1127
  220.7 24.5 %collective-permute-start.27 = (bf16[512,256]{1,0:T(8,128)(2,1)}, bf16[512,256]{1,0:T(8,128)(2,1)S(1)}, u32[]{:S(2)}, u32[]{:S(2)}) collective-permute-start(bf16[512,256]{1,0:T(8,128)(2,1)} %get-tuple-element.216), channel_id=1, source_target_pairs={{0,1},{1,0},{2,3},{3,2},{4,5},{5,4},{6,7},{7,6},{8,9},{9,8},{10,11... | collective-permute-start | bytes 786440 | tf_op jit(solution)/shard_map/ppermute | solution.py:31
  220.8 24.9 %collective-permute-start.28 = (bf16[512,256]{1,0:T(8,128)(2,1)}, bf16[512,256]{1,0:T(8,128)(2,1)S(1)}, u32[]{:S(2)}, u32[]{:S(2)}) collective-permute-start(bf16[512,256]{1,0:T(8,128)(2,1)} %get-tuple-element.217), channel_id=1, source_target_pairs={{0,2},{1,3},{2,0},{3,1},{4,6},{5,7},{6,4},{7,5},{8,10},{9,11},{10,... | collective-permute-start | bytes 786440 | tf_op jit(solution)/shard_map/ppermute | solution.py:31
  222.4 23.4 %collective-permute-start.29 = (bf16[512,256]{1,0:T(8,128)(2,1)}, bf16[512,256]{1,0:T(8,128)(2,1)}, u32[]{:S(2)}, u32[]{:S(2)}) collective-permute-start(bf16[512,256]{1,0:T(8,128)(2,1)} %get-tuple-element.218), channel_id=1, source_target_pairs={{0,3},{1,2},{2,1},{3,0},{4,7},{5,6},{6,5},{7,4},{8,11},{9,10},{10,... | collective-permute-start | bytes 786440 | tf_op jit(solution)/shard_map/ppermute | solution.py:31
  245.3 40.6 %collective-permute-start.34 = (bf16[1024,256]{1,0:T(8,128)(2,1)}, bf16[1024,256]{1,0:T(8,128)(2,1)S(1)}, u32[]{:S(2)}, u32[]{:S(2)}) collective-permute-start(bf16[1024,256]{1,0:T(8,128)(2,1)} %get-tuple-element.226), channel_id=1, source_target_pairs={{0,1},{1,0},{2,3},{3,2},{4,5},{5,4},{6,7},{7,6},{8,9},{9,8},{10,11... | collective-permute-start | bytes 1572872 | tf_op jit(solution)/shard_map/ppermute | solution.py:31
  248.2 37.7 %collective-permute-start.32 = (bf16[512,1024]{1,0:T(8,128)(2,1)S(1)}, bf16[512,1024]{1,0:T(8,128)(2,1)}, u32[]{:S(2)}, u32[]{:S(2)}) collective-permute-start(bf16[512,1024]{1,0:T(8,128)(2,1)S(1)} %add_convert_fusion.2), channel_id=1, source_target_pairs={{0,2},{1,3},{2,0},{3,1},{4,6},{5,7},{6,4},{7,5},{8,10},{9,11},{10,... | collective-permute-start | bytes 3145736 | tf_op jit(solution)/shard_map/ppermute | solution.py:31
  249.6 36.3 %collective-permute-start.33 = (bf16[1024,256]{1,0:T(8,128)(2,1)S(1)}, bf16[1024,256]{1,0:T(8,128)(2,1)S(1)}, u32[]{:S(2)}, u32[]{:S(2)}) collective-permute-start(bf16[1024,256]{1,0:T(8,128)(2,1)S(1)} %add_convert_fusion.4), channel_id=1, source_target_pairs={{0,2},{1,3},{2,0},{3,1},{4,6},{5,7},{6,4},{7,5},{8,10},{9,11},{10,... | collective-permute-start | bytes 1572872 | tf_op jit(solution)/shard_map/ppermute | solution.py:31
  251.0 34.3 %all-to-all-start.1 = ((f32[32,1,384]{2,1,0:T(1,128)}), f32[32,1,384]{2,1,0:T(1,128)S(1)}, u32[]{:S(2)}, u32[]{:S(2)}) async-start(f32[32,1,384]{2,1,0:T(1,128)} %copy.143), calls=%async_computation.3 | async-start | bytes 98304 | tf_op jit(solution)/shard_map/all_to_all | solution.py:94
  294.2 43.7 %all-to-all-start.2 = ((bf16[8,144,640]{2,1,0:T(8,128)(2,1)}), bf16[8,144,640]{2,1,0:T(8,128)(2,1)}, u32[]{:S(2)}, u32[]{:S(2)}) async-start(bf16[8,144,640]{2,1,0:T(8,128)(2,1)} %attend_rows.3), calls=%async_computation.4 | async-start | bytes 2949120 | tf_op jit(solution)/shard_map/all_to_all | solution.py:152
  344.0 49.2 %collective-permute-start.40 = (bf16[512,1024]{1,0:T(8,128)(2,1)}, bf16[512,1024]{1,0:T(8,128)(2,1)}, u32[]{:S(2)}, u32[]{:S(2)}) collective-permute-start(bf16[512,1024]{1,0:T(8,128)(2,1)} %get-tuple-element.221), channel_id=1, source_target_pairs={{0,1},{1,0},{2,3},{3,2},{4,5},{5,4},{6,7},{7,6},{8,9},{9,8},{10,11... | collective-permute-start | bytes 3145736 | tf_op jit(solution)/shard_map/ppermute | solution.py:31
  344.3 32.1 %all-to-all-start.3 = ((bf16[8,144,384]{2,1,0:T(8,128)(2,1)}), bf16[8,144,384]{2,1,0:T(8,128)(2,1)S(1)}, u32[]{:S(2)}, u32[]{:S(2)}) async-start(bf16[8,144,384]{2,1,0:T(8,128)(2,1)} %attend_rows.2), calls=%async_computation.5 | async-start | bytes 1769472 | tf_op jit(solution)/shard_map/all_to_all | solution.py:152
  351.0 46.5 %collective-permute-start.39 = (bf16[512,1024]{1,0:T(8,128)(2,1)}, bf16[512,1024]{1,0:T(8,128)(2,1)}, u32[]{:S(2)}, u32[]{:S(2)}) collective-permute-start(bf16[512,1024]{1,0:T(8,128)(2,1)} %add_convert_fusion.1), channel_id=1, source_target_pairs={{0,2},{1,3},{2,0},{3,1},{4,6},{5,7},{6,4},{7,5},{8,10},{9,11},{10,... | collective-permute-start | bytes 3145736 | tf_op jit(solution)/shard_map/ppermute | solution.py:31
  (66 other events, 939.7 us)
Sparse Core Ops, SparseCore 0:
  59.5 74.5 all-gather.1
  207.8 65.2 reduce-scatter.4
  276.6 87.5 reduce-scatter.2

commit v4 on v3

--- a/solution.py
+++ b/solution.py
@@ -678,6 +678,10 @@
     return jnp.concatenate([grads, below], axis=1)
 
 
+def lanes(value):
+    return sum(value[:, i : i + LANES] for i in range(0, value.shape[1], LANES))
+
+
 def attend_sums(piece, work, gains, width):
     groups, rows, columns = piece.shape
     shard = rows - EXTRA
@@ -690,13 +694,18 @@
         below = jnp.sum(total[shard:, :width], axis=0, keepdims=True)
         gain, bias = gain_ref[:, 0:1], gain_ref[:, 1:2]
         work = work_ref[...].astype(F32)
-        grad_ref[...] = gain * grad + bias * below
+        result = gain * grad + bias * below
+        grad_ref[...] = result
+        squares = lanes(fold(result * result))
         for k, value in enumerate((grad * work, below * work)):
             outs[0][:, k : k + 1] = jnp.sum(value, axis=1, keepdims=True)
         if columns > width:
-            outs[1][...] = total[:shard, width:]
-
-    outs = [((shard, width), F32), ((shard, 2), F32)]
+            value = total[:shard, width:]
+            outs[2][...] = value
+            squares = squares + lanes(fold(value * value))
+        outs[1][...] = squares
+
+    outs = [((shard, width), F32), ((shard, 2), F32), ((8, LANES), F32)]
     if columns > width:
         outs.append(((shard, columns - width), F32))
     return pl.pallas_call(
@@ -1144,12 +1153,13 @@
     local_squares, near_terms, pieces = lax.optimization_barrier((local_squares, near_terms, pieces))
     norm_sums = jnp.sum(term_sums, axis=0)
     outer_rows = lax.dynamic_slice_in_dim(outer, lax.axis_index("dp") * shard, shard, 1).T
-    attend_parts, outer_terms = [], 0.0
+    attend_parts, outer_terms, all_parts = [], 0.0, 0.0
     for pair, piece in enumerate(pieces):
-        grad, sums, *beside = attend_sums(
+        grad, sums, part_squares, *beside = attend_sums(
             piece, by_pair[:, 3 * LANES * pair : 3 * LANES * (pair + 1)], outer_rows, 3 * LANES
         )
         attend_parts.append(grad)
+        all_parts = all_parts + part_squares
         outer_terms = outer_terms + sums
         if beside:
             mixing_grad = beside[0]
@@ -1165,7 +1175,8 @@
         norm_sums[half + sizes[1] :].reshape(unit_norms.shape),
     ]
 
-    for gradient in [*norm_grads, mixing_grad, *attend_parts]:
+    local_squares = local_squares + jnp.sum(all_parts)
+    for gradient in norm_grads:
         local_squares = local_squares + jnp.sum(gradient * gradient)
     all_squares = exchange_all(jnp.broadcast_to(local_squares, (device_count, 128)))
     result = middle + sum_near(feed_terms[:2], after(feed_arrived, [local_squares]))

time: 424 us -> 422 us (level)
  transfers between devices with their start and end apart: 49 -> 49, of which waited for: 18 -> 18; matrix products, arithmetic and copies ran while one was open for 8% -> 8% of each run, Pallas kernels for 47% -> 48%
where the time goes in v4:
time: 422 us; the launch traced here: 418 us
  Pallas kernels  226 us (54%)
  waiting for transfers between devices  80.4 us (19%)
  starting transfers between devices  50.8 us (12%)
  other arithmetic  26.7 us (6%)
  between operations  20.5 us (5%)
  local copies, waits for them, and re-layouts  14.3 us (3%)
    pallas_call x9, Pallas kernels, call(): pl.pallas_call(body, grid_spec=pltpu.PrefetchScalarGridSpec(num_scalar_pr...  78.9 us
    pallas_call x2, Pallas kernels, attention_backward(): pl.pallas_call(partial(backward_kernel, block=block, count=table.shape[0]...  55.3 us
    pallas_call x1, Pallas kernels, attention_forward(): pl.pallas_call(kernel, grid_spec=pltpu.PrefetchScalarGridSpec(num_scalar_...  28.2 us
    ppermute x34, waiting for transfers between devices, swap(): return lax.ppermute(value, 'mp', [(i, i ^ bit) for i in range(count)])  25.4 us
    ppermute x34, starting transfers between devices, swap(): return lax.ppermute(value, 'mp', [(i, i ^ bit) for i in range(count)])  22.5 us
    pallas_call x2, Pallas kernels, weight_grad(): pl.pallas_call(kernel, grid=(left.shape[1] // block,), in_specs=[pl.Block...  17.4 us
    all_to_all x3, waiting for transfers between devices, exchange_all(): return lax.all_to_all(value, ALL, 0, 0, tiled=True)  16.6 us
    pallas_call x2, Pallas kernels, attend_rows(): pl.pallas_call(kernel, grid=(groups,), in_specs=[pl.BlockSpec((length, D)...  16.5 us
  transfers between devices with their start and end apart: 49, of which 18 were waited for; matrix products, arithmetic and copies ran while one was open for 8% of the time, Pallas kernels for 48%

profile of v4, /device:TPU:0, one launch (start us, length us, event | category | flops | bytes accessed | tf_op | source)
XLA Modules:
  0.0 418.5 jit_solution(4674609854791626822)
XLA Ops:
  29.0 12.9 %all-to-all-done = f32[32,1,448]{2,1,0:T(1,128)S(1)} async-done(((f32[32,1,448]{2,1,0:T(1,128)}), f32[32,1,448]{2,1,0:T(1,128)S(1)}, u32[]{:S(2)}, u32[]{:S(2)}) %all-to-all-start) | async-done | bytes 57376 | tf_op jit(solution)/shard_map/all_to_all | solution.py:94
  44.0 7.3 %collective-permute-done.7.refs_5_ = bf16[128,1024]{1,0:T(8,128)(2,1)S(1)} collective-permute-done((bf16[128,1024]{1,0:T(8,128)(2,1)}, bf16[128,1024]{1,0:T(8,128)(2,1)S(1)}, u32[]{:S(2)}, u32[]{:S(2)}) %collective-permute-start.7) | collective-permute-done | bytes 262176 | tf_op jit(solution)/shard_map/ppermute | solution.py:99
  64.3 9.0 %project.1 = (bf16[2048,1024]{1,0:T(8,128)(2,1)}, bf16[2048,768]{1,0:T(8,128)(2,1)}) custom-call(bf16[512,1024]{1,0:T(8,128)(2,1)S(1)} %copy-done, bf16[512,1024]{1,0:T(8,128)(2,1)S(1)} %collective-permute-done.refs_1_, bf16[512,1024]{1,0:T(8,128)(2,1)S(1)} %collective-permute-done.1.refs_2_, bf16[512,1024]{1,0:T(8,128)(2,1)} %collective-permute-done.9.refs_3_, ...), custom_call_target="tpu_custom_call" | custom-call | flops 36800000000 | bytes 3200000 | tf_op jit(solution)/shard_map/project/pallas_call | solution.py:281
  73.9 28.2 %attention_forward.1 = (bf16[512,256]{1,0:T(8,128)(2,1)S(1)}, bf16[512,256]{1,0:T(8,128)(2,1)S(1)}, bf16[512,256]{1,0:T(8,128)(2,1)S(1)}, bf16[512,256]{1,0:T(8,128)(2,1)S(1)}, f32[16,2048]{1,0:T(8,128)S(1)}) custom-call(s32[6]{0:T(128)S(1)} %pad_add_fusion.table_ref.refs_0_, ...), custom_call_target="tpu_custom_call" | custom-call | flops 147200000000 | bytes 12800000 | tf_op jit(solution)/shard_map/attention_forward/pallas_call | solution.py:802
  106.1 6.6 %collective-permute-done.14.refs_2_.refs_9_ = bf16[512,256]{1,0:T(8,128)(2,1)} collective-permute-done((bf16[512,256]{1,0:T(8,128)(2,1)S(1)}, bf16[512,256]{1,0:T(8,128)(2,1)}, u32[]{:S(2)}, u32[]{:S(2)}) %collective-permute-start.14) | collective-permute-done | bytes 262176 | tf_op jit(solution)/shard_map/ppermute | solution.py:31
  117.5 5.8 %mix_rows.1 = (f32[512,1024]{1,0:T(8,128)}, bf16[512,1024]{1,0:T(8,128)(2,1)}, bf16[512,1024]{1,0:T(8,128)(2,1)}) custom-call(s32[6]{0:T(128)S(1)} %pad_add_fusion.table_ref.refs_0_, bf16[512,256]{1,0:T(8,128)(2,1)S(1)} %copy-done.18, bf16[512,256]{1,0:T(8,128)(2,1)S(1)} %collective-permute-done.13.refs_1_.refs_8_, ...), custom_call_target="tpu_custom_call" | custom-call | flops 27599998976 | bytes 2400000 | tf_op jit(solution)/shard_map/mix_rows/pallas_call | solution.py:337
  125.6 8.4 %all-gather.2.cloned.1.call-done.refs_5_.refs_2_.refs_1_ = bf16[1024,2048]{1,0:T(8,128)(2,1)} async-done(((bf16[128,2048]{1,0:T(8,128)(2,1)}), bf16[1024,2048]{1,0:T(8,128)(2,1)}) %all-gather.2.cloned.1.call-update) | async-done | bytes 4194320 | tf_op jit(solution)/shard_map/all_gather | solution.py:1048
  134.1 9.8 %feed_back.1 = (bf16[2048,1024]{1,0:T(8,128)(2,1)}, bf16[2048,1024]{1,0:T(8,128)(2,1)}) custom-call(s32[6]{0:T(128)S(1)} %pad_add_fusion.table_ref.refs_0_, bf16[512,1024]{1,0:T(8,128)(2,1)} %refs_4_.1, bf16[512,1024]{1,0:T(8,128)(2,1)S(1)} %collective-permute-done.19.refs_2_, bf16[512,1024]{1,0:T(8,128)(2,1)} %collective-permute-done.12.refs_3_, ...), custom_call_target="tpu_custom_call" | custom-call | flops 36800000000 | bytes 3200000 | tf_op jit(solution)/shard_map/feed_back/pallas_call | solution.py:281
  145.1 9.2 %widen.2 = (bf16[2048,1024]{1,0:T(8,128)(2,1)}, f32[2048,1024]{1,0:T(8,128)}, bf16[2048,1024]{1,0:T(8,128)(2,1)}, f32[4,2048]{1,0:T(4,128)S(1)}) custom-call(bf16[512,1024]{1,0:T(8,128)(2,1)S(1)} %copy-done.7, bf16[512,1024]{1,0:T(8,128)(2,1)} %collective-permute-done.18.refs_1_, bf16[1024,2048]{1,0:T(8,128)(2,1)} %all-gather.2.cloned.1.call-done.refs_5_.refs_2_.refs_1_, ...), custom_call_target="tpu_custom_call" | custom-call | flops 18400000000 | bytes 1600000 | tf_op jit(solution)/shard_map/widen/pallas_call | solution.py:281
  157.0 8.5 %widen.3 = (bf16[2048,1024]{1,0:T(8,128)(2,1)}, f32[2048,1024]{1,0:T(8,128)}, bf16[2048,1024]{1,0:T(8,128)(2,1)}, f32[4,2048]{1,0:T(4,128)S(1)}) custom-call(bf16[512,1024]{1,0:T(8,128)(2,1)S(1)} %collective-permute-done.17.refs_0_, ...), custom_call_target="tpu_custom_call", output_to_operand_aliasing={{0}: (5, {}), {1}: (6, {}), {2}: (7, {}), {3}: (8, {})} | custom-call | flops 18400000000 | bytes 1600000 | tf_op jit(solution)/shard_map/widen/pallas_call | solution.py:281
  170.8 11.1 %narrow_back.2 = (bf16[2048,1024]{1,0:T(8,128)(2,1)}, bf16[2048,1024]{1,0:T(8,128)(2,1)}, f32[16,1024]{1,0:T(8,128)S(1)}, bf16[512,1024]{1,0:T(8,128)(2,1)}, bf16[512,1024]{1,0:T(8,128)(2,1)}) custom-call(f32[2048,1024]{1,0:T(8,128)} %get-tuple-element.199.refs_0_, bf16[2048,1024]{1,0:T(8,128)(2,1)} %get-tuple-element.204.refs_1_, ...), custom_call_target="tpu_custom_call" | custom-call | flops 18400000000 | bytes 1600000 | tf_op jit(solution)/shard_map/narrow_back/pallas_call | solution.py:281
  187.9 11.1 %narrow_back.3 = (bf16[2048,1024]{1,0:T(8,128)(2,1)}, bf16[2048,1024]{1,0:T(8,128)(2,1)}, f32[16,1024]{1,0:T(8,128)S(1)}, bf16[512,1024]{1,0:T(8,128)(2,1)}, bf16[512,1024]{1,0:T(8,128)(2,1)}) custom-call(f32[2048,1024]{1,0:T(8,128)} %get-tuple-element.199.refs_0_, ...), custom_call_target="tpu_custom_call", output_to_operand_aliasing={{0}: (6, {}), {1}: (7, {})} | custom-call | flops 18400000000 | bytes 1600000 | tf_op jit(solution)/shard_map/narrow_back/pallas_call | solution.py:281
  199.0 8.7 %weight_grad.2 = bf16[1024,1024]{1,0:T(8,128)(2,1)} custom-call(bf16[2048,1024]{1,0:T(8,128)(2,1)} %get-tuple-element.210.left_ref, bf16[2048,1024]{1,0:T(8,128)(2,1)} %get-tuple-element.221.right_ref.refs_0_), custom_call_target="tpu_custom_call" | custom-call | flops 36800000000 | bytes 3200000 | tf_op jit(solution)/shard_map/weight_grad/pallas_call | solution.py:577
  211.8 8.9 %mix_rows_back.1 = (f32[512,1024]{1,0:T(8,128)}, bf16[512,1024]{1,0:T(8,128)(2,1)}, f32[16,1024]{1,0:T(8,128)S(1)}, f32[16,1024]{1,0:T(8,128)S(1)}, bf16[512,256...) custom-call(s32[6]{0:T(128)S(1)} %pad_add_fusion.table_ref.refs_0_, ...), custom_call_target="tpu_custom_call" | custom-call | flops 36800000000 | bytes 3200000 | tf_op jit(solution)/shard_map/mix_rows_back/pallas_call | solution.py:337
  222.6 9.7 %feed_rows.1 = (bf16[512,1024]{1,0:T(8,128)(2,1)}, bf16[512,1024]{1,0:T(8,128)(2,1)}, bf16[512,1024]{1,0:T(8,128)(2,1)}, bf16[512,1024]{1,0:T(8,128)(2,1)}) custom-call(bf16[2048,1024]{1,0:T(8,128)(2,1)} %get-tuple-element.221.right_ref.refs_0_, bf16[1024,2048]{1,0:T(8,128)(2,1)} %all-gather.2.cloned.1.call-done.refs_5_.refs_2_.refs_1_), custom_call_target="tpu_custom_call" | custom-call | flops 36800000000 | bytes 3200000 | tf_op jit(solution)/shard_map/feed_rows/pallas_call | solution.py:281
  235.9 8.7 %weight_grad.3 = bf16[1024,1024]{1,0:T(8,128)(2,1)} custom-call(bf16[2048,1024]{1,0:T(8,128)(2,1)} %get-tuple-element.198.left_ref, bf16[2048,1024]{1,0:T(8,128)(2,1)} %get-tuple-element.215.right_ref), custom_call_target="tpu_custom_call" | custom-call | flops 36800000000 | bytes 3200000 | tf_op jit(solution)/shard_map/weight_grad/pallas_call | solution.py:577
  253.8 27.7 %attention_backward.2.back_ref.refs_0_ = bf16[2048,384]{1,0:T(8,128)(2,1)} custom-call(s32[6]{0:T(128)} %copy-done.6, bf16[2048,768]{1,0:T(8,128)(2,1)} %get-tuple-element.173.refs_0_.refs_1_.refs_2_.refs_3_.refs_4_.refs_5_.q_ref.k_ref.v_ref, bf16[2048,768]{1,0:T(8,128)(2,1)} %get-tuple-element.173.refs_0_.refs_1_.refs_2_.refs_3_.refs_4_.refs_5_.q_ref.k_ref.v_ref, ...), custom_call_target="tpu_custom_call" | custom-call | flops 138000007168 | bytes 12000000 | tf_op jit(solution)/shard_map/attention_backward/pallas_call | solution.py:882
  285.9 8.3 %attend_rows.3 = bf16[8,144,640]{2,1,0:T(8,128)(2,1)} custom-call(bf16[2048,1024]{1,0:T(8,128)(2,1)} %get-tuple-element.180.normed_ref, bf16[2048,384]{1,0:T(8,128)(2,1)} %attention_backward.2.back_ref.refs_0_, bf16[1024,256]{1,0:T(8,128)(2,1)S(1)} %copy-done.16, bf16[1024,256]{1,0:T(8,128)(2,1)S(1)} %collective-permute-done.34.refs_1_, ...), custom_call_target="tpu_custom_call" | custom-call | flops 23000000512 | bytes 2000000 | tf_op jit(solution)/shard_map/attend_rows/pallas_call | solution.py:647
  298.7 27.6 %attention_backward.3.back_ref.refs_1_ = bf16[2048,384]{1,0:T(8,128)(2,1)} custom-call(s32[6]{0:T(128)} %copy-done.6, bf16[2048,768]{1,0:T(8,128)(2,1)} %get-tuple-element.173.refs_0_.refs_1_.refs_2_.refs_3_.refs_4_.refs_5_.q_ref.k_ref.v_ref, bf16[2048,768]{1,0:T(8,128)(2,1)} %get-tuple-element.173.refs_0_.refs_1_.refs_2_.refs_3_.refs_4_.refs_5_.q_ref.k_ref.v_ref, ...), custom_call_target="tpu_custom_call" | custom-call | flops 138000007168 | bytes 12000000 | tf_op jit(solution)/shard_map/attention_backward/pallas_call | solution.py:882
  326.2 8.2 %attend_rows.2 = bf16[8,144,384]{2,1,0:T(8,128)(2,1)} custom-call(bf16[2048,1024]{1,0:T(8,128)(2,1)} %get-tuple-element.180.normed_ref, bf16[2048,384]{1,0:T(8,128)(2,1)} %attention_backward.3.back_ref.refs_1_), custom_call_target="tpu_custom_call" | custom-call | flops 23000000512 | bytes 2000000 | tf_op jit(solution)/shard_map/attend_rows/pallas_call | solution.py:647
  352.4 5.3 %input_back.3 = (bf16[512,1024]{1,0:T(8,128)(2,1)}, bf16[512,1024]{1,0:T(8,128)(2,1)}) custom-call(bf16[2048,384]{1,0:T(8,128)(2,1)} %attention_backward.2.back_ref.refs_0_, bf16[2048,384]{1,0:T(8,128)(2,1)} %attention_backward.3.back_ref.refs_1_, bf16[1024,768]{1,0:T(8,128)(2,1)S(1)} %copy-done.13), custom_call_target="tpu_custom_call" | custom-call | flops 18400000000 | bytes 1600000 | tf_op jit(solution)/shard_map/input_back/pallas_call | solution.py:281
  357.7 6.6 %reduce-scatter.3.cloned.1.call-done.refs_3_ = bf16[128,1024]{1,0:T(8,128)(2,1)} async-done(((bf16[1024,1024]{1,0:T(8,128)(2,1)}), bf16[128,1024]{1,0:T(8,128)(2,1)}) %reduce-scatter.3.cloned.1.call-update) | async-done | bytes 262160 | tf_op jit(solution)/shard_map/reduce_scatter | solution.py:1136
  369.9 6.4 %all-to-all-done.3.piece_ref = bf16[8,144,384]{2,1,0:T(8,128)(2,1)S(1)} async-done(((bf16[8,144,384]{2,1,0:T(8,128)(2,1)}), bf16[8,144,384]{2,1,0:T(8,128)(2,1)S(1)}, u32[]{:S(2)}, u32[]{:S(2)}) %all-to-all-start.3) | async-done | bytes 884768 | tf_op jit(solution)/shard_map/all_to_all | solution.py:152
  403.6 6.9 %adamw.1 = (f32[3,128,256]{2,1,0:T(8,128)}, f32[3,128,256]{2,1,0:T(8,128)}, f32[3,128,256]{2,1,0:T(8,128)}, f32[3,128,256]{2,1,0:T(8,128)}, f32[256,128]{1,0:T(8...) custom-call(f32[3]{0:T(128)S(1)} %pad_maximum_fusion.5.scale_ref, ...), custom_call_target="tpu_custom_call" | custom-call | flops 27599998976 | bytes 2400000 | tf_op jit(solution)/shard_map/adamw/pallas_call | solution.py:979
  (260 shorter events, 137.0 us)
Async XLA Ops:
  7.3 34.7 %collective-permute-start.1 = (bf16[512,1024]{1,0:T(8,128)(2,1)}, bf16[512,1024]{1,0:T(8,128)(2,1)S(1)}, u32[]{:S(2)}, u32[]{:S(2)}) collective-permute-start(bf16[512,1024]{1,0:T(8,128)(2,1)} %refs_9_.2), channel_id=1, source_target_pairs={{0,2},{1,3},{2,0},{3,1},{4,6},{5,7},{6,4},{7,5},{8,10},{9,11},{10,... | collective-permute-start | bytes 3145736 | tf_op jit(solution)/shard_map/ppermute | solution.py:31
  14.3 27.6 %collective-permute-start.4 = (bf16[128,1024]{1,0:T(8,128)(2,1)S(1)}, bf16[128,1024]{1,0:T(8,128)(2,1)}, u32[]{:S(2)}, u32[]{:S(2)}) collective-permute-start(bf16[128,1024]{1,0:T(8,128)(2,1)S(1)} %pad_maximum_fusion.1.refs_0_), channel_id=1, source_target_pairs={{0,16},{4,20},{8,24},{12,28},{16,0},{20,4},{24,8},{28,12},{1,17},{... | collective-permute-start | bytes 786440 | tf_op jit(solution)/shard_map/ppermute | solution.py:99
  16.9 25.0 %collective-permute-start.5 = (bf16[128,1024]{1,0:T(8,128)(2,1)S(1)}, bf16[128,1024]{1,0:T(8,128)(2,1)}, u32[]{:S(2)}, u32[]{:S(2)}) collective-permute-start(bf16[128,1024]{1,0:T(8,128)(2,1)S(1)} %pad_maximum_fusion.1.refs_0_), channel_id=1, source_target_pairs={{0,24},{4,28},{8,16},{12,20},{16,8},{20,12},{24,0},{28,4},{1,25},{... | collective-permute-start | bytes 786440 | tf_op jit(solution)/shard_map/ppermute | solution.py:99
  18.2 23.7 %collective-permute-start.6 = (bf16[128,1024]{1,0:T(8,128)(2,1)S(1)}, bf16[128,1024]{1,0:T(8,128)(2,1)}, u32[]{:S(2)}, u32[]{:S(2)}) collective-permute-start(bf16[128,1024]{1,0:T(8,128)(2,1)S(1)} %pad_maximum_fusion.1.refs_0_), channel_id=1, source_target_pairs={{0,8},{4,12},{8,0},{12,4},{16,24},{20,28},{24,16},{28,20},{1,9},{5... | collective-permute-start | bytes 786440 | tf_op jit(solution)/shard_map/ppermute | solution.py:99
  20.6 21.3 %collective-permute-start.3 = (bf16[128,1024]{1,0:T(8,128)(2,1)}, bf16[128,1024]{1,0:T(8,128)(2,1)}, u32[]{:S(2)}, u32[]{:S(2)}) collective-permute-start(bf16[128,1024]{1,0:T(8,128)(2,1)} %collective-permute-done.2.refs_1_), channel_id=1, source_target_pairs={{0,8},{4,12},{8,0},{12,4},{16,24},{20,28},{24,16},{28,20},{1,9},{5... | collective-permute-start | bytes 786440 | tf_op jit(solution)/shard_map/ppermute | solution.py:99
  26.9 107.2 %all-gather.2.cloned.1.call-start = ((), (), s32[]{:S(2)}) async-start(), calls=%async_computation.7 | async-start | bytes 4718592 | tf_op jit(solution)/shard_map/all_gather | solution.py:1048
  59.4 298.3 %reduce-scatter.5.cloned.1.call-start = ((), (), s32[]{:S(2)}) async-start(), calls=%async_computation.9 | async-start | bytes 2359296 | tf_op jit(solution)/shard_map/reduce_scatter | solution.py:1136
  62.4 40.5 %collective-permute-start.10 = (bf16[1024,256]{1,0:T(8,128)(2,1)}, bf16[1024,256]{1,0:T(8,128)(2,1)}, u32[]{:S(2)}, u32[]{:S(2)}) collective-permute-start(bf16[1024,256]{1,0:T(8,128)(2,1)} %get-tuple-element.186.refs_4_.refs_11_), channel_id=1, source_target_pairs={{0,1},{1,0},{2,3},{3,2},{4,5},{5,4},{6,7},{7,6},{8,9},{9,8},{10,11... | collective-permute-start | bytes 1572872 | tf_op jit(solution)/shard_map/ppermute | solution.py:31
  62.9 40.0 %collective-permute-start.11 = (bf16[1024,256]{1,0:T(8,128)(2,1)}, bf16[1024,256]{1,0:T(8,128)(2,1)}, u32[]{:S(2)}, u32[]{:S(2)}) collective-permute-start(bf16[1024,256]{1,0:T(8,128)(2,1)} %get-tuple-element.186.refs_4_.refs_11_), channel_id=1, source_target_pairs={{0,2},{1,3},{2,0},{3,1},{4,6},{5,7},{6,4},{7,5},{8,10},{9,11},{10,... | collective-permute-start | bytes 1572872 | tf_op jit(solution)/shard_map/ppermute | solution.py:31
  73.3 29.6 %collective-permute-start.12 = (bf16[512,1024]{1,0:T(8,128)(2,1)}, bf16[512,1024]{1,0:T(8,128)(2,1)}, u32[]{:S(2)}, u32[]{:S(2)}) collective-permute-start(bf16[512,1024]{1,0:T(8,128)(2,1)} %refs_4_.1), channel_id=1, source_target_pairs={{0,2},{1,3},{2,0},{3,1},{4,6},{5,7},{6,4},{7,5},{8,10},{9,11},{10,... | collective-permute-start | bytes 3145736 | tf_op jit(solution)/shard_map/ppermute | solution.py:31
  123.3 30.9 %collective-permute-start.17 = (bf16[512,1024]{1,0:T(8,128)(2,1)}, bf16[512,1024]{1,0:T(8,128)(2,1)S(1)}, u32[]{:S(2)}, u32[]{:S(2)}) collective-permute-start(bf16[512,1024]{1,0:T(8,128)(2,1)} %get-tuple-element.189.refs_0_), channel_id=1, source_target_pairs={{0,2},{1,3},{2,0},{3,1},{4,6},{5,7},{6,4},{7,5},{8,10},{9,11},{10,... | collective-permute-start | bytes 3145736 | tf_op jit(solution)/shard_map/ppermute | solution.py:31
  186.4 25.4 %collective-permute-start.26 = (bf16[512,1024]{1,0:T(8,128)(2,1)S(1)}, bf16[512,1024]{1,0:T(8,128)(2,1)}, u32[]{:S(2)}, u32[]{:S(2)}) collective-permute-start(bf16[512,1024]{1,0:T(8,128)(2,1)S(1)} %add_convert_fusion.3), channel_id=1, source_target_pairs={{0,2},{1,3},{2,0},{3,1},{4,6},{5,7},{6,4},{7,5},{8,10},{9,11},{10,... | collective-permute-start | bytes 3145736 | tf_op jit(solution)/shard_map/ppermute | solution.py:31
  207.7 156.6 %reduce-scatter.3.cloned.1.call-start = ((), (), s32[]{:S(2)}) async-start(), calls=%async_computation.8 | async-start | bytes 2359296 | tf_op jit(solution)/shard_map/reduce_scatter | solution.py:1136
  220.7 24.5 %collective-permute-start.27 = (bf16[512,256]{1,0:T(8,128)(2,1)}, bf16[512,256]{1,0:T(8,128)(2,1)S(1)}, u32[]{:S(2)}, u32[]{:S(2)}) collective-permute-start(bf16[512,256]{1,0:T(8,128)(2,1)} %get-tuple-element.218), channel_id=1, source_target_pairs={{0,1},{1,0},{2,3},{3,2},{4,5},{5,4},{6,7},{7,6},{8,9},{9,8},{10,11... | collective-permute-start | bytes 786440 | tf_op jit(solution)/shard_map/ppermute | solution.py:31
  220.8 24.9 %collective-permute-start.28 = (bf16[512,256]{1,0:T(8,128)(2,1)}, bf16[512,256]{1,0:T(8,128)(2,1)S(1)}, u32[]{:S(2)}, u32[]{:S(2)}) collective-permute-start(bf16[512,256]{1,0:T(8,128)(2,1)} %get-tuple-element.219), channel_id=1, source_target_pairs={{0,2},{1,3},{2,0},{3,1},{4,6},{5,7},{6,4},{7,5},{8,10},{9,11},{10,... | collective-permute-start | bytes 786440 | tf_op jit(solution)/shard_map/ppermute | solution.py:31
  222.3 23.3 %collective-permute-start.29 = (bf16[512,256]{1,0:T(8,128)(2,1)}, bf16[512,256]{1,0:T(8,128)(2,1)}, u32[]{:S(2)}, u32[]{:S(2)}) collective-permute-start(bf16[512,256]{1,0:T(8,128)(2,1)} %get-tuple-element.220), channel_id=1, source_target_pairs={{0,3},{1,2},{2,1},{3,0},{4,7},{5,6},{6,5},{7,4},{8,11},{9,10},{10,... | collective-permute-start | bytes 786440 | tf_op jit(solution)/shard_map/ppermute | solution.py:31
  245.2 40.6 %collective-permute-start.34 = (bf16[1024,256]{1,0:T(8,128)(2,1)}, bf16[1024,256]{1,0:T(8,128)(2,1)S(1)}, u32[]{:S(2)}, u32[]{:S(2)}) collective-permute-start(bf16[1024,256]{1,0:T(8,128)(2,1)} %get-tuple-element.228), channel_id=1, source_target_pairs={{0,1},{1,0},{2,3},{3,2},{4,5},{5,4},{6,7},{7,6},{8,9},{9,8},{10,11... | collective-permute-start | bytes 1572872 | tf_op jit(solution)/shard_map/ppermute | solution.py:31
  248.2 37.7 %collective-permute-start.32 = (bf16[512,1024]{1,0:T(8,128)(2,1)S(1)}, bf16[512,1024]{1,0:T(8,128)(2,1)}, u32[]{:S(2)}, u32[]{:S(2)}) collective-permute-start(bf16[512,1024]{1,0:T(8,128)(2,1)S(1)} %add_convert_fusion.2), channel_id=1, source_target_pairs={{0,2},{1,3},{2,0},{3,1},{4,6},{5,7},{6,4},{7,5},{8,10},{9,11},{10,... | collective-permute-start | bytes 3145736 | tf_op jit(solution)/shard_map/ppermute | solution.py:31
  249.5 36.3 %collective-permute-start.33 = (bf16[1024,256]{1,0:T(8,128)(2,1)S(1)}, bf16[1024,256]{1,0:T(8,128)(2,1)S(1)}, u32[]{:S(2)}, u32[]{:S(2)}) collective-permute-start(bf16[1024,256]{1,0:T(8,128)(2,1)S(1)} %add_convert_fusion.4), channel_id=1, source_target_pairs={{0,2},{1,3},{2,0},{3,1},{4,6},{5,7},{6,4},{7,5},{8,10},{9,11},{10,... | collective-permute-start | bytes 1572872 | tf_op jit(solution)/shard_map/ppermute | solution.py:31
  250.9 34.3 %all-to-all-start.1 = ((f32[32,1,384]{2,1,0:T(1,128)}), f32[32,1,384]{2,1,0:T(1,128)S(1)}, u32[]{:S(2)}, u32[]{:S(2)}) async-start(f32[32,1,384]{2,1,0:T(1,128)} %copy.143), calls=%async_computation.3 | async-start | bytes 98304 | tf_op jit(solution)/shard_map/all_to_all | solution.py:94
  294.1 43.8 %all-to-all-start.2 = ((bf16[8,144,640]{2,1,0:T(8,128)(2,1)}), bf16[8,144,640]{2,1,0:T(8,128)(2,1)}, u32[]{:S(2)}, u32[]{:S(2)}) async-start(bf16[8,144,640]{2,1,0:T(8,128)(2,1)} %attend_rows.3), calls=%async_computation.4 | async-start | bytes 2949120 | tf_op jit(solution)/shard_map/all_to_all | solution.py:152
  344.0 47.3 %collective-permute-start.40 = (bf16[512,1024]{1,0:T(8,128)(2,1)}, bf16[512,1024]{1,0:T(8,128)(2,1)}, u32[]{:S(2)}, u32[]{:S(2)}) collective-permute-start(bf16[512,1024]{1,0:T(8,128)(2,1)} %get-tuple-element.223), channel_id=1, source_target_pairs={{0,1},{1,0},{2,3},{3,2},{4,5},{5,4},{6,7},{7,6},{8,9},{9,8},{10,11... | collective-permute-start | bytes 3145736 | tf_op jit(solution)/shard_map/ppermute | solution.py:31
  344.4 32.0 %all-to-all-start.3 = ((bf16[8,144,384]{2,1,0:T(8,128)(2,1)}), bf16[8,144,384]{2,1,0:T(8,128)(2,1)S(1)}, u32[]{:S(2)}, u32[]{:S(2)}) async-start(bf16[8,144,384]{2,1,0:T(8,128)(2,1)} %attend_rows.2), calls=%async_computation.5 | async-start | bytes 1769472 | tf_op jit(solution)/shard_map/all_to_all | solution.py:152
  351.1 44.5 %collective-permute-start.39 = (bf16[512,1024]{1,0:T(8,128)(2,1)}, bf16[512,1024]{1,0:T(8,128)(2,1)}, u32[]{:S(2)}, u32[]{:S(2)}) collective-permute-start(bf16[512,1024]{1,0:T(8,128)(2,1)} %add_convert_fusion.1), channel_id=1, source_target_pairs={{0,2},{1,3},{2,0},{3,1},{4,6},{5,7},{6,4},{7,5},{8,10},{9,11},{10,... | collective-permute-start | bytes 3145736 | tf_op jit(solution)/shard_map/ppermute | solution.py:31
  (66 other events, 937.9 us)
Sparse Core Ops, SparseCore 0:
  59.5 74.5 all-gather.1
  207.8 65.2 reduce-scatter.4
  276.7 87.5 reduce-scatter.2
